TPU v7x, 256 devices: a whole 4x4x8 slice. The times are simulated.
256 devices in a mesh: freq: 8 (over z), lat: 8 (over x, y_hi), lon: 4 (over y_lo, core).
Axes of the slice: x: 4, y: 4 (y_hi: 2, y_lo: 2; y = y_hi * 2 + y_lo), z: 8, core: 2. Of those that a mesh axis runs over, the one named last changes fastest.
Arguments:
- direction: float32 [3, 32, 1024, 2048], P(None, 'freq', 'lat', 'lon'), may hold values from -6 to 6
- base_flow: float32 [2, 32, 1024, 2048], P(None, 'freq', 'lat', 'lon'), may hold values from -2 to 2
- water_depth: float32 [1024, 2048], P('lat', 'lon'), may hold values from 0.5 to 2
- drag_factor: float32 [1024, 2048], P('lat', 'lon'), may hold values from 0.2 to 2
- wet_mask: int32 [1024, 2048], P('lat', 'lon'), may hold values 0 or 1
Outputs:
- result: float32 [3, 32, 1024, 2048], P(None, 'freq', 'lat', 'lon')
All inputs are finite; a program needn't handle non-finite values. No bound on the sum of `wet_mask` on one device may be relied on, other than what follows from the above.
Results may differ from a plain program's by a relative error of at most 0.000071.
Values sent between devices are 32-bit elements; how exact they have to be, the bound alone decides.
A program may use at most 128 MiB of HBM per device.

v0:
```python
import functools
import math

import jax
import jax.numpy as jnp
from jax import lax
from jax.experimental import pallas as pl
from jax.experimental.pallas import tpu as pltpu
from jax.sharding import PartitionSpec as P

NCON = 16
NTIME = 256


LINEAR_DRAG = 0.5
GRAVITY = 1.0
OMEGA_STEP = 0.25
SPEED_SOFT = 0.01


def extended_2(block, sides, width):
    for axis, dim in sides:
        count = lax.axis_size(axis)
        forward = [(i, i + 1) for i in range(count - 1)]
        forward.append((count - 1, 0))
        backward = [(target, source) for source, target in forward]
        low = lax.ppermute(
            lax.slice_in_dim(block, block.shape[dim] - width, None, axis=dim), axis, forward
        )
        high = lax.ppermute(lax.slice_in_dim(block, 0, width, axis=dim), axis, backward)
        block = jnp.concatenate([low, block, high], axis=dim)
    return block


def samples_table(sample_count, constituents):
    sample_index = jnp.arange(sample_count, dtype=jnp.int32)
    harmonic = jnp.arange(1, constituents + 1, dtype=jnp.int32)
    wrapped_turns = sample_index[:, None] * harmonic[None, :] % sample_count
    phase_angle = wrapped_turns.astype(jnp.float32) * (2.0 * math.pi / sample_count)
    table = jnp.stack([jnp.cos(phase_angle), jnp.sin(phase_angle)], axis=2)
    return table.reshape(sample_count, 2 * constituents)


def rotation_of(row_index, total_rows):
    return 0.5 + (row_index.astype(jnp.float32) + 0.5) / total_rows


def tendency(values, angular):
    cos_sin = values.reshape((values.shape[0] // 2, 2) + values.shape[1:])
    moved = jnp.stack([angular * cos_sin[:, 1], -angular * cos_sin[:, 0]], axis=1)
    return moved.reshape(values.shape)


def linear_residual(extended, tile_rows, tile_cols, angular, rotation):

    def neighbour(plane, row_step, col_step):
        return extended[
            plane,
            :,
            1 + row_step : 1 + row_step + tile_rows,
            1 + col_step : 1 + col_step + tile_cols,
        ]

    height = neighbour(0, 0, 0)
    east = neighbour(1, 0, 0)
    north = neighbour(2, 0, 0)
    res_height = (
        tendency(height, angular)
        + neighbour(3, 0, 0)
        - neighbour(3, 0, -1)
        + neighbour(4, 0, 0)
        - neighbour(4, -1, 0)
    )
    north_mean = 0.25 * (north + neighbour(2, 0, 1) + neighbour(2, -1, 0) + neighbour(2, -1, 1))
    east_mean = 0.25 * (east + neighbour(1, 0, -1) + neighbour(1, 1, 0) + neighbour(1, 1, -1))
    res_east = (
        tendency(east, angular)
        + LINEAR_DRAG * east
        - rotation * north_mean
        + GRAVITY * (neighbour(0, 0, 1) - height)
    )
    res_north = (
        tendency(north, angular)
        + LINEAR_DRAG * north
        + rotation * east_mean
        + GRAVITY * (neighbour(0, 1, 0) - height)
    )
    return jnp.stack([res_height, res_east, res_north])


def friction_row(row_block, drag_row, table):
    highest = lax.Precision.HIGHEST
    series = jnp.einsum("tc,fcn->ftn", table, row_block, precision=highest)
    base_east, base_north, step_east, step_north = (series[0], series[1], series[2], series[3])
    magnitude = jnp.sqrt(base_east * base_east + base_north * base_north + SPEED_SOFT)
    projected = (base_east * step_east + base_north * step_north) / magnitude
    force_east = drag_row * (magnitude * step_east + base_east * projected)
    force_north = drag_row * (magnitude * step_north + base_north * projected)
    forces = jnp.stack([force_east, force_north])
    analysed = jnp.einsum("tc,ftn->fcn", table, forces, precision=highest) * (2.0 / table.shape[0])
    drag_rate = drag_row * jnp.mean(magnitude, axis=0)
    return (analysed, drag_rate)


def precondition(residual, angular, rotation, drag_rate):
    shaped = residual.reshape((3, residual.shape[1] // 2, 2) + residual.shape[2:])
    cos_part = shaped[:, :, 0]
    sin_part = shaped[:, :, 1]
    height_cos = -sin_part[0] / angular
    height_sin = cos_part[0] / angular
    real_rate = drag_rate + LINEAR_DRAG
    det_real = real_rate * real_rate - angular * angular + rotation * rotation
    det_imag = 2.0 * real_rate * angular
    det_norm = det_real * det_real + det_imag * det_imag
    inv_real = det_real / det_norm
    inv_imag = -det_imag / det_norm
    east_re = cos_part[1]
    east_im = -sin_part[1]
    north_re = cos_part[2]
    north_im = -sin_part[2]
    num_east_re = real_rate * east_re - angular * east_im + rotation * north_re
    num_east_im = real_rate * east_im + angular * east_re + rotation * north_im
    num_north_re = -rotation * east_re + real_rate * north_re - angular * north_im
    num_north_im = -rotation * east_im + real_rate * north_im + angular * north_re
    east_out_re = num_east_re * inv_real - num_east_im * inv_imag
    east_out_im = num_east_re * inv_imag + num_east_im * inv_real
    north_out_re = num_north_re * inv_real - num_north_im * inv_imag
    north_out_im = num_north_re * inv_imag + num_north_im * inv_real
    cosines = jnp.stack([height_cos, east_out_re, north_out_re])
    sines = jnp.stack([height_sin, -east_out_im, -north_out_im])
    return jnp.stack([cosines, sines], axis=2).reshape(residual.shape)


def split_three(values):
    high = values.astype(jnp.bfloat16)
    rest = values - high.astype(jnp.float32)
    middle = rest.astype(jnp.bfloat16)
    low = (rest - middle.astype(jnp.float32)).astype(jnp.bfloat16)
    return high, middle, low


def friction_kernel(
    groups, stacked_ref, table_t_ref, flows_ref, drag_ref, out_ref, rate_ref, parts_ref
):
    highest = lax.Precision.HIGHEST
    stacked = stacked_ref[...]
    coefs = flows_ref.shape[1]

    def synth(field):
        high, middle, low = split_three(flows_ref[field])
        for slot, part in enumerate((high, middle, high, low, high, middle)):
            parts_ref[slot * coefs : (slot + 1) * coefs, :] = part
        return jnp.dot(stacked, parts_ref[...], preferred_element_type=jnp.float32)

    base_east, base_north, step_east, step_north = synth(0), synth(1), synth(2), synth(3)
    drag_row = drag_ref[...]
    magnitude = jnp.sqrt(base_east * base_east + base_north * base_north + SPEED_SOFT)
    projected = (base_east * step_east + base_north * step_north) / magnitude
    force_east = drag_row * (magnitude * step_east + base_east * projected)
    force_north = drag_row * (magnitude * step_north + base_north * projected)
    table_t = table_t_ref[...]
    scale = 2.0 / stacked.shape[0]
    analysed_east = (
        jnp.dot(table_t, force_east, precision=highest, preferred_element_type=jnp.float32) * scale
    )
    analysed_north = (
        jnp.dot(table_t, force_north, precision=highest, preferred_element_type=jnp.float32)
        * scale
    )
    rate_ref[...] = drag_row * jnp.mean(magnitude, axis=0, keepdims=True)
    per = coefs // groups
    for group in range(groups):
        out_ref[group, 0:per, :] = analysed_east[group * per : (group + 1) * per]
        out_ref[group, per : 2 * per, :] = analysed_north[group * per : (group + 1) * per]


def friction_band(flows_band, drag_band, table, groups, block=512):
    fields, coefs, cells = flows_band.shape
    per = coefs // groups
    table_t = jnp.transpose(table)
    high = lax.reduce_precision(table, exponent_bits=8, mantissa_bits=7)
    rest = table - high
    middle = lax.reduce_precision(rest, exponent_bits=8, mantissa_bits=7)
    low = lax.reduce_precision(rest - middle, exponent_bits=8, mantissa_bits=7)
    stacked = jnp.concatenate([high, middle, middle, high, low, high], axis=1)
    stacked = stacked.astype(jnp.bfloat16)
    return pl.pallas_call(
        functools.partial(friction_kernel, groups),
        grid=(cells // block,),
        in_specs=[
            pl.BlockSpec(stacked.shape, lambda i: (0, 0)),
            pl.BlockSpec(table_t.shape, lambda i: (0, 0)),
            pl.BlockSpec((fields, coefs, block), lambda i: (0, 0, i)),
            pl.BlockSpec((1, block), lambda i: (0, i)),
        ],
        out_specs=[
            pl.BlockSpec((groups, 2 * per, block), lambda i: (0, 0, i)),
            pl.BlockSpec((1, block), lambda i: (0, i)),
        ],
        out_shape=[
            jax.ShapeDtypeStruct((groups, 2 * per, cells), jnp.float32),
            jax.ShapeDtypeStruct((1, cells), jnp.float32),
        ],
        scratch_shapes=[pltpu.VMEM((6 * coefs, block), jnp.bfloat16)],
        compiler_params=pltpu.CompilerParams(vmem_limit_bytes=48 * 1024 * 1024),
    )(stacked, table_t, flows_band, drag_band)


def local(direction, base_flow, water_depth, drag_factor, wet_mask):
    local_coefs = direction.shape[1]
    tile_rows = direction.shape[2]
    tile_cols = direction.shape[3]
    groups = lax.axis_size("freq")
    member = lax.axis_index("freq")
    band_rows = tile_rows // groups
    band_cells = band_rows * tile_cols
    lat_place = lax.axis_index("lat")
    lat_count = lax.axis_size("lat")
    total_rows = tile_rows * lat_count
    wet_cells = wet_mask.astype(jnp.float32)
    height = direction[0] * wet_cells
    east = direction[1] * wet_cells
    north = direction[2] * wet_cells
    flows = jnp.concatenate([base_flow, jnp.stack([east, north])], axis=0)
    flows = jnp.moveaxis(flows.reshape(4, local_coefs, groups, band_cells), 2, 0)
    flows_band = lax.all_to_all(flows, "freq", split_axis=0, concat_axis=2, tiled=True)
    flows_band = flows_band.reshape(4, local_coefs * groups, band_cells)
    planes = jnp.stack([height, east, north, water_depth * east, water_depth * north])
    extended = extended_2(planes, (("lat", 2), ("lon", 3)), 1)
    rim_keep = jnp.ones((tile_rows + 2,), jnp.float32)
    rim_keep = rim_keep.at[0].set(jnp.where(lat_place == 0, 0.0, 1.0))
    rim_keep = rim_keep.at[tile_rows + 1].set(jnp.where(lat_place == lat_count - 1, 0.0, 1.0))
    extended = extended * rim_keep[:, None]
    local_count = local_coefs // 2
    first_con = member * local_count
    angular_local = OMEGA_STEP * (first_con + jnp.arange(local_count, dtype=jnp.int32) + 1).astype(
        jnp.float32
    )
    row_global = lat_place * tile_rows + jnp.arange(tile_rows, dtype=jnp.int32)
    rotation = rotation_of(row_global, total_rows)
    linear_part = linear_residual(
        extended, tile_rows, tile_cols, angular_local[:, None, None], rotation[:, None]
    )
    flows_band, linear_part = lax.optimization_barrier((flows_band, linear_part))
    table = samples_table(NTIME, NCON)
    band_start = member * band_rows
    drag_band = lax.dynamic_slice_in_dim(drag_factor, band_start, band_rows, 0)
    packed, rate = friction_band(flows_band, drag_band.reshape(1, band_cells), table, groups)
    back = lax.all_to_all(packed, "freq", split_axis=0, concat_axis=0, tiled=True)
    back = back.reshape(groups, 2 * local_coefs, band_rows, tile_cols)
    back = jnp.moveaxis(back, 0, 1).reshape(2, local_coefs, tile_rows, tile_cols)
    friction = back
    rate = jnp.broadcast_to(rate.reshape(1, band_rows, tile_cols), (groups, band_rows, tile_cols))
    drag_rate = lax.all_to_all(rate, "freq", split_axis=0, concat_axis=0, tiled=True)
    drag_rate = drag_rate.reshape(tile_rows, tile_cols)
    residual = (
        linear_part + jnp.concatenate([jnp.zeros_like(friction[:1]), friction], axis=0)
    ) * wet_cells
    return precondition(residual, angular_local[:, None, None], rotation[:, None], drag_rate)


def solution(mesh):
    placed = (
        P(None, "freq", "lat", "lon"),
        P(None, "freq", "lat", "lon"),
        P("lat", "lon"),
        P("lat", "lon"),
        P("lat", "lon"),
    )
    return jax.shard_map(
        local, mesh=mesh, in_specs=placed, out_specs=P(None, "freq", "lat", "lon"), check_vma=False
    )
```

profile of v0, /device:TPU:8, one launch (start us, length us, event | category | flops | bytes accessed | tf_op | source)
XLA Modules:
  0.0 241.2 jit_solution(7099639417852941113)
XLA Ops:
  0.0 1.0 convert_element_type.48
  1.0 2.4 %multiply_dynamic-update-slice_fusion.2 = f32[5,4,128,512]{3,2,1,0:T(8,128)} fusion(f32[3,4,128,512]{3,2,1,0:T(8,128)} %param.9, f32[128,512]{1,0:T(8,128)S(1)} %convert_element_type.48), kind=kLoop, calls=%fused_computation.35 | loop fusion | flops 262143 | bytes 2359296
  3.5 2.5 %constant_dynamic-update-slice_fusion.1 = (f32[5,4,128,512]{3,2,1,0:T(8,128)}, f32[1,4,128,512]{3,2,1,0:T(8,128)S(1)}) fusion(f32[5,4,128,512]{3,2,1,0:T(8,128)} %multiply_dynamic-update-slice_fusion.2, f32[128,512]{1,0:T(8,128)S(1)} %convert_element_type.48, f32[3,4,128,512]{3,2,1,0:T(8,128)} %param.9), kind=kLoop, calls=%fused_computation.86 | loop fusion | flops 262144 | bytes 3407872
  5.9 2.5 %constant_dynamic-update-slice_fusion = (f32[5,4,128,512]{3,2,1,0:T(8,128)}, f32[1,4,128,512]{3,2,1,0:T(8,128)S(1)}) fusion(f32[5,4,128,512]{3,2,1,0:T(8,128)} %get-tuple-element.45, f32[128,512]{1,0:T(8,128)S(1)} %convert_element_type.48, f32[3,4,128,512]{3,2,1,0:T(8,128)} %param.9), kind=kLoop, calls=%fused_computation.85 | loop fusion | flops 262144 | bytes 3407872
  8.6 1.2 concatenate.28
  9.8 2.7 %concatenate.27 = f32[2,4,8,8192]{3,2,1,0:T(8,128)} reshape(f32[2,4,128,512]{3,2,1,0:T(8,128)} %param.10) | data formatting | bytes 4194304 | tf_op jit(solution)/shard_map/concatenate | solution.py:224
  12.5 2.2 maximum_bitcast_fusion
  14.8 4.8 %copy.48 = f32[8,4,4,8192]{3,2,1,0:T(4,128)} copy(f32[8,4,4,8192]{3,0,2,1:T(8,128)S(1)} %maximum_bitcast_fusion) | data formatting | bytes 8388608 | tf_op jit(solution)/shard_map/transpose | solution.py:225
  19.6 8.6 %all-to-all-start = ((f32[8,4,4,8192]{3,2,1,0:T(4,128)}), f32[8,4,4,8192]{3,2,1,0:T(4,128)}, u32[]{:S(2)}, u32[]{:S(2)}) async-start(f32[8,4,4,8192]{3,2,1,0:T(4,128)} %copy.48), calls=%async_computation | async-start | bytes 8388608 | tf_op jit(solution)/shard_map/all_to_all | solution.py:226
  28.2 1.1 multiply_dynamic-update-slice_fusion.1
  29.3 1.2 multiply_dynamic-update-slice_fusion
  30.4 1.1 fusion.31
  31.6 2.4 collective-permute-start
  33.9 3.3 %collective-permute-start.1 = (f32[5,4,1,512]{3,2,1,0:T(1,128)S(1)}, f32[5,4,1,512]{3,2,1,0:T(1,128)S(1)}, u32[]{:S(2)}, u32[]{:S(2)}) collective-permute-start(f32[5,4,1,512]{3,2,1,0:T(1,128)S(1)} %get-tuple-element.55), channel_id=1, source_target_pairs={{4,0},{8,4},{12,8},{16,12},{20,16},{24,20},{28,24},{0,28},{5,1},{9... | collective-permute-start | bytes 122888 | tf_op jit(solution)/shard_map/ppermute | solution.py:30
  37.7 1.6 collective-permute-done
  39.3 0.4 collective-permute-done.1
  39.7 2.3 pad_maximum_fusion.4
  42.0 1.2 copy.50
  43.2 1.2 copy.51
  44.5 2.0 collective-permute-start.3
  46.6 0.5 copy.52
  47.1 0.9 collective-permute-done.3
  48.0 0.5 copy.53
  48.5 5.9 %maximum_multiply_fusion = f32[5,4,130,514]{3,2,1,0:T(8,128)S(1)} fusion(f32[5,4,130,1]{3,2,1,0:T(8,128)S(1)} %copy.53, f32[5,4,1,512]{3,2,1,0:T(1,128)S(1)} %collective-permute-done.1, f32[5,4,128,512]{3,2,1,0:T(8,128)} %multiply_dynamic-update-slice_fusion, f32[5,4,1,512]{3,2,1,0:T(1,128)S(1)} %collective-permute-done, f32[5,4,130,1]{3,2,1,0:T(8,128)S(1)} %copy.52, ...), kind=kLoop, calls=%fused_computation | loop fusion | flops 6682000 | bytes 10691720 | tf_op jit(solution)/shard_map/mul | solution.py:233
  54.4 0.4 slice.171
  55.1 1.8 slice_subtract_fusion.2
  56.8 0.4 slice_multiply_fusion.3
  57.4 2.7 %fusion.3 = (f32[1,4,128,512]{3,2,1,0:T(8,128)S(1)}, f32[1,4,128,512]{3,2,1,0:T(8,128)S(1)}) fusion(f32[5,4,130,514]{3,2,1,0:T(8,128)S(1)} %maximum_multiply_fusion, f32[128]{0:T(128)S(1)} %broadcast_multiply_fusion.1, f32[1,4,128,512]{3,2,1,0:T(8,128)S(1)} %bitcast.149, f32[1,4,128,512]{3,2,1,0:T(8,128)S(1)} %bitcast.148), kind=kLoop, calls=%fused_computation.18 | loop fusion | flops 4718592 | bytes 15729152 | tf_op jit(solution)/shard_map/add | solution.py:77
  60.1 0.3 pad_maximum_fusion
  60.4 64.1 %all-to-all-done = f32[8,4,4,8192]{3,2,1,0:T(4,128)} async-done(((f32[8,4,4,8192]{3,2,1,0:T(4,128)}), f32[8,4,4,8192]{3,2,1,0:T(4,128)}, u32[]{:S(2)}, u32[]{:S(2)}) %all-to-all-start) | async-done | bytes 4194336 | tf_op jit(solution)/shard_map/all_to_all | solution.py:226
  124.5 4.6 %copy.49 = f32[1,4,8,4,8192]{4,3,2,1,0:T(4,128)} copy(f32[1,4,8,4,8192]{4,3,1,2,0:T(4,128)} %bitcast.2) | data formatting | bytes 8388608 | tf_op jit(solution)/shard_map/all_to_all | solution.py:226
  129.1 5.4 %reshape.518.flows_ref = f32[4,32,8192]{2,1,0:T(8,128)} reshape(f32[1,4,8,4,8192]{4,3,2,1,0:T(4,128)} %copy.49) | data formatting | bytes 8388608 | tf_op jit(solution)/shard_map/reshape | solution.py:227
  134.5 26.2 %shard_map.55 = (f32[8,8,8192]{2,1,0:T(8,128)}, f32[1,8192]{1,0:T(1,128)S(1)}) custom-call(bf16[256,192]{1,0:T(8,128)(2,1)S(1)} %copy.55.stacked_ref, f32[32,256]{1,0:T(8,128)S(1)} %bitcast.142, f32[4,32,8192]{2,1,0:T(8,128)} %reshape.518.flows_ref, f32[1,8192]{1,0:T(1,128)S(1)} %bitcast.143), custom_call_target="tpu_custom_call" | custom-call | tf_op jit(solution)/shard_map/pallas_call | solution.py:187
  160.7 0.5 broadcast.546
  161.3 0.7 reduce.7
  162.0 15.4 %all_to_all.25 = f32[8,16,512]{2,1,0:T(8,128)} all-to-all(f32[8,16,512]{2,1,0:T(8,128)S(1)} %broadcast_in_dim.5), channel_id=1, replica_groups=mesh['freq'=8,'lat'=8,'lon'=4] {'freq'}, dimensions={0} | all-to-all | bytes 524288 | tf_op jit(solution)/shard_map/all_to_all | solution.py:254
  177.4 4.6 %all-to-all-start.1 = ((f32[8,8,8192]{2,1,0:T(8,128)}), f32[8,8,8192]{2,1,0:T(8,128)}, u32[]{:S(2)}, u32[]{:S(2)}) async-start(f32[8,8,8192]{2,1,0:T(8,128)} %get-tuple-element.35), calls=%async_computation.1 | async-start | bytes 4194304 | tf_op jit(solution)/shard_map/all_to_all | solution.py:249
  182.0 1.0 broadcast_add_fusion
  183.1 0.7 copy-done.6
  183.7 0.8 bitcast_multiply_fusion
  184.6 48.8 %all-to-all-done.1 = f32[8,8,8192]{2,1,0:T(8,128)} async-done(((f32[8,8,8192]{2,1,0:T(8,128)}), f32[8,8,8192]{2,1,0:T(8,128)}, u32[]{:S(2)}, u32[]{:S(2)}) %all-to-all-start.1) | async-done | bytes 2097184 | tf_op jit(solution)/shard_map/all_to_all | solution.py:249
  233.4 2.8 %copy.56 = f32[8,8,16,512]{3,2,0,1:T(8,128)S(1)} copy(f32[8,8,16,512]{3,1,2,0:T(8,128)} %bitcast.12) | data formatting | bytes 4194304 | tf_op jit(solution)/shard_map/reshape | solution.py:250
  236.3 0.7 add_multiply_fusion
  236.9 0.2 copy-done.4
  237.3 0.8 multiply_subtract_fusion.2
  238.2 0.4 add_negate_fusion.1
  238.9 0.3 pad_maximum_fusion.1
  239.2 2.0 copy.62
  (48 shorter events, 1.7 us)
Async XLA Ops:
  0.0 37.5 %copy-start = (f32[128,512]{1,0:T(8,128)S(1)}, f32[128,512]{1,0:T(8,128)}, u32[]{:S(2)}) copy-start(f32[128,512]{1,0:T(8,128)} %param.12) | copy-start | bytes 786436
  1.0 7.4 %copy-start.2 = (f32[128,512]{1,0:T(8,128)}, f32[128,512]{1,0:T(8,128)S(1)}, u32[]{:S(2)}) copy-start(f32[128,512]{1,0:T(8,128)S(1)} %convert_element_type.48) | copy-start | bytes 786436
  19.6 8.6 %copy-start.8 = (f32[128,512]{1,0:T(8,128)S(1)}, f32[128,512]{1,0:T(8,128)}, u32[]{:S(2)}) copy-start(f32[128,512]{1,0:T(8,128)} %param.11) | copy-start | bytes 786436
  19.6 105.0 %all-to-all-start = ((f32[8,4,4,8192]{3,2,1,0:T(4,128)}), f32[8,4,4,8192]{3,2,1,0:T(4,128)}, u32[]{:S(2)}, u32[]{:S(2)}) async-start(f32[8,4,4,8192]{3,2,1,0:T(4,128)} %copy.48), calls=%async_computation | async-start | bytes 8388608 | tf_op jit(solution)/shard_map/all_to_all | solution.py:226
  31.6 7.7 %collective-permute-start = (f32[5,4,1,512]{3,2,1,0:T(1,128)S(1)}, f32[5,4,1,512]{3,2,1,0:T(1,128)S(1)}, u32[]{:S(2)}, u32[]{:S(2)}) collective-permute-start(f32[5,4,1,512]{3,2,1,0:T(1,128)S(1)} %get-tuple-element.54), channel_id=1, source_target_pairs={{0,4},{4,8},{8,12},{12,16},{16,20},{20,24},{24,28},{28,0},{1,5},{5... | collective-permute-start | bytes 122888 | tf_op jit(solution)/shard_map/ppermute | solution.py:27
  33.9 5.8 %collective-permute-start.1 = (f32[5,4,1,512]{3,2,1,0:T(1,128)S(1)}, f32[5,4,1,512]{3,2,1,0:T(1,128)S(1)}, u32[]{:S(2)}, u32[]{:S(2)}) collective-permute-start(f32[5,4,1,512]{3,2,1,0:T(1,128)S(1)} %get-tuple-element.55), channel_id=1, source_target_pairs={{4,0},{8,4},{12,8},{16,12},{20,16},{24,20},{28,24},{0,28},{5,1},{9... | collective-permute-start | bytes 122888 | tf_op jit(solution)/shard_map/ppermute | solution.py:30
  43.2 3.4 %collective-permute-start.2 = (f32[5,4,130,1]{2,0,3,1:T(8,128)S(1)}, f32[5,4,130,1]{2,0,3,1:T(8,128)S(1)}, u32[]{:S(2)}, u32[]{:S(2)}) collective-permute-start(f32[5,4,130,1]{2,0,3,1:T(8,128)S(1)} %copy.50), channel_id=1, source_target_pairs={{0,1},{1,2},{2,3},{3,0},{4,5},{5,6},{6,7},{7,4},{8,9},{9,10},{10,1... | collective-permute-start | bytes 31208 | tf_op jit(solution)/shard_map/ppermute | solution.py:27
  44.5 3.6 %collective-permute-start.3 = (f32[5,4,130,1]{2,0,3,1:T(8,128)S(1)}, f32[5,4,130,1]{2,0,3,1:T(8,128)S(1)}, u32[]{:S(2)}, u32[]{:S(2)}) collective-permute-start(f32[5,4,130,1]{2,0,3,1:T(8,128)S(1)} %copy.51), channel_id=1, source_target_pairs={{1,0},{2,1},{3,2},{0,3},{5,4},{6,5},{7,6},{4,7},{9,8},{10,9},{11,1... | collective-permute-start | bytes 31208 | tf_op jit(solution)/shard_map/ppermute | solution.py:30
  177.4 56.0 %all-to-all-start.1 = ((f32[8,8,8192]{2,1,0:T(8,128)}), f32[8,8,8192]{2,1,0:T(8,128)}, u32[]{:S(2)}, u32[]{:S(2)}) async-start(f32[8,8,8192]{2,1,0:T(8,128)} %get-tuple-element.35), calls=%async_computation.1 | async-start | bytes 4194304 | tf_op jit(solution)/shard_map/all_to_all | solution.py:249
  182.0 54.2 %copy-start.3 = (f32[128,512]{1,0:T(8,128)S(1)}, f32[128,512]{1,0:T(8,128)}, u32[]{:S(2)}) copy-start(f32[128,512]{1,0:T(8,128)} %copy-done.2) | copy-start | bytes 786436
  183.0 0.7 copy-start.6
  236.2 1.0 copy-start.4
  236.2 1.0 copy-start.5
  236.2 1.1 copy-start.7
  238.9 2.3 copy-start.1
where the time goes:
time: 242 us; the launch traced here: 241 us
  waiting for transfers between devices  116 us (48%)
  other arithmetic  31.9 us (13%)
  local copies, waits for them, and re-layouts  30.5 us (13%)
  Pallas kernels  26.2 us (11%)
  starting transfers between devices  20.9 us (9%)
  blocking collectives  15.4 us (6%)
    all_to_all x1, waiting for transfers between devices, local(): lax.all_to_all(flows, 'freq', split_axis=0, concat_axis=2, tiled=True)  64.1 us
    all_to_all x1, waiting for transfers between devices, local(): lax.all_to_all(packed, 'freq', split_axis=0, concat_axis=0, tiled=True)  48.8 us
    pallas_call x1, Pallas kernels, friction_band(): pl.pallas_call(functools.partial(friction_kernel, groups), grid=(cells //...  26.2 us
    all_to_all x1, blocking collectives, local(): lax.all_to_all(rate, 'freq', split_axis=0, concat_axis=0, tiled=True)  15.4 us
    all_to_all x1, starting transfers between devices, local(): lax.all_to_all(flows, 'freq', split_axis=0, concat_axis=2, tiled=True)  8.6 us
    unnamed x9, other arithmetic  8.56 us
    mul x1, other arithmetic, local(): extended = extended * rim_keep[:, None]  5.89 us
    reshape x1, local copies, waits for them, and re-layouts, local(): flows_band = flows_band.reshape(4, local_coefs * groups, band_cells)  5.39 us
  transfers between devices with their start and end apart: 6, of which 5 were waited for; matrix products, arithmetic and copies ran while one was open for 10% of the time, Pallas kernels for 0%

commit v1 on v0

--- a/solution.py
+++ b/solution.py
@@ -140,14 +140,19 @@
 
 
 def friction_kernel(
-    groups, stacked_ref, table_t_ref, flows_ref, drag_ref, out_ref, rate_ref, parts_ref
+    groups, stacked_ref, table_t_ref, flows_ref, drag_ref, out_ref, rate_ref, gather_ref, parts_ref
 ):
     highest = lax.Precision.HIGHEST
     stacked = stacked_ref[...]
-    coefs = flows_ref.shape[1]
+    coefs = gather_ref.shape[0]
+    per = coefs // groups
 
     def synth(field):
-        high, middle, low = split_three(flows_ref[field])
+        for source in range(groups):
+            gather_ref[source * per : (source + 1) * per, :] = flows_ref[
+                source, field * per : (field + 1) * per, :
+            ]
+        high, middle, low = split_three(gather_ref[...])
         for slot, part in enumerate((high, middle, high, low, high, middle)):
             parts_ref[slot * coefs : (slot + 1) * coefs, :] = part
         return jnp.dot(stacked, parts_ref[...], preferred_element_type=jnp.float32)
@@ -168,14 +173,14 @@
         * scale
     )
     rate_ref[...] = drag_row * jnp.mean(magnitude, axis=0, keepdims=True)
-    per = coefs // groups
     for group in range(groups):
         out_ref[group, 0:per, :] = analysed_east[group * per : (group + 1) * per]
         out_ref[group, per : 2 * per, :] = analysed_north[group * per : (group + 1) * per]
 
 
-def friction_band(flows_band, drag_band, table, groups, block=512):
-    fields, coefs, cells = flows_band.shape
+def friction_band(flows_band, drag_band, table, block):
+    groups, rows_in, cells = flows_band.shape
+    coefs = table.shape[1]
     per = coefs // groups
     table_t = jnp.transpose(table)
     high = lax.reduce_precision(table, exponent_bits=8, mantissa_bits=7)
@@ -184,36 +189,41 @@
     low = lax.reduce_precision(rest - middle, exponent_bits=8, mantissa_bits=7)
     stacked = jnp.concatenate([high, middle, middle, high, low, high], axis=1)
     stacked = stacked.astype(jnp.bfloat16)
+    steps = cells // block
     return pl.pallas_call(
         functools.partial(friction_kernel, groups),
-        grid=(cells // block,),
+        grid=(steps,),
         in_specs=[
             pl.BlockSpec(stacked.shape, lambda i: (0, 0)),
             pl.BlockSpec(table_t.shape, lambda i: (0, 0)),
-            pl.BlockSpec((fields, coefs, block), lambda i: (0, 0, i)),
+            pl.BlockSpec((groups, rows_in, block), lambda i: (0, 0, i)),
             pl.BlockSpec((1, block), lambda i: (0, i)),
         ],
         out_specs=[
             pl.BlockSpec((groups, 2 * per, block), lambda i: (0, 0, i)),
-            pl.BlockSpec((1, block), lambda i: (0, i)),
+            pl.BlockSpec((pl.Squeezed(), 1, block), lambda i: (i, 0, 0)),
         ],
         out_shape=[
             jax.ShapeDtypeStruct((groups, 2 * per, cells), jnp.float32),
-            jax.ShapeDtypeStruct((1, cells), jnp.float32),
-        ],
-        scratch_shapes=[pltpu.VMEM((6 * coefs, block), jnp.bfloat16)],
+            jax.ShapeDtypeStruct((steps, 1, block), jnp.float32),
+        ],
+        scratch_shapes=[
+            pltpu.VMEM((coefs, block), jnp.float32),
+            pltpu.VMEM((6 * coefs, block), jnp.bfloat16),
+        ],
         compiler_params=pltpu.CompilerParams(vmem_limit_bytes=48 * 1024 * 1024),
     )(stacked, table_t, flows_band, drag_band)
 
 
-def local(direction, base_flow, water_depth, drag_factor, wet_mask):
+def local(direction, base_flow, water_depth, drag_factor, wet_mask, pieces=2):
     local_coefs = direction.shape[1]
     tile_rows = direction.shape[2]
     tile_cols = direction.shape[3]
     groups = lax.axis_size("freq")
     member = lax.axis_index("freq")
     band_rows = tile_rows // groups
-    band_cells = band_rows * tile_cols
+    piece_rows = band_rows // pieces
+    piece_cells = piece_rows * tile_cols
     lat_place = lax.axis_index("lat")
     lat_count = lax.axis_size("lat")
     total_rows = tile_rows * lat_count
@@ -222,9 +232,15 @@
     east = direction[1] * wet_cells
     north = direction[2] * wet_cells
     flows = jnp.concatenate([base_flow, jnp.stack([east, north])], axis=0)
-    flows = jnp.moveaxis(flows.reshape(4, local_coefs, groups, band_cells), 2, 0)
-    flows_band = lax.all_to_all(flows, "freq", split_axis=0, concat_axis=2, tiled=True)
-    flows_band = flows_band.reshape(4, local_coefs * groups, band_cells)
+    flows = flows.reshape(4 * local_coefs, groups, pieces, piece_rows, tile_cols)
+    table = samples_table(NTIME, NCON)
+    band_start = member * band_rows
+    drag_band = lax.dynamic_slice_in_dim(drag_factor, band_start, band_rows, 0)
+    drag_band = drag_band.reshape(pieces, 1, piece_cells)
+    sent = []
+    for piece in range(pieces):
+        payload = jnp.moveaxis(flows[:, :, piece], 1, 0).reshape(groups, 4 * local_coefs, piece_cells)
+        sent.append(lax.all_to_all(payload, "freq", split_axis=0, concat_axis=0, tiled=True))
     planes = jnp.stack([height, east, north, water_depth * east, water_depth * north])
     extended = extended_2(planes, (("lat", 2), ("lon", 3)), 1)
     rim_keep = jnp.ones((tile_rows + 2,), jnp.float32)
@@ -241,18 +257,22 @@
     linear_part = linear_residual(
         extended, tile_rows, tile_cols, angular_local[:, None, None], rotation[:, None]
     )
-    flows_band, linear_part = lax.optimization_barrier((flows_band, linear_part))
-    table = samples_table(NTIME, NCON)
-    band_start = member * band_rows
-    drag_band = lax.dynamic_slice_in_dim(drag_factor, band_start, band_rows, 0)
-    packed, rate = friction_band(flows_band, drag_band.reshape(1, band_cells), table, groups)
-    back = lax.all_to_all(packed, "freq", split_axis=0, concat_axis=0, tiled=True)
-    back = back.reshape(groups, 2 * local_coefs, band_rows, tile_cols)
-    back = jnp.moveaxis(back, 0, 1).reshape(2, local_coefs, tile_rows, tile_cols)
-    friction = back
-    rate = jnp.broadcast_to(rate.reshape(1, band_rows, tile_cols), (groups, band_rows, tile_cols))
-    drag_rate = lax.all_to_all(rate, "freq", split_axis=0, concat_axis=0, tiled=True)
-    drag_rate = drag_rate.reshape(tile_rows, tile_cols)
+    frictions, rates = [], []
+    for piece in range(pieces):
+        packed, rate = friction_band(sent[piece], drag_band[piece], table, tile_cols)
+        rate = jnp.broadcast_to(
+            rate.reshape(1, 1, piece_cells).reshape(1, 2 * local_coefs, piece_cells // (2 * local_coefs)),
+            (groups, 2 * local_coefs, piece_cells // (2 * local_coefs)),
+        )
+        payload = jnp.concatenate([packed, rate], axis=2)
+        back = lax.all_to_all(payload, "freq", split_axis=0, concat_axis=0, tiled=True)
+        frictions.append(
+            back[:, :, :piece_cells].reshape(groups, 2 * local_coefs, piece_rows, tile_cols)
+        )
+        rates.append(back[:, :, piece_cells:].reshape(groups, piece_rows, tile_cols))
+    friction = jnp.stack(frictions, axis=2)
+    friction = jnp.moveaxis(friction, 0, 1).reshape(2, local_coefs, tile_rows, tile_cols)
+    drag_rate = jnp.stack(rates, axis=1).reshape(tile_rows, tile_cols)
     residual = (
         linear_part + jnp.concatenate([jnp.zeros_like(friction[:1]), friction], axis=0)
     ) * wet_cells

time: 242 us -> 224 us (0.926)
  waiting for transfers between devices: 116 us -> 99.3 us
  blocking collectives: 15.4 us -> 0 us
  starting transfers between devices: 20.9 us -> 29.8 us
    all_to_all x2 -> x4, waiting for transfers between devices: 113 us -> 94.1 us  [local(): lax.all_to_all(payload, 'freq', split_axis=0, concat_axis=0, tiled=True)]
    all_to_all x1 -> x0, blocking collectives: 15.4 us -> none  [local(): lax.all_to_all(rate, 'freq', split_axis=0, concat_axis=0, tiled=True)]
    all_to_all x2 -> x4, starting transfers between devices: 13.2 us -> 23.5 us  [local(): lax.all_to_all(payload, 'freq', split_axis=0, concat_axis=0, tiled=True)]
    unnamed x20 -> x33, local copies, waits for them, and re-layouts: 1.17 us -> 7.79 us
    transpose x1 -> x0, local copies, waits for them, and re-layouts: 4.78 us -> none  [local(): jnp.moveaxis(flows.reshape(4, local_coefs, groups, band_cells), 2, 0)]
    all_to_all x1 -> x0, local copies, waits for them, and re-layouts: 4.6 us -> none  [local(): lax.all_to_all(flows, 'freq', split_axis=0, concat_axis=2, tiled=True)]
    slice x0 -> x3, local copies, waits for them, and re-layouts: none -> 4.45 us  [the longest x2 2.68 us: local(): back[:, :, :piece_cells]]
    concatenate x3 -> x0, local copies, waits for them, and re-layouts: 4.09 us -> none  [local(): flows = jnp.concatenate([base_flow, jnp.stack([east, north])], axis=0)]
  transfers between devices with their start and end apart: 6 -> 8, of which waited for: 5 -> 6; matrix products, arithmetic and copies ran while one was open for 10% -> 19% of each run, Pallas kernels for 0% -> 12%
where the time goes in v1:
time: 224 us; the launch traced here: 222 us
  waiting for transfers between devices  99.3 us (44%)
  other arithmetic  34 us (15%)
  local copies, waits for them, and re-layouts  32.6 us (15%)
  starting transfers between devices  29.8 us (13%)
  Pallas kernels  25.6 us (11%)
    all_to_all x4, waiting for transfers between devices, local(): lax.all_to_all(payload, 'freq', split_axis=0, concat_axis=0, tiled=True)  94.1 us
    pallas_call x2, Pallas kernels, friction_band(): pl.pallas_call(functools.partial(friction_kernel, groups), grid=(steps,),...  25.6 us
    all_to_all x4, starting transfers between devices, local(): lax.all_to_all(payload, 'freq', split_axis=0, concat_axis=0, tiled=True)  23.5 us
    unnamed x9, other arithmetic  9.74 us
    unnamed x33, local copies, waits for them, and re-layouts  7.79 us
    mul x1, other arithmetic, local(): extended = extended * rim_keep[:, None]  5.89 us
    ppermute x2, waiting for transfers between devices, extended_2(): lax.ppermute(lax.slice_in_dim(block, block.shape[dim] - width, None, axis...  4.83 us
  transfers between devices with their start and end apart: 8, of which 6 were waited for; matrix products, arithmetic and copies ran while one was open for 19% of the time, Pallas kernels for 12%

profile of v1, /device:TPU:8, one launch (start us, length us, event | category | flops | bytes accessed | tf_op | source)
XLA Modules:
  0.0 221.8 jit_solution(4073276026093998897)
XLA Ops:
  0.0 1.0 convert_element_type.50
  1.0 2.4 %multiply_dynamic-update-slice_fusion.2 = f32[5,4,128,512]{3,2,1,0:T(8,128)} fusion(f32[3,4,128,512]{3,2,1,0:T(8,128)} %param.9, f32[128,512]{1,0:T(8,128)S(1)} %convert_element_type.50), kind=kLoop, calls=%fused_computation.42 | loop fusion | flops 262143 | bytes 2359296
  3.4 2.6 %constant_dynamic-update-slice_fusion.1 = (f32[5,4,128,512]{3,2,1,0:T(8,128)}, f32[1,4,128,512]{3,2,1,0:T(8,128)S(1)}) fusion(f32[5,4,128,512]{3,2,1,0:T(8,128)} %multiply_dynamic-update-slice_fusion.2, f32[128,512]{1,0:T(8,128)S(1)} %convert_element_type.50, f32[3,4,128,512]{3,2,1,0:T(8,128)} %param.9), kind=kLoop, calls=%fused_computation.92 | loop fusion | flops 262144 | bytes 3407872
  6.1 2.5 %constant_dynamic-update-slice_fusion = (f32[5,4,128,512]{3,2,1,0:T(8,128)}, f32[1,4,128,512]{3,2,1,0:T(8,128)S(1)}) fusion(f32[5,4,128,512]{3,2,1,0:T(8,128)} %get-tuple-element.45, f32[128,512]{1,0:T(8,128)S(1)} %convert_element_type.50, f32[3,4,128,512]{3,2,1,0:T(8,128)} %param.9), kind=kLoop, calls=%fused_computation.91 | loop fusion | flops 262144 | bytes 3407872
  8.6 0.6 pad_maximum_fusion
  9.2 0.6 copy-done.2
  9.8 1.8 fusion.33
  11.8 1.5 reshape.524
  13.4 8.5 %all-to-all-start = ((f32[8,16,4096]{2,1,0:T(8,128)}), f32[8,16,4096]{2,1,0:T(8,128)S(1)}, u32[]{:S(2)}, u32[]{:S(2)}) async-start(f32[8,16,4096]{2,1,0:T(8,128)} %reshape.524), calls=%async_computation | async-start | bytes 4194304 | tf_op jit(solution)/shard_map/all_to_all | solution.py:243
  21.8 3.2 %copy.104 = f32[16,8,1,8,512]{4,3,0,1,2:T(8,128)} copy(f32[16,8,1,8,512]{4,3,2,1,0:T(8,128)} %get-tuple-element.57) | data formatting | bytes 4194304
  25.0 2.7 %reshape.525 = f32[8,16,4096]{2,1,0:T(8,128)} reshape(f32[8,16,8,512]{3,2,1,0:T(8,128)} %bitcast.168) | data formatting | bytes 4194304 | tf_op jit(solution)/shard_map/reshape | solution.py:242
  27.8 45.3 %all-to-all-done.flows_ref = f32[8,16,4096]{2,1,0:T(8,128)S(1)} async-done(((f32[8,16,4096]{2,1,0:T(8,128)}), f32[8,16,4096]{2,1,0:T(8,128)S(1)}, u32[]{:S(2)}, u32[]{:S(2)}) %all-to-all-start) | async-done | bytes 2097184 | tf_op jit(solution)/shard_map/all_to_all | solution.py:243
  73.0 1.3 copy-done
  74.4 3.6 %all-to-all-start.2 = ((f32[8,16,4096]{2,1,0:T(8,128)}), f32[8,16,4096]{2,1,0:T(8,128)S(1)}, u32[]{:S(2)}, u32[]{:S(2)}) async-start(f32[8,16,4096]{2,1,0:T(8,128)} %reshape.525), calls=%async_computation.2 | async-start | bytes 4194304 | tf_op jit(solution)/shard_map/all_to_all | solution.py:243
  78.0 0.7 dynamic-slice_bitcast_fusion.1
  79.2 1.6 copy-done.1
  80.8 12.8 %shard_map.55 = (f32[8,8,4096]{2,1,0:T(8,128)S(1)}, f32[8,1,512]{2,1,0:T(1,128)S(1)}) custom-call(bf16[256,192]{1,0:T(8,128)(2,1)S(1)} %copy.77.stacked_ref, f32[32,256]{1,0:T(8,128)S(1)} %bitcast.161, f32[8,16,4096]{2,1,0:T(8,128)S(1)} %copy-done.1, f32[1,4096]{1,0:T(1,128)S(1)} %bitcast.163), custom_call_target="tpu_custom_call" | custom-call | tf_op jit(solution)/shard_map/pallas_call | solution.py:193
  93.6 1.2 pad_maximum_fusion.6
  94.8 32.6 %all-to-all-done.2.flows_ref = f32[8,16,4096]{2,1,0:T(8,128)S(1)} async-done(((f32[8,16,4096]{2,1,0:T(8,128)}), f32[8,16,4096]{2,1,0:T(8,128)S(1)}, u32[]{:S(2)}, u32[]{:S(2)}) %all-to-all-start.2) | async-done | bytes 2097184 | tf_op jit(solution)/shard_map/all_to_all | solution.py:243
  127.4 4.3 %all-to-all-start.1 = ((f32[8,8,4608]{2,1,0:T(8,128)}), f32[8,8,4608]{2,1,0:T(8,128)}, u32[]{:S(2)}, u32[]{:S(2)}) async-start(f32[8,8,4608]{2,1,0:T(8,128)} %pad_maximum_fusion.6), calls=%async_computation.1 | async-start | bytes 2359296 | tf_op jit(solution)/shard_map/all_to_all | solution.py:268
  131.7 2.1 multiply_dynamic-update-slice_fusion.1
  133.8 2.4 %multiply_dynamic-update-slice_fusion = f32[5,4,128,512]{3,2,1,0:T(8,128)} fusion(f32[5,4,128,512]{3,2,1,0:T(8,128)} %multiply_dynamic-update-slice_fusion.1, f32[1,4,128,512]{3,2,1,0:T(8,128)} %copy-done.2, f32[128,512]{1,0:T(8,128)} %param.11), kind=kLoop, calls=%fused_computation.38 | loop fusion | flops 262144 | bytes 2359296 | tf_op jit(solution)/shard_map/stack | solution.py:244
  136.2 1.1 fusion.32
  137.3 2.4 %collective-permute-start = (f32[5,4,1,512]{3,2,1,0:T(1,128)S(1)}, f32[5,4,1,512]{3,2,1,0:T(1,128)S(1)}, u32[]{:S(2)}, u32[]{:S(2)}) collective-permute-start(f32[5,4,1,512]{3,2,1,0:T(1,128)S(1)} %get-tuple-element.54), channel_id=1, source_target_pairs={{0,4},{4,8},{8,12},{12,16},{16,20},{20,24},{24,28},{28,0},{1,5},{5... | collective-permute-start | bytes 122888 | tf_op jit(solution)/shard_map/ppermute | solution.py:27
  139.7 3.3 %collective-permute-start.1 = (f32[5,4,1,512]{3,2,1,0:T(1,128)S(1)}, f32[5,4,1,512]{3,2,1,0:T(1,128)S(1)}, u32[]{:S(2)}, u32[]{:S(2)}) collective-permute-start(f32[5,4,1,512]{3,2,1,0:T(1,128)S(1)} %get-tuple-element.55), channel_id=1, source_target_pairs={{4,0},{8,4},{12,8},{16,12},{20,16},{24,20},{28,24},{0,28},{5,1},{9... | collective-permute-start | bytes 122888 | tf_op jit(solution)/shard_map/ppermute | solution.py:30
  143.1 1.9 collective-permute-done
  145.5 3.9 %pad_maximum_fusion.5 = (f32[5,4,130,1]{3,2,1,0:T(8,128)}, f32[5,4,130,1]{3,2,1,0:T(8,128)}) fusion(f32[5,4,1,512]{3,2,1,0:T(1,128)S(1)} %collective-permute-done.1, f32[5,4,128,512]{3,2,1,0:T(8,128)} %multiply_dynamic-update-slice_fusion, f32[5,4,1,512]{3,2,1,0:T(1,128)S(1)} %collective-permute-done), kind=kLoop, calls=%fused_computation.12 | loop fusion | flops 10400 | bytes 5345600 | tf_op jit(solution)/shard_map/slice | solution.py:28
  149.3 2.5 %copy.71 = f32[5,4,130,1]{2,0,3,1:T(8,128)S(1)} copy(f32[5,4,130,1]{3,2,1,0:T(8,128)} %get-tuple-element.52) | data formatting | bytes 20800 | tf_op jit(solution)/shard_map/slice | solution.py:28
  151.9 2.6 %copy.72 = f32[5,4,130,1]{2,0,3,1:T(8,128)S(1)} copy(f32[5,4,130,1]{3,2,1,0:T(8,128)} %get-tuple-element.53) | data formatting | bytes 20800 | tf_op jit(solution)/shard_map/slice | solution.py:30
  155.0 2.9 %collective-permute-done.2 = f32[5,4,130,1]{2,0,3,1:T(8,128)S(1)} collective-permute-done((f32[5,4,130,1]{2,0,3,1:T(8,128)S(1)}, f32[5,4,130,1]{2,0,3,1:T(8,128)S(1)}, u32[]{:S(2)}, u32[]{:S(2)}) %collective-permute-start.2) | collective-permute-done | bytes 10432 | tf_op jit(solution)/shard_map/ppermute | solution.py:27
  157.9 1.6 copy.73
  159.6 1.6 copy.74
  161.2 12.8 %shard_map.56 = (f32[8,8,4096]{2,1,0:T(8,128)S(1)}, f32[8,1,512]{2,1,0:T(1,128)S(1)}) custom-call(bf16[256,192]{1,0:T(8,128)(2,1)S(1)} %copy.77.stacked_ref, f32[32,256]{1,0:T(8,128)S(1)} %bitcast.162, f32[8,16,4096]{2,1,0:T(8,128)S(1)} %all-to-all-done.2.flows_ref, f32[1,4096]{1,0:T(1,128)S(1)} %bitcast.164), custom_call_target="tpu_custom_call" | custom-call | tf_op jit(solution)/shard_map/pallas_call | solution.py:193
  174.0 1.1 pad_maximum_fusion.7
  175.2 7.2 %all-to-all-start.3 = ((f32[8,8,4608]{2,1,0:T(8,128)}), f32[8,8,4608]{2,1,0:T(8,128)}, u32[]{:S(2)}, u32[]{:S(2)}) async-start(f32[8,8,4608]{2,1,0:T(8,128)} %pad_maximum_fusion.7), calls=%async_computation.3 | async-start | bytes 2359296 | tf_op jit(solution)/shard_map/all_to_all | solution.py:268
  182.4 5.9 %maximum_multiply_fusion = f32[5,4,130,514]{3,2,1,0:T(8,128)S(1)} fusion(f32[5,4,130,1]{3,2,1,0:T(8,128)S(1)} %copy-done.6, f32[5,4,1,512]{3,2,1,0:T(1,128)S(1)} %copy-done.12, f32[5,4,128,512]{3,2,1,0:T(8,128)} %multiply_dynamic-update-slice_fusion, f32[5,4,1,512]{3,2,1,0:T(1,128)S(1)} %copy-done.10, f32[5,4,130,1]{3,2,1,0:T(8,128)S(1)} %copy-done.5, ...), kind=kLoop, calls=%fused_computation | loop fusion | flops 6682000 | bytes 10691720 | tf_op jit(solution)/shard_map/mul | solution.py:249
  189.0 1.8 slice_subtract_fusion.2
  191.3 2.7 %fusion.4 = (f32[1,4,128,512]{3,2,1,0:T(8,128)S(1)}, f32[1,4,128,512]{3,2,1,0:T(8,128)S(1)}) fusion(f32[5,4,130,514]{3,2,1,0:T(8,128)S(1)} %maximum_multiply_fusion, f32[128]{0:T(128)S(1)} %broadcast_multiply_fusion.1, f32[1,4,128,512]{3,2,1,0:T(8,128)S(1)} %bitcast.173, f32[1,4,128,512]{3,2,1,0:T(8,128)S(1)} %bitcast.172), kind=kLoop, calls=%fused_computation.23 | loop fusion | flops 4718592 | bytes 15729152 | tf_op jit(solution)/shard_map/add | solution.py:77
  194.0 1.3 slice.227
  195.3 1.6 copy.80
  196.9 16.2 %all-to-all-done.3 = f32[8,8,4608]{2,1,0:T(8,128)} async-done(((f32[8,8,4608]{2,1,0:T(8,128)}), f32[8,8,4608]{2,1,0:T(8,128)}, u32[]{:S(2)}, u32[]{:S(2)}) %all-to-all-start.3) | async-done | bytes 1179680 | tf_op jit(solution)/shard_map/all_to_all | solution.py:268
  213.1 1.4 slice.229
  214.5 0.6 copy.81
  215.1 0.9 slice_bitcast_fusion.7
  216.0 1.0 slice_bitcast_fusion.6
  217.3 0.7 fusion
  218.0 0.8 multiply_subtract_fusion.2
  219.9 2.0 copy.88
  (68 shorter events, 4.3 us)
Async XLA Ops:
  1.0 7.6 %copy-start.3 = (f32[128,512]{1,0:T(8,128)}, f32[128,512]{1,0:T(8,128)S(1)}, u32[]{:S(2)}) copy-start(f32[128,512]{1,0:T(8,128)S(1)} %convert_element_type.50) | copy-start | bytes 786436
  3.4 5.2 %copy-start.8 = (f32[2,4,128,512]{3,2,1,0:T(8,128)S(1)}, f32[2,4,128,512]{3,2,1,0:T(8,128)}, u32[]{:S(2)}) copy-start(f32[2,4,128,512]{3,2,1,0:T(8,128)} %param.10) | copy-start | bytes 6291460
  8.6 1.2 copy-start.2
  13.4 59.7 %all-to-all-start = ((f32[8,16,4096]{2,1,0:T(8,128)}), f32[8,16,4096]{2,1,0:T(8,128)S(1)}, u32[]{:S(2)}, u32[]{:S(2)}) async-start(f32[8,16,4096]{2,1,0:T(8,128)} %reshape.524), calls=%async_computation | async-start | bytes 4194304 | tf_op jit(solution)/shard_map/all_to_all | solution.py:243
  73.0 1.3 copy-start
  74.4 53.0 %all-to-all-start.2 = ((f32[8,16,4096]{2,1,0:T(8,128)}), f32[8,16,4096]{2,1,0:T(8,128)S(1)}, u32[]{:S(2)}, u32[]{:S(2)}) async-start(f32[8,16,4096]{2,1,0:T(8,128)} %reshape.525), calls=%async_computation.2 | async-start | bytes 4194304 | tf_op jit(solution)/shard_map/all_to_all | solution.py:243
  79.2 1.6 copy-start.1
  127.4 47.8 %all-to-all-start.1 = ((f32[8,8,4608]{2,1,0:T(8,128)}), f32[8,8,4608]{2,1,0:T(8,128)}, u32[]{:S(2)}, u32[]{:S(2)}) async-start(f32[8,8,4608]{2,1,0:T(8,128)} %pad_maximum_fusion.6), calls=%async_computation.1 | async-start | bytes 2359296 | tf_op jit(solution)/shard_map/all_to_all | solution.py:268
  137.3 7.7 %collective-permute-start = (f32[5,4,1,512]{3,2,1,0:T(1,128)S(1)}, f32[5,4,1,512]{3,2,1,0:T(1,128)S(1)}, u32[]{:S(2)}, u32[]{:S(2)}) collective-permute-start(f32[5,4,1,512]{3,2,1,0:T(1,128)S(1)} %get-tuple-element.54), channel_id=1, source_target_pairs={{0,4},{4,8},{8,12},{12,16},{16,20},{20,24},{24,28},{28,0},{1,5},{5... | collective-permute-start | bytes 122888 | tf_op jit(solution)/shard_map/ppermute | solution.py:27
  139.7 5.8 %collective-permute-start.1 = (f32[5,4,1,512]{3,2,1,0:T(1,128)S(1)}, f32[5,4,1,512]{3,2,1,0:T(1,128)S(1)}, u32[]{:S(2)}, u32[]{:S(2)}) collective-permute-start(f32[5,4,1,512]{3,2,1,0:T(1,128)S(1)} %get-tuple-element.55), channel_id=1, source_target_pairs={{4,0},{8,4},{12,8},{16,12},{20,16},{24,20},{28,24},{0,28},{5,1},{9... | collective-permute-start | bytes 122888 | tf_op jit(solution)/shard_map/ppermute | solution.py:30
  145.0 4.3 %copy-start.9 = (f32[5,4,1,512]{3,2,1,0:T(1,128)}, f32[5,4,1,512]{3,2,1,0:T(1,128)S(1)}, u32[]{:S(2)}) copy-start(f32[5,4,1,512]{3,2,1,0:T(1,128)S(1)} %collective-permute-done) | copy-start | bytes 122884
  145.4 3.9 %copy-start.11 = (f32[5,4,1,512]{3,2,1,0:T(1,128)}, f32[5,4,1,512]{3,2,1,0:T(1,128)S(1)}, u32[]{:S(2)}) copy-start(f32[5,4,1,512]{3,2,1,0:T(1,128)S(1)} %collective-permute-done.1) | copy-start | bytes 122884
  154.4 5.2 %collective-permute-start.3 = (f32[5,4,130,1]{2,0,3,1:T(8,128)S(1)}, f32[5,4,130,1]{2,0,3,1:T(8,128)S(1)}, u32[]{:S(2)}, u32[]{:S(2)}) collective-permute-start(f32[5,4,130,1]{2,0,3,1:T(8,128)S(1)} %copy.72), channel_id=1, source_target_pairs={{1,0},{2,1},{3,2},{0,3},{5,4},{6,5},{7,6},{4,7},{9,8},{10,9},{11,1... | collective-permute-start | bytes 31208 | tf_op jit(solution)/shard_map/ppermute | solution.py:30
  154.6 3.3 %collective-permute-start.2 = (f32[5,4,130,1]{2,0,3,1:T(8,128)S(1)}, f32[5,4,130,1]{2,0,3,1:T(8,128)S(1)}, u32[]{:S(2)}, u32[]{:S(2)}) collective-permute-start(f32[5,4,130,1]{2,0,3,1:T(8,128)S(1)} %copy.71), channel_id=1, source_target_pairs={{0,1},{1,2},{2,3},{3,0},{4,5},{5,6},{6,7},{7,4},{8,9},{9,10},{10,1... | collective-permute-start | bytes 31208 | tf_op jit(solution)/shard_map/ppermute | solution.py:27
  174.0 8.4 %copy-start.5 = (f32[5,4,130,1]{3,2,1,0:T(8,128)S(1)}, f32[5,4,130,1]{3,2,1,0:T(8,128)}, u32[]{:S(2)}) copy-start(f32[5,4,130,1]{3,2,1,0:T(8,128)} %copy.73) | copy-start | bytes 31204
  174.0 8.4 %copy-start.6 = (f32[5,4,130,1]{3,2,1,0:T(8,128)S(1)}, f32[5,4,130,1]{3,2,1,0:T(8,128)}, u32[]{:S(2)}) copy-start(f32[5,4,130,1]{3,2,1,0:T(8,128)} %copy.74) | copy-start | bytes 31204
  174.0 8.4 %copy-start.10 = (f32[5,4,1,512]{3,2,1,0:T(1,128)S(1)}, f32[5,4,1,512]{3,2,1,0:T(1,128)}, u32[]{:S(2)}) copy-start(f32[5,4,1,512]{3,2,1,0:T(1,128)} %copy-done.9) | copy-start | bytes 122884
  174.0 8.4 %copy-start.12 = (f32[5,4,1,512]{3,2,1,0:T(1,128)S(1)}, f32[5,4,1,512]{3,2,1,0:T(1,128)}, u32[]{:S(2)}) copy-start(f32[5,4,1,512]{3,2,1,0:T(1,128)} %copy-done.11) | copy-start | bytes 122884
  175.2 37.9 %all-to-all-start.3 = ((f32[8,8,4608]{2,1,0:T(8,128)}), f32[8,8,4608]{2,1,0:T(8,128)}, u32[]{:S(2)}, u32[]{:S(2)}) async-start(f32[8,8,4608]{2,1,0:T(8,128)} %pad_maximum_fusion.7), calls=%async_computation.3 | async-start | bytes 2359296 | tf_op jit(solution)/shard_map/all_to_all | solution.py:268
  213.1 4.0 %copy-start.7 = (f32[8,8,1,8,512]{4,3,2,0,1:T(8,128)S(1)}, f32[8,8,1,8,512]{4,3,2,0,1:T(8,128)}, u32[]{:S(2)}) copy-start(f32[8,8,1,8,512]{4,3,2,0,1:T(8,128)} %copy.80) | copy-start | bytes 3145732
  216.0 1.3 copy-start.4

commit v2 on v1

--- a/solution.py
+++ b/solution.py
@@ -237,10 +237,11 @@
     band_start = member * band_rows
     drag_band = lax.dynamic_slice_in_dim(drag_factor, band_start, band_rows, 0)
     drag_band = drag_band.reshape(pieces, 1, piece_cells)
-    sent = []
-    for piece in range(pieces):
-        payload = jnp.moveaxis(flows[:, :, piece], 1, 0).reshape(groups, 4 * local_coefs, piece_cells)
-        sent.append(lax.all_to_all(payload, "freq", split_axis=0, concat_axis=0, tiled=True))
+    payloads = [
+        jnp.moveaxis(flows[:, :, piece], 1, 0).reshape(groups, 4 * local_coefs, piece_cells)
+        for piece in range(pieces)
+    ]
+    sent = [lax.all_to_all(payloads[0], "freq", split_axis=0, concat_axis=0, tiled=True)]
     planes = jnp.stack([height, east, north, water_depth * east, water_depth * north])
     extended = extended_2(planes, (("lat", 2), ("lon", 3)), 1)
     rim_keep = jnp.ones((tile_rows + 2,), jnp.float32)
@@ -257,7 +258,15 @@
     linear_part = linear_residual(
         extended, tile_rows, tile_cols, angular_local[:, None, None], rotation[:, None]
     )
-    frictions, rates = [], []
+    later = lax.optimization_barrier((payloads[1:], linear_part))
+    linear_part = later[1]
+    for payload in later[0]:
+        sent.append(lax.all_to_all(payload, "freq", split_axis=0, concat_axis=0, tiled=True))
+    shape_piece = (groups, pieces, piece_rows, tile_cols)
+    linear_part = linear_part.reshape(3, local_coefs, *shape_piece)
+    wet_piece = wet_cells.reshape(shape_piece)
+    rotation_piece = rotation.reshape(groups, pieces, piece_rows, 1)
+    results = []
     for piece in range(pieces):
         packed, rate = friction_band(sent[piece], drag_band[piece], table, tile_cols)
         rate = jnp.broadcast_to(
@@ -266,17 +275,22 @@
         )
         payload = jnp.concatenate([packed, rate], axis=2)
         back = lax.all_to_all(payload, "freq", split_axis=0, concat_axis=0, tiled=True)
-        frictions.append(
-            back[:, :, :piece_cells].reshape(groups, 2 * local_coefs, piece_rows, tile_cols)
+        friction = back[:, :, :piece_cells].reshape(groups, 2, local_coefs, piece_rows, tile_cols)
+        friction = jnp.moveaxis(friction, 0, 2)
+        drag_rate = back[:, :, piece_cells:].reshape(groups, piece_rows, tile_cols)
+        linear_piece = linear_part[:, :, :, piece]
+        residual = (
+            linear_piece + jnp.concatenate([jnp.zeros_like(friction[:1]), friction], axis=0)
+        ) * wet_piece[:, piece]
+        results.append(
+            precondition(
+                residual,
+                angular_local[:, None, None, None],
+                rotation_piece[:, piece],
+                drag_rate,
+            )
         )
-        rates.append(back[:, :, piece_cells:].reshape(groups, piece_rows, tile_cols))
-    friction = jnp.stack(frictions, axis=2)
-    friction = jnp.moveaxis(friction, 0, 1).reshape(2, local_coefs, tile_rows, tile_cols)
-    drag_rate = jnp.stack(rates, axis=1).reshape(tile_rows, tile_cols)
-    residual = (
-        linear_part + jnp.concatenate([jnp.zeros_like(friction[:1]), friction], axis=0)
-    ) * wet_cells
-    return precondition(residual, angular_local[:, None, None], rotation[:, None], drag_rate)
+    return jnp.stack(results, axis=3).reshape(3, local_coefs, tile_rows, tile_cols)
 
 
 def solution(mesh):

time: 224 us -> 206 us (0.920)
  waiting for transfers between devices: 99.3 us -> 84 us
  local copies, waits for them, and re-layouts: 32.6 us -> 27.4 us
  other arithmetic: 34 us -> 37.1 us
    all_to_all x4 -> x3, waiting for transfers between devices: 94.1 us -> 77 us  [local(): lax.all_to_all(payload, 'freq', split_axis=0, concat_axis=0, tiled=True)]
    all_to_all x4 -> x3, starting transfers between devices: 23.5 us -> 11.7 us  [local(): lax.all_to_all(payload, 'freq', split_axis=0, concat_axis=0, tiled=True)]
    all_to_all x0 -> x1, starting transfers between devices: none -> 8.47 us  [local(): lax.all_to_all(payloads[0], 'freq', split_axis=0, concat_axis=0, tiled=True)]
    all_to_all x0 -> x1, waiting for transfers between devices: none -> 4.53 us  [local(): lax.all_to_all(payloads[0], 'freq', split_axis=0, concat_axis=0, tiled=True)]
    ppermute x2, waiting for transfers between devices: 4.83 us -> 1.98 us  [extended_2(): lax.ppermute(lax.slice_in_dim(block, block.shape[dim] - width, None, axis...]
    slice x2, local copies, waits for them, and re-layouts: 2.68 us -> 0.14 us  [local(): back[:, :, :piece_cells]]
    unnamed x33 -> x37, local copies, waits for them, and re-layouts: 7.79 us -> 7.61 us
  transfers between devices with their start and end apart: 8 -> 8, of which waited for: 6 -> 6; matrix products, arithmetic and copies ran while one was open for 19% -> 22% of each run, Pallas kernels for 12% -> 13%
where the time goes in v2:
time: 206 us; the launch traced here: 203 us
  waiting for transfers between devices  84 us (41%)
  other arithmetic  37.1 us (18%)
  starting transfers between devices  27.9 us (14%)
  local copies, waits for them, and re-layouts  27.4 us (13%)
  Pallas kernels  26.4 us (13%)
    all_to_all x3, waiting for transfers between devices, local(): lax.all_to_all(payload, 'freq', split_axis=0, concat_axis=0, tiled=True)  77 us
    pallas_call x2, Pallas kernels, friction_band(): pl.pallas_call(functools.partial(friction_kernel, groups), grid=(steps,),...  26.4 us
    all_to_all x3, starting transfers between devices, local(): lax.all_to_all(payload, 'freq', split_axis=0, concat_axis=0, tiled=True)  11.7 us
    unnamed x9, other arithmetic  9.73 us
    all_to_all x1, starting transfers between devices, local(): lax.all_to_all(payloads[0], 'freq', split_axis=0, concat_axis=0, tiled=True)  8.47 us
    unnamed x37, local copies, waits for them, and re-layouts  7.61 us
    mul x1, other arithmetic, local(): extended = extended * rim_keep[:, None]  6.24 us
    ppermute x2, starting transfers between devices, extended_2(): lax.ppermute(lax.slice_in_dim(block, 0, width, axis=dim), axis, backward)  5.3 us
  transfers between devices with their start and end apart: 8, of which 6 were waited for; matrix products, arithmetic and copies ran while one was open for 22% of the time, Pallas kernels for 13%

profile of v2, /device:TPU:8, one launch (start us, length us, event | category | flops | bytes accessed | tf_op | source)
XLA Modules:
  0.0 203.3 jit_solution(1782849295987372209)
XLA Ops:
  0.0 1.0 convert_element_type.54
  1.0 2.4 %multiply_dynamic-update-slice_fusion.2 = f32[5,4,128,512]{3,2,1,0:T(8,128)} fusion(f32[3,4,128,512]{3,2,1,0:T(8,128)} %param.9, f32[128,512]{1,0:T(8,128)S(1)} %convert_element_type.54), kind=kLoop, calls=%fused_computation.46 | loop fusion | flops 262143 | bytes 2359296
  3.3 2.5 %constant_dynamic-update-slice_fusion.1 = (f32[5,4,128,512]{3,2,1,0:T(8,128)}, f32[1,4,128,512]{3,2,1,0:T(8,128)S(1)}) fusion(f32[5,4,128,512]{3,2,1,0:T(8,128)} %multiply_dynamic-update-slice_fusion.2, f32[128,512]{1,0:T(8,128)S(1)} %convert_element_type.54, f32[3,4,128,512]{3,2,1,0:T(8,128)} %param.9), kind=kLoop, calls=%fused_computation.132 | loop fusion | flops 262144 | bytes 3407872
  5.9 2.6 %constant_dynamic-update-slice_fusion = (f32[5,4,128,512]{3,2,1,0:T(8,128)}, f32[1,4,128,512]{3,2,1,0:T(8,128)S(1)}) fusion(f32[5,4,128,512]{3,2,1,0:T(8,128)} %get-tuple-element.55, f32[128,512]{1,0:T(8,128)S(1)} %convert_element_type.54, f32[3,4,128,512]{3,2,1,0:T(8,128)} %param.9), kind=kLoop, calls=%fused_computation.131 | loop fusion | flops 262144 | bytes 3407872
  8.5 0.6 pad_maximum_fusion
  9.1 0.6 copy-done.1
  9.7 1.8 fusion.51
  11.7 1.5 reshape.871
  13.2 8.5 %all-to-all-start = ((f32[8,16,4096]{2,1,0:T(8,128)}), f32[8,16,4096]{2,1,0:T(8,128)S(1)}, u32[]{:S(2)}, u32[]{:S(2)}) async-start(f32[8,16,4096]{2,1,0:T(8,128)} %reshape.871), calls=%async_computation | async-start | bytes 4194304 | tf_op jit(solution)/shard_map/all_to_all | solution.py:244
  21.7 2.2 %multiply_dynamic-update-slice_fusion.1 = f32[5,4,128,512]{3,2,1,0:T(8,128)} fusion(f32[5,4,128,512]{3,2,1,0:T(8,128)} %get-tuple-element.53, f32[1,4,128,512]{3,2,1,0:T(8,128)S(1)} %get-tuple-element.56, f32[128,512]{1,0:T(8,128)} %param.11), kind=kLoop, calls=%fused_computation.45 | loop fusion | flops 262144 | bytes 2359296
  23.9 1.1 multiply_dynamic-update-slice_fusion
  25.0 1.1 fusion.50
  26.2 2.4 %collective-permute-start = (f32[5,4,1,512]{3,2,1,0:T(1,128)S(1)}, f32[5,4,1,512]{3,2,1,0:T(1,128)S(1)}, u32[]{:S(2)}, u32[]{:S(2)}) collective-permute-start(f32[5,4,1,512]{3,2,1,0:T(1,128)S(1)} %get-tuple-element.64), channel_id=1, source_target_pairs={{0,4},{4,8},{8,12},{12,16},{16,20},{20,24},{24,28},{28,0},{1,5},{5... | collective-permute-start | bytes 122888 | tf_op jit(solution)/shard_map/ppermute | solution.py:27
  28.6 3.3 %collective-permute-start.1 = (f32[5,4,1,512]{3,2,1,0:T(1,128)S(1)}, f32[5,4,1,512]{3,2,1,0:T(1,128)S(1)}, u32[]{:S(2)}, u32[]{:S(2)}) collective-permute-start(f32[5,4,1,512]{3,2,1,0:T(1,128)S(1)} %get-tuple-element.65), channel_id=1, source_target_pairs={{4,0},{8,4},{12,8},{16,12},{20,16},{24,20},{28,24},{0,28},{5,1},{9... | collective-permute-start | bytes 122888 | tf_op jit(solution)/shard_map/ppermute | solution.py:30
  31.9 2.0 collective-permute-done
  34.3 3.9 %pad_maximum_fusion.7 = (f32[5,4,130,1]{3,2,1,0:T(8,128)}, f32[5,4,130,1]{3,2,1,0:T(8,128)}) fusion(f32[5,4,1,512]{3,2,1,0:T(1,128)S(1)} %collective-permute-done.1, f32[5,4,128,512]{3,2,1,0:T(8,128)} %multiply_dynamic-update-slice_fusion, f32[5,4,1,512]{3,2,1,0:T(1,128)S(1)} %collective-permute-done), kind=kLoop, calls=%fused_computation.16 | loop fusion | flops 10400 | bytes 5345600 | tf_op jit(solution)/shard_map/slice | solution.py:28
  38.2 2.5 %copy.129 = f32[5,4,130,1]{2,0,3,1:T(8,128)S(1)} copy(f32[5,4,130,1]{3,2,1,0:T(8,128)} %get-tuple-element.62) | data formatting | bytes 20800 | tf_op jit(solution)/shard_map/slice | solution.py:28
  40.8 2.6 %copy.130 = f32[5,4,130,1]{2,0,3,1:T(8,128)S(1)} copy(f32[5,4,130,1]{3,2,1,0:T(8,128)} %get-tuple-element.63) | data formatting | bytes 20800 | tf_op jit(solution)/shard_map/slice | solution.py:30
  43.4 2.0 collective-permute-start.3
  45.3 3.1 %copy.184 = f32[16,8,1,8,512]{4,3,0,1,2:T(8,128)} copy(f32[16,8,1,8,512]{4,3,2,1,0:T(8,128)} %get-tuple-element.67) | data formatting | bytes 4194304
  48.5 2.8 %reshape.864 = f32[8,16,4096]{2,1,0:T(8,128)} reshape(f32[8,16,8,512]{3,2,1,0:T(8,128)} %bitcast.311) | data formatting | bytes 4194304 | tf_op jit(solution)/shard_map/reshape | solution.py:241
  51.3 1.6 copy.131
  52.9 1.6 copy.132
  54.5 6.2 %maximum_multiply_fusion = f32[5,4,130,514]{3,2,1,0:T(8,128)S(1)} fusion(f32[5,4,130,1]{3,2,1,0:T(8,128)} %copy.132, f32[5,4,1,512]{3,2,1,0:T(1,128)S(1)} %collective-permute-done.1, f32[5,4,128,512]{3,2,1,0:T(8,128)} %multiply_dynamic-update-slice_fusion, f32[5,4,1,512]{3,2,1,0:T(1,128)S(1)} %collective-permute-done, f32[5,4,130,1]{3,2,1,0:T(8,128)} %copy.131, ...), kind=kLoop, calls=%fused_computation | loop fusion | flops 6682000 | bytes 10691720 | tf_op jit(solution)/shard_map/mul | solution.py:250
  61.4 1.8 slice_subtract_fusion.2
  63.7 2.7 %fusion.7 = (f32[1,4,128,512]{3,2,1,0:T(8,128)S(1)}, f32[1,4,128,512]{3,2,1,0:T(8,128)S(1)}) fusion(f32[5,4,130,514]{3,2,1,0:T(8,128)S(1)} %maximum_multiply_fusion, f32[128]{0:T(128)S(1)} %add_multiply_fusion, f32[1,4,128,512]{3,2,1,0:T(8,128)S(1)} %bitcast.322, f32[1,4,128,512]{3,2,1,0:T(8,128)S(1)} %bitcast.323), kind=kLoop, calls=%fused_computation.27 | loop fusion | flops 4718592 | bytes 15729152 | tf_op jit(solution)/shard_map/add | solution.py:77
  66.4 2.0 pad_maximum_fusion.1
  68.4 4.5 %all-to-all-done.flows_ref = f32[8,16,4096]{2,1,0:T(8,128)S(1)} async-done(((f32[8,16,4096]{2,1,0:T(8,128)}), f32[8,16,4096]{2,1,0:T(8,128)S(1)}, u32[]{:S(2)}, u32[]{:S(2)}) %all-to-all-start) | async-done | bytes 2097184 | tf_op jit(solution)/shard_map/all_to_all | solution.py:244
  72.9 4.4 %all-to-all-start.2 = ((f32[8,16,4096]{2,1,0:T(8,128)}), f32[8,16,4096]{2,1,0:T(8,128)}, u32[]{:S(2)}, u32[]{:S(2)}) async-start(f32[8,16,4096]{2,1,0:T(8,128)} %reshape.864), calls=%async_computation.2 | async-start | bytes 4194304 | tf_op jit(solution)/shard_map/all_to_all | solution.py:264
  77.7 0.7 dynamic-slice_bitcast_fusion.1
  78.5 12.8 %shard_map.55 = (f32[8,8,4096]{2,1,0:T(8,128)S(1)}, f32[8,1,512]{2,1,0:T(1,128)S(1)}) custom-call(bf16[256,192]{1,0:T(8,128)(2,1)S(1)} %copy.135.stacked_ref, f32[32,256]{1,0:T(8,128)S(1)} %bitcast.304, f32[8,16,4096]{2,1,0:T(8,128)S(1)} %all-to-all-done.flows_ref, f32[1,4096]{1,0:T(1,128)S(1)} %bitcast.307), custom_call_target="tpu_custom_call" | custom-call | tf_op jit(solution)/shard_map/pallas_call | solution.py:193
  91.3 1.1 pad_maximum_fusion.8
  92.4 34.1 %all-to-all-done.2.flows_ref = f32[8,16,4096]{2,1,0:T(8,128)} async-done(((f32[8,16,4096]{2,1,0:T(8,128)}), f32[8,16,4096]{2,1,0:T(8,128)}, u32[]{:S(2)}, u32[]{:S(2)}) %all-to-all-start.2) | async-done | bytes 2097184 | tf_op jit(solution)/shard_map/all_to_all | solution.py:264
  126.5 3.8 %all-to-all-start.1 = ((f32[8,8,4608]{2,1,0:T(8,128)}), f32[8,8,4608]{2,1,0:T(8,128)S(1)}, u32[]{:S(2)}, u32[]{:S(2)}) async-start(f32[8,8,4608]{2,1,0:T(8,128)} %pad_maximum_fusion.8), calls=%async_computation.1 | async-start | bytes 2359296 | tf_op jit(solution)/shard_map/all_to_all | solution.py:277
  130.4 13.6 %shard_map.56 = (f32[8,8,4096]{2,1,0:T(8,128)S(1)}, f32[8,1,512]{2,1,0:T(1,128)S(1)}) custom-call(bf16[256,192]{1,0:T(8,128)(2,1)S(1)} %copy.135.stacked_ref, f32[32,256]{1,0:T(8,128)S(1)} %bitcast.305, f32[8,16,4096]{2,1,0:T(8,128)} %all-to-all-done.2.flows_ref, f32[1,4096]{1,0:T(1,128)S(1)} %bitcast.306), custom_call_target="tpu_custom_call" | custom-call | tf_op jit(solution)/shard_map/pallas_call | solution.py:193
  144.0 1.1 pad_maximum_fusion.9
  145.2 16.9 %all-to-all-done.1 = f32[8,8,4608]{2,1,0:T(8,128)S(1)} async-done(((f32[8,8,4608]{2,1,0:T(8,128)}), f32[8,8,4608]{2,1,0:T(8,128)S(1)}, u32[]{:S(2)}, u32[]{:S(2)}) %all-to-all-start.1) | async-done | bytes 1179680 | tf_op jit(solution)/shard_map/all_to_all | solution.py:277
  162.1 3.6 %all-to-all-start.3 = ((f32[8,8,4608]{2,1,0:T(8,128)}), f32[8,8,4608]{2,1,0:T(8,128)S(1)}, u32[]{:S(2)}, u32[]{:S(2)}) async-start(f32[8,8,4608]{2,1,0:T(8,128)} %pad_maximum_fusion.9), calls=%async_computation.3 | async-start | bytes 2359296 | tf_op jit(solution)/shard_map/all_to_all | solution.py:277
  166.2 0.6 slice_bitcast_fusion.17
  166.8 0.6 fusion.44
  167.4 0.7 slice_bitcast_fusion.15
  168.2 0.6 copy.175
  168.9 0.8 slice_add_fusion.9
  169.6 26.0 %all-to-all-done.3 = f32[8,8,4608]{2,1,0:T(8,128)S(1)} async-done(((f32[8,8,4608]{2,1,0:T(8,128)}), f32[8,8,4608]{2,1,0:T(8,128)S(1)}, u32[]{:S(2)}, u32[]{:S(2)}) %all-to-all-start.3) | async-done | bytes 1179680 | tf_op jit(solution)/shard_map/all_to_all | solution.py:277
  195.7 0.6 copy.177
  196.4 1.2 copy-done
  197.6 0.7 fusion.3
  201.4 2.0 copy.155
  (77 shorter events, 6.2 us)
Async XLA Ops:
  5.8 2.6 %copy-start.3 = (f32[2,4,128,512]{3,2,1,0:T(8,128)S(1)}, f32[2,4,128,512]{3,2,1,0:T(8,128)}, u32[]{:S(2)}) copy-start(f32[2,4,128,512]{3,2,1,0:T(8,128)} %param.10) | copy-start | bytes 6291460
  8.5 1.2 copy-start.1
  13.2 59.7 %all-to-all-start = ((f32[8,16,4096]{2,1,0:T(8,128)}), f32[8,16,4096]{2,1,0:T(8,128)S(1)}, u32[]{:S(2)}, u32[]{:S(2)}) async-start(f32[8,16,4096]{2,1,0:T(8,128)} %reshape.871), calls=%async_computation | async-start | bytes 4194304 | tf_op jit(solution)/shard_map/all_to_all | solution.py:244
  21.7 2.2 %copy-start.2 = (f32[1,4,128,512]{3,2,1,0:T(8,128)S(1)}, f32[1,4,128,512]{3,2,1,0:T(8,128)}, u32[]{:S(2)}) copy-start(f32[1,4,128,512]{3,2,1,0:T(8,128)} %copy-done.1) | copy-start | bytes 3145732
  21.7 2.2 %copy-start.5 = (f32[128,512]{1,0:T(8,128)S(1)}, f32[128,512]{1,0:T(8,128)}, u32[]{:S(2)}) copy-start(f32[128,512]{1,0:T(8,128)} %param.11) | copy-start | bytes 786436
  26.2 7.7 %collective-permute-start = (f32[5,4,1,512]{3,2,1,0:T(1,128)S(1)}, f32[5,4,1,512]{3,2,1,0:T(1,128)S(1)}, u32[]{:S(2)}, u32[]{:S(2)}) collective-permute-start(f32[5,4,1,512]{3,2,1,0:T(1,128)S(1)} %get-tuple-element.64), channel_id=1, source_target_pairs={{0,4},{4,8},{8,12},{12,16},{16,20},{20,24},{24,28},{28,0},{1,5},{5... | collective-permute-start | bytes 122888 | tf_op jit(solution)/shard_map/ppermute | solution.py:27
  28.6 5.8 %collective-permute-start.1 = (f32[5,4,1,512]{3,2,1,0:T(1,128)S(1)}, f32[5,4,1,512]{3,2,1,0:T(1,128)S(1)}, u32[]{:S(2)}, u32[]{:S(2)}) collective-permute-start(f32[5,4,1,512]{3,2,1,0:T(1,128)S(1)} %get-tuple-element.65), channel_id=1, source_target_pairs={{4,0},{8,4},{12,8},{16,12},{20,16},{24,20},{28,24},{0,28},{5,1},{9... | collective-permute-start | bytes 122888 | tf_op jit(solution)/shard_map/ppermute | solution.py:30
  31.9 31.2 %copy-start.11 = (f32[2]{0:T(128)}, f32[2]{0:T(128)S(1)}, u32[]{:S(2)}) copy-start(f32[2]{0:T(128)S(1)} %convert_multiply_fusion) | copy-start | bytes 28
  40.7 10.5 %collective-permute-start.2 = (f32[5,4,130,1]{2,0,3,1:T(8,128)S(1)}, f32[5,4,130,1]{2,0,3,1:T(8,128)S(1)}, u32[]{:S(2)}, u32[]{:S(2)}) collective-permute-start(f32[5,4,130,1]{2,0,3,1:T(8,128)S(1)} %copy.129), channel_id=1, source_target_pairs={{0,1},{1,2},{2,3},{3,0},{4,5},{5,6},{6,7},{7,4},{8,9},{9,10},{10,1... | collective-permute-start | bytes 31208 | tf_op jit(solution)/shard_map/ppermute | solution.py:27
  43.4 9.5 %collective-permute-start.3 = (f32[5,4,130,1]{2,0,3,1:T(8,128)S(1)}, f32[5,4,130,1]{2,0,3,1:T(8,128)S(1)}, u32[]{:S(2)}, u32[]{:S(2)}) collective-permute-start(f32[5,4,130,1]{2,0,3,1:T(8,128)S(1)} %copy.130), channel_id=1, source_target_pairs={{1,0},{2,1},{3,2},{0,3},{5,4},{6,5},{7,6},{4,7},{9,8},{10,9},{11,1... | collective-permute-start | bytes 31208 | tf_op jit(solution)/shard_map/ppermute | solution.py:30
  72.9 53.6 %all-to-all-start.2 = ((f32[8,16,4096]{2,1,0:T(8,128)}), f32[8,16,4096]{2,1,0:T(8,128)}, u32[]{:S(2)}, u32[]{:S(2)}) async-start(f32[8,16,4096]{2,1,0:T(8,128)} %reshape.864), calls=%async_computation.2 | async-start | bytes 4194304 | tf_op jit(solution)/shard_map/all_to_all | solution.py:264
  126.5 35.5 %all-to-all-start.1 = ((f32[8,8,4608]{2,1,0:T(8,128)}), f32[8,8,4608]{2,1,0:T(8,128)S(1)}, u32[]{:S(2)}, u32[]{:S(2)}) async-start(f32[8,8,4608]{2,1,0:T(8,128)} %pad_maximum_fusion.8), calls=%async_computation.1 | async-start | bytes 2359296 | tf_op jit(solution)/shard_map/all_to_all | solution.py:277
  162.1 33.6 %all-to-all-start.3 = ((f32[8,8,4608]{2,1,0:T(8,128)}), f32[8,8,4608]{2,1,0:T(8,128)S(1)}, u32[]{:S(2)}, u32[]{:S(2)}) async-start(f32[8,8,4608]{2,1,0:T(8,128)} %pad_maximum_fusion.9), calls=%async_computation.3 | async-start | bytes 2359296 | tf_op jit(solution)/shard_map/all_to_all | solution.py:277
  195.7 1.9 copy-start
  195.7 1.9 copy-start.6
  195.7 1.9 copy-start.7
  197.6 0.8 copy-start.9
  197.6 0.8 copy-start.10
  197.6 0.8 copy-start.12
  197.6 0.8 copy-start.13
  198.4 0.9 copy-start.4
  198.4 1.0 copy-start.8

commit v3 on v2

--- a/solution.py
+++ b/solution.py
@@ -213,6 +213,179 @@
         ],
         compiler_params=pltpu.CompilerParams(vmem_limit_bytes=48 * 1024 * 1024),
     )(stacked, table_t, flows_band, drag_band)
+
+
+MESH = pl.DeviceIdType.MESH
+
+
+def friction_block(groups, stacked, table_t, flows_ref, drag_row, offset, width, gather_ref, parts_ref):
+    coefs = gather_ref.shape[0]
+    per = coefs // groups
+    cells = pl.ds(offset, width)
+
+    def synth(field):
+        for source in range(groups):
+            gather_ref[source * per : (source + 1) * per, :] = flows_ref[
+                source, field * per : (field + 1) * per, cells
+            ]
+        high, middle, low = split_three(gather_ref[...])
+        for slot, part in enumerate((high, middle, high, low, high, middle)):
+            parts_ref[slot * coefs : (slot + 1) * coefs, :] = part
+        return jnp.dot(stacked, parts_ref[...], preferred_element_type=jnp.float32)
+
+    highest = lax.Precision.HIGHEST
+    base_east, base_north, step_east, step_north = synth(0), synth(1), synth(2), synth(3)
+    magnitude = jnp.sqrt(base_east * base_east + base_north * base_north + SPEED_SOFT)
+    projected = (base_east * step_east + base_north * step_north) / magnitude
+    force_east = drag_row * (magnitude * step_east + base_east * projected)
+    force_north = drag_row * (magnitude * step_north + base_north * projected)
+    scale = 2.0 / stacked.shape[0]
+    analysed_east = (
+        jnp.dot(table_t, force_east, precision=highest, preferred_element_type=jnp.float32) * scale
+    )
+    analysed_north = (
+        jnp.dot(table_t, force_north, precision=highest, preferred_element_type=jnp.float32)
+        * scale
+    )
+    drag_rate = drag_row * jnp.mean(magnitude, axis=0, keepdims=True)
+    return analysed_east, analysed_north, drag_rate
+
+
+def exchange_kernel(
+    groups,
+    width,
+    stacked_ref,
+    table_t_ref,
+    first_ref,
+    second_ref,
+    drag_ref,
+    back_first_ref,
+    back_second_ref,
+    arrived,
+    results,
+    landed,
+    gather_ref,
+    parts_ref,
+    send_sems,
+    recv_sems,
+    local_sems,
+):
+    me = lax.axis_index("freq")
+    lat = lax.axis_index("lat")
+    lon = lax.axis_index("lon")
+    cells = first_ref.shape[2]
+    coefs = gather_ref.shape[0]
+    per = coefs // groups
+    blocks = cells // width
+
+    barrier = pltpu.get_barrier_semaphore()
+    for distance in range(1, groups):
+        peer = lax.rem(me + distance, groups)
+        pl.semaphore_signal(barrier, inc=1, device_id=(peer, lat, lon), device_id_type=MESH)
+    pl.semaphore_wait(barrier, groups - 1)
+
+    def exchange(phase, source_of, target_of):
+        copies = []
+        for distance in range(1, groups):
+            peer = lax.rem(me + distance, groups)
+            copy = pltpu.make_async_remote_copy(
+                src_ref=source_of(peer),
+                dst_ref=target_of(me),
+                send_sem=send_sems.at[phase, distance],
+                recv_sem=recv_sems.at[phase, distance],
+                device_id=(peer, lat, lon),
+                device_id_type=MESH,
+            )
+            copy.start()
+            copies.append(copy)
+        local = pltpu.make_async_copy(source_of(me), target_of(me), local_sems.at[phase])
+        local.start()
+        return copies, local
+
+    def wait_arrivals(phase, source_of, target_of):
+        for distance in range(1, groups):
+            sender = lax.rem(me + groups - distance, groups)
+            pltpu.make_async_remote_copy(
+                src_ref=source_of(sender),
+                dst_ref=target_of(sender),
+                send_sem=send_sems.at[phase, distance],
+                recv_sem=recv_sems.at[phase, distance],
+                device_id=(sender, lat, lon),
+                device_id_type=MESH,
+            ).wait_recv()
+
+    sending = [exchange(0, lambda g: second_ref.at[g], lambda g: arrived.at[g])]
+    stacked = stacked_ref[...]
+    table_t = table_t_ref[...]
+
+    def compute(piece, flows_ref):
+        def block(index, carry):
+            offset = pl.multiple_of(index * width, width)
+            drag_row = drag_ref[piece, :, pl.ds(offset, width)]
+            east, north, rate = friction_block(
+                groups, stacked, table_t, flows_ref, drag_row, offset, width, gather_ref, parts_ref
+            )
+            for group in range(groups):
+                results[piece, group, 0:per, pl.ds(offset, width)] = east[
+                    group * per : (group + 1) * per
+                ]
+                results[piece, group, per : 2 * per, pl.ds(offset, width)] = north[
+                    group * per : (group + 1) * per
+                ]
+                results[piece, group, pl.ds(index, 1), pl.ds(cells, width)] = rate
+            return carry
+
+        lax.fori_loop(0, blocks, block, 0)
+
+    compute(0, first_ref)
+    sending.append(exchange(1, lambda g: results.at[0, g], lambda g: landed.at[0, g]))
+    wait_arrivals(0, lambda g: second_ref.at[g], lambda g: arrived.at[g])
+    sending[0][1].wait()
+    compute(1, arrived)
+    sending.append(exchange(2, lambda g: results.at[1, g], lambda g: landed.at[1, g]))
+    for copies, local in sending:
+        for copy in copies:
+            copy.wait_send()
+    sending[1][1].wait()
+    sending[2][1].wait()
+    wait_arrivals(1, lambda g: results.at[0, g], lambda g: landed.at[0, g])
+    wait_arrivals(2, lambda g: results.at[1, g], lambda g: landed.at[1, g])
+    back_first_ref[...] = landed[0]
+    back_second_ref[...] = landed[1]
+
+
+def exchange_friction(first, second, drag_band, table, width):
+    groups, rows_in, cells = first.shape
+    coefs = table.shape[1]
+    per = coefs // groups
+    table_t = jnp.transpose(table)
+    high = lax.reduce_precision(table, exponent_bits=8, mantissa_bits=7)
+    rest = table - high
+    middle = lax.reduce_precision(rest, exponent_bits=8, mantissa_bits=7)
+    low = lax.reduce_precision(rest - middle, exponent_bits=8, mantissa_bits=7)
+    stacked = jnp.concatenate([high, middle, middle, high, low, high], axis=1)
+    stacked = stacked.astype(jnp.bfloat16)
+    returned = (groups, 2 * per, cells + cells // (2 * per))
+    vmem = pl.BlockSpec(memory_space=pltpu.VMEM)
+    return pl.pallas_call(
+        functools.partial(exchange_kernel, groups, width),
+        in_specs=[vmem] * 5,
+        out_specs=[vmem, vmem],
+        out_shape=[jax.ShapeDtypeStruct(returned, jnp.float32)] * 2,
+        scratch_shapes=[
+            pltpu.VMEM(first.shape, jnp.float32),
+            pltpu.VMEM((2,) + returned, jnp.float32),
+            pltpu.VMEM((2,) + returned, jnp.float32),
+            pltpu.VMEM((coefs, width), jnp.float32),
+            pltpu.VMEM((6 * coefs, width), jnp.bfloat16),
+            pltpu.SemaphoreType.DMA((3, groups)),
+            pltpu.SemaphoreType.DMA((3, groups)),
+            pltpu.SemaphoreType.DMA((3,)),
+        ],
+        compiler_params=pltpu.CompilerParams(
+            collective_id=0, has_side_effects=True, vmem_limit_bytes=60 * 1024 * 1024
+        ),
+    )(stacked, table_t, first, second, drag_band)
 
 
 def local(direction, base_flow, water_depth, drag_factor, wet_mask, pieces=2):
@@ -258,23 +431,16 @@
     linear_part = linear_residual(
         extended, tile_rows, tile_cols, angular_local[:, None, None], rotation[:, None]
     )
-    later = lax.optimization_barrier((payloads[1:], linear_part))
+    later = lax.optimization_barrier((payloads[1], linear_part))
     linear_part = later[1]
-    for payload in later[0]:
-        sent.append(lax.all_to_all(payload, "freq", split_axis=0, concat_axis=0, tiled=True))
     shape_piece = (groups, pieces, piece_rows, tile_cols)
     linear_part = linear_part.reshape(3, local_coefs, *shape_piece)
     wet_piece = wet_cells.reshape(shape_piece)
     rotation_piece = rotation.reshape(groups, pieces, piece_rows, 1)
+    backs = exchange_friction(sent[0], later[0], drag_band, table, tile_cols)
     results = []
     for piece in range(pieces):
-        packed, rate = friction_band(sent[piece], drag_band[piece], table, tile_cols)
-        rate = jnp.broadcast_to(
-            rate.reshape(1, 1, piece_cells).reshape(1, 2 * local_coefs, piece_cells // (2 * local_coefs)),
-            (groups, 2 * local_coefs, piece_cells // (2 * local_coefs)),
-        )
-        payload = jnp.concatenate([packed, rate], axis=2)
-        back = lax.all_to_all(payload, "freq", split_axis=0, concat_axis=0, tiled=True)
+        back = backs[piece]
         friction = back[:, :, :piece_cells].reshape(groups, 2, local_coefs, piece_rows, tile_cols)
         friction = jnp.moveaxis(friction, 0, 2)
         drag_rate = back[:, :, piece_cells:].reshape(groups, piece_rows, tile_cols)

time: 206 us -> 191 us (0.927); the launches traced: 203 us -> 191 us
  Pallas kernels: 26.4 us -> 104 us
  waiting for transfers between devices: 84 us -> 23 us
  other arithmetic: 37.1 us -> 25.1 us
  starting transfers between devices: 27.9 us -> 16 us
  local copies, waits for them, and re-layouts: 27.4 us -> 21.9 us
    pallas_call x2 -> x1, Pallas kernels: 26.4 us -> 104 us  [exchange_friction(): pl.pallas_call(functools.partial(exchange_kernel, groups, width), in_spec...]
    all_to_all x3 -> x0, waiting for transfers between devices: 77 us -> none  [local(): lax.all_to_all(payload, 'freq', split_axis=0, concat_axis=0, tiled=True)]
    all_to_all x1, waiting for transfers between devices: 4.53 us -> 23 us  [local(): lax.all_to_all(payloads[0], 'freq', split_axis=0, concat_axis=0, tiled=True)]
    all_to_all x3 -> x0, starting transfers between devices: 11.7 us -> none  [local(): lax.all_to_all(payload, 'freq', split_axis=0, concat_axis=0, tiled=True)]
    unnamed x9, other arithmetic: 9.73 us -> 4.33 us
    slice x2, local copies, waits for them, and re-layouts: 3.69 us -> 1.27 us  [extended_2(): lax.slice_in_dim(block, block.shape[dim] - width, None, axis=dim)]
    concatenate x3 -> x1, other arithmetic: 2.23 us -> 0.01 us  [exchange_friction(): stacked = jnp.concatenate([high, middle, middle, high, low, high], axis=1)]
    unnamed x37 -> x36, local copies, waits for them, and re-layouts: 7.61 us -> 5.84 us
  transfers between devices with their start and end apart: 8 -> 5, of which waited for: 6 -> 1; matrix products, arithmetic and copies ran while one was open for 22% -> 16% of each run, Pallas kernels for 13% -> 0%
where the time goes in v3:
time: 191 us
  Pallas kernels  104 us (54%)
  other arithmetic  25.1 us (13%)
  waiting for transfers between devices  23 us (12%)
  local copies, waits for them, and re-layouts  21.9 us (11%)
  starting transfers between devices  16 us (8%)
    pallas_call x1, Pallas kernels, exchange_friction(): pl.pallas_call(functools.partial(exchange_kernel, groups, width), in_spec...  104 us
    all_to_all x1, waiting for transfers between devices, local(): lax.all_to_all(payloads[0], 'freq', split_axis=0, concat_axis=0, tiled=True)  23 us
    all_to_all x1, starting transfers between devices, local(): lax.all_to_all(payloads[0], 'freq', split_axis=0, concat_axis=0, tiled=True)  8.47 us
    mul x1, other arithmetic, local(): extended = extended * rim_keep[:, None]  5.92 us
    unnamed x36, local copies, waits for them, and re-layouts  5.84 us
    ppermute x2, starting transfers between devices, extended_2(): lax.ppermute(lax.slice_in_dim(block, 0, width, axis=dim), axis, backward)  5.12 us
    unnamed x9, other arithmetic  4.33 us
  transfers between devices with their start and end apart: 5, of which 1 were waited for; matrix products, arithmetic and copies ran while one was open for 16% of the time, Pallas kernels for 0%

profile of v3, /device:TPU:8, one launch (start us, length us, event | category | flops | bytes accessed | tf_op | source)
XLA Modules:
  0.0 190.6 jit_solution(1686025371461099279)
XLA Ops:
  0.0 1.0 convert_element_type.53
  1.0 1.3 multiply_dynamic-update-slice_fusion.2
  2.4 1.4 constant_dynamic-update-slice_fusion.1
  3.8 1.4 constant_dynamic-update-slice_fusion
  5.5 2.3 %copy-done.2 = f32[5,4,128,512]{3,2,1,0:T(8,128)} copy-done((f32[5,4,128,512]{3,2,1,0:T(8,128)}, f32[5,4,128,512]{3,2,1,0:T(8,128)S(1)}, u32[]{:S(2)}) %copy-start.2) | copy-done | bytes 5242904
  7.9 2.4 %collective-permute-start = (f32[5,4,1,512]{3,2,1,0:T(1,128)S(1)}, f32[5,4,1,512]{3,2,1,0:T(1,128)S(1)}, u32[]{:S(2)}, u32[]{:S(2)}) collective-permute-start(f32[5,4,1,512]{3,2,1,0:T(1,128)S(1)} %get-tuple-element.60), channel_id=1, source_target_pairs={{0,4},{4,8},{8,12},{12,16},{16,20},{20,24},{24,28},{28,0},{1,5},{5... | collective-permute-start | bytes 122888 | tf_op jit(solution)/shard_map/ppermute | solution.py:27
  10.3 3.3 %collective-permute-start.1 = (f32[5,4,1,512]{3,2,1,0:T(1,128)S(1)}, f32[5,4,1,512]{3,2,1,0:T(1,128)}, u32[]{:S(2)}, u32[]{:S(2)}) collective-permute-start(f32[5,4,1,512]{3,2,1,0:T(1,128)S(1)} %get-tuple-element.61), channel_id=1, source_target_pairs={{4,0},{8,4},{12,8},{16,12},{20,16},{24,20},{28,24},{0,28},{5,1},{9... | collective-permute-start | bytes 122888 | tf_op jit(solution)/shard_map/ppermute | solution.py:30
  13.6 0.6 pad_maximum_fusion
  14.2 1.8 fusion.51
  16.0 0.2 copy.172
  16.2 1.6 reshape.867
  17.8 8.5 %all-to-all-start = ((f32[8,16,4096]{2,1,0:T(8,128)}), f32[8,16,4096]{2,1,0:T(8,128)}, u32[]{:S(2)}, u32[]{:S(2)}) async-start(f32[8,16,4096]{2,1,0:T(8,128)} %reshape.867), calls=%async_computation | async-start | bytes 4194304 | tf_op jit(solution)/shard_map/all_to_all | solution.py:417
  26.3 0.6 fusion.44
  26.9 0.6 slice_bitcast_fusion.17
  27.8 0.6 constant_dynamic-slice_fusion
  28.4 0.5 convert_multiply_fusion
  29.0 0.7 slice_bitcast_fusion.15
  29.7 2.3 %pad_maximum_fusion.7 = (f32[5,4,130,1]{3,2,1,0:T(8,128)S(1)}, f32[5,4,130,1]{3,2,1,0:T(8,128)S(1)}) fusion(f32[5,4,1,512]{3,2,1,0:T(1,128)} %collective-permute-done.1, f32[5,4,128,512]{3,2,1,0:T(8,128)} %copy-done.2, f32[5,4,1,512]{3,2,1,0:T(1,128)S(1)} %collective-permute-done), kind=kLoop, calls=%fused_computation.16 | loop fusion | flops 10400 | bytes 5345600 | tf_op jit(solution)/shard_map/slice | solution.py:28
  32.1 1.2 copy.124
  33.3 1.2 copy.125
  34.5 1.8 collective-permute-start.3
  36.3 1.8 copy.173
  38.2 1.7 reshape.860.second_ref
  39.9 0.8 copy.130.stacked_ref
  40.6 0.6 reshape.868.drag_ref
  41.3 0.5 copy.126
  41.8 0.5 copy.127
  42.3 5.9 %maximum_multiply_fusion = f32[5,4,130,514]{3,2,1,0:T(8,128)S(1)} fusion(f32[5,4,130,1]{3,2,1,0:T(8,128)S(1)} %copy.127, f32[5,4,1,512]{3,2,1,0:T(1,128)} %collective-permute-done.1, f32[5,4,128,512]{3,2,1,0:T(8,128)} %copy-done.2, f32[5,4,1,512]{3,2,1,0:T(1,128)S(1)} %collective-permute-done, f32[5,4,130,1]{3,2,1,0:T(8,128)S(1)} %copy.126, ...), kind=kLoop, calls=%fused_computation | loop fusion | flops 6682000 | bytes 10691720 | tf_op jit(solution)/shard_map/mul | solution.py:423
  48.2 0.4 slice.258
  48.6 0.2 slice_multiply_fusion.7
  48.9 1.8 slice_subtract_fusion.2
  50.7 0.3 slice_multiply_fusion.3
  51.2 2.7 %fusion.7 = (f32[1,4,128,512]{3,2,1,0:T(8,128)S(1)}, f32[1,4,128,512]{3,2,1,0:T(8,128)S(1)}) fusion(f32[5,4,130,514]{3,2,1,0:T(8,128)S(1)} %maximum_multiply_fusion, f32[128]{0:T(128)S(1)} %add_multiply_fusion, f32[1,4,128,512]{3,2,1,0:T(8,128)S(1)} %bitcast.304, f32[1,4,128,512]{3,2,1,0:T(8,128)S(1)} %bitcast.302), kind=kLoop, calls=%fused_computation.25 | loop fusion | flops 4718592 | bytes 15729152 | tf_op jit(solution)/shard_map/add | solution.py:77
  53.9 0.3 pad_maximum_fusion.1
  54.2 23.0 %all-to-all-done.first_ref = f32[8,16,4096]{2,1,0:T(8,128)} async-done(((f32[8,16,4096]{2,1,0:T(8,128)}), f32[8,16,4096]{2,1,0:T(8,128)}, u32[]{:S(2)}, u32[]{:S(2)}) %all-to-all-start) | async-done | bytes 2097184 | tf_op jit(solution)/shard_map/all_to_all | solution.py:417
  77.1 104.0 %shard_map.55 = (f32[8,8,4608]{2,1,0:T(8,128)}, f32[8,8,4608]{2,1,0:T(8,128)}) custom-call(bf16[256,192]{1,0:T(8,128)(2,1)} %copy.130.stacked_ref, f32[32,256]{1,0:T(8,128)} %bitcast.311, f32[8,16,4096]{2,1,0:T(8,128)} %all-to-all-done.first_ref, f32[8,16,4096]{2,1,0:T(8,128)} %reshape.860.second_ref, f32[2,1,4096]{2,1,0:T(1,128)} %reshape.868.drag_ref), custom_call_target="tpu_custom_call" | custom-call | tf_op jit(solution)/shard_map/pallas_call | solution.py:370
  181.2 1.4 slice.234
  182.6 0.9 slice_add_fusion.9
  183.7 0.6 copy.167
  184.4 0.6 copy.166
  185.1 0.2 copy-done.7
  185.3 0.7 fusion.3
  186.0 0.5 multiply_subtract_fusion.2
  186.5 0.4 multiply_subtract_fusion.5
  187.0 0.4 add_negate_fusion.3
  187.5 0.2 pad_maximum_fusion.4
  188.1 0.5 pad_maximum_fusion.2
  188.6 2.0 %copy.149 = f32[3,4,8,2,8,512]{5,4,3,2,1,0:T(8,128)} copy(f32[3,4,8,2,8,512]{5,4,2,1,0,3:T(8,128)S(1)} %pad_maximum_fusion.2) | data formatting | bytes 6291456 | tf_op jit(solution)/shard_map/stack | solution.py:459
  (67 shorter events, 1.8 us)
Async XLA Ops:
  0.0 27.8 %copy-start = (f32[128,512]{1,0:T(8,128)S(1)}, f32[128,512]{1,0:T(8,128)}, u32[]{:S(2)}) copy-start(f32[128,512]{1,0:T(8,128)} %param.12) | copy-start | bytes 786436
  3.8 1.5 copy-start.6
  5.2 8.4 %copy-start.4 = (f32[2,4,128,512]{3,2,1,0:T(8,128)S(1)}, f32[2,4,128,512]{3,2,1,0:T(8,128)}, u32[]{:S(2)}) copy-start(f32[2,4,128,512]{3,2,1,0:T(8,128)} %param.10) | copy-start | bytes 6291460
  5.5 2.3 %copy-start.2 = (f32[5,4,128,512]{3,2,1,0:T(8,128)}, f32[5,4,128,512]{3,2,1,0:T(8,128)S(1)}, u32[]{:S(2)}) copy-start(f32[5,4,128,512]{3,2,1,0:T(8,128)S(1)} %multiply_dynamic-update-slice_fusion) | copy-start | bytes 15728644
  7.9 21.8 %collective-permute-start = (f32[5,4,1,512]{3,2,1,0:T(1,128)S(1)}, f32[5,4,1,512]{3,2,1,0:T(1,128)S(1)}, u32[]{:S(2)}, u32[]{:S(2)}) collective-permute-start(f32[5,4,1,512]{3,2,1,0:T(1,128)S(1)} %get-tuple-element.60), channel_id=1, source_target_pairs={{0,4},{4,8},{8,12},{12,16},{16,20},{20,24},{24,28},{28,0},{1,5},{5... | collective-permute-start | bytes 122888 | tf_op jit(solution)/shard_map/ppermute | solution.py:27
  10.3 19.4 %collective-permute-start.1 = (f32[5,4,1,512]{3,2,1,0:T(1,128)S(1)}, f32[5,4,1,512]{3,2,1,0:T(1,128)}, u32[]{:S(2)}, u32[]{:S(2)}) collective-permute-start(f32[5,4,1,512]{3,2,1,0:T(1,128)S(1)} %get-tuple-element.61), channel_id=1, source_target_pairs={{4,0},{8,4},{12,8},{16,12},{20,16},{24,20},{28,24},{0,28},{5,1},{9... | collective-permute-start | bytes 122888 | tf_op jit(solution)/shard_map/ppermute | solution.py:30
  17.8 59.3 %all-to-all-start = ((f32[8,16,4096]{2,1,0:T(8,128)}), f32[8,16,4096]{2,1,0:T(8,128)}, u32[]{:S(2)}, u32[]{:S(2)}) async-start(f32[8,16,4096]{2,1,0:T(8,128)} %reshape.867), calls=%async_computation | async-start | bytes 4194304 | tf_op jit(solution)/shard_map/all_to_all | solution.py:417
  27.7 4.3 %copy-start.3 = (f32[256,32]{0,1:T(8,128)}, f32[256,32]{0,1:T(8,128)S(1)}, u32[]{:S(2)}) copy-start(f32[256,32]{0,1:T(8,128)S(1)} %reshape.866) | copy-start | bytes 98308
  29.0 21.7 %copy-start.13 = (f32[2]{0:T(128)}, f32[2]{0:T(128)S(1)}, u32[]{:S(2)}) copy-start(f32[2]{0:T(128)S(1)} %get-tuple-element.106) | copy-start | bytes 28
  29.0 0.7 copy-start.8
  33.3 8.0 %collective-permute-start.2 = (f32[5,4,130,1]{2,0,3,1:T(8,128)S(1)}, f32[5,4,130,1]{2,0,3,1:T(8,128)S(1)}, u32[]{:S(2)}, u32[]{:S(2)}) collective-permute-start(f32[5,4,130,1]{2,0,3,1:T(8,128)S(1)} %copy.124), channel_id=1, source_target_pairs={{0,1},{1,2},{2,3},{3,0},{4,5},{5,6},{6,7},{7,4},{8,9},{9,10},{10,1... | collective-permute-start | bytes 31208 | tf_op jit(solution)/shard_map/ppermute | solution.py:27
  34.5 7.3 %collective-permute-start.3 = (f32[5,4,130,1]{2,0,3,1:T(8,128)S(1)}, f32[5,4,130,1]{2,0,3,1:T(8,128)S(1)}, u32[]{:S(2)}, u32[]{:S(2)}) collective-permute-start(f32[5,4,130,1]{2,0,3,1:T(8,128)S(1)} %copy.125), channel_id=1, source_target_pairs={{1,0},{2,1},{3,2},{0,3},{5,4},{6,5},{7,6},{4,7},{9,8},{10,9},{11,1... | collective-permute-start | bytes 31208 | tf_op jit(solution)/shard_map/ppermute | solution.py:30
  38.2 1.7 copy-start.9
  38.2 2.5 %copy-start.10 = (f32[16,512]{1,0:T(8,128)S(1)}, f32[16,512]{1,0:T(8,128)}, u32[]{:S(2)}) copy-start(f32[16,512]{1,0:T(8,128)} %constant_dynamic-slice_fusion) | copy-start | bytes 98308
  181.2 2.4 %copy-start.5 = (f32[8,8,4608]{2,1,0:T(8,128)S(1)}, f32[8,8,4608]{2,1,0:T(8,128)}, u32[]{:S(2)}) copy-start(f32[8,8,4608]{2,1,0:T(8,128)} %get-tuple-element.36) | copy-start | bytes 3538948
  184.4 0.9 copy-start.7
  185.3 0.7 copy-start.11
  185.3 0.7 copy-start.12
  185.3 0.7 copy-start.14
  185.3 0.7 copy-start.15
  188.1 2.5 %copy-start.1 = (f32[128,512]{1,0:T(8,128)S(1)}, f32[128,512]{1,0:T(8,128)}, u32[]{:S(2)}) copy-start(f32[128,512]{1,0:T(8,128)} %param.12) | copy-start | bytes 786436

commit v4 on v3

--- a/solution.py
+++ b/solution.py
@@ -318,7 +318,7 @@
     stacked = stacked_ref[...]
     table_t = table_t_ref[...]
 
-    def compute(piece, flows_ref):
+    def compute(piece, flows_ref, first_block, last_block):
         def block(index, carry):
             offset = pl.multiple_of(index * width, width)
             drag_row = drag_ref[piece, :, pl.ds(offset, width)]
@@ -335,21 +335,31 @@
                 results[piece, group, pl.ds(index, 1), pl.ds(cells, width)] = rate
             return carry
 
-        lax.fori_loop(0, blocks, block, 0)
-
-    compute(0, first_ref)
+        lax.fori_loop(first_block, last_block, block, 0)
+
+    half = blocks // 2
+    early = pl.ds(0, half * width)
+    late = pl.ds(half * width, cells + cells // (2 * per) - half * width)
+    compute(0, first_ref, 0, blocks)
     sending.append(exchange(1, lambda g: results.at[0, g], lambda g: landed.at[0, g]))
     wait_arrivals(0, lambda g: second_ref.at[g], lambda g: arrived.at[g])
     sending[0][1].wait()
-    compute(1, arrived)
-    sending.append(exchange(2, lambda g: results.at[1, g], lambda g: landed.at[1, g]))
+    compute(1, arrived, 0, half)
+    sending.append(
+        exchange(2, lambda g: results.at[1, g, :, early], lambda g: landed.at[1, g, :, early])
+    )
+    compute(1, arrived, half, blocks)
+    sending.append(
+        exchange(3, lambda g: results.at[1, g, :, late], lambda g: landed.at[1, g, :, late])
+    )
     for copies, local in sending:
         for copy in copies:
             copy.wait_send()
-    sending[1][1].wait()
-    sending[2][1].wait()
+    for copies, local in sending[1:]:
+        local.wait()
     wait_arrivals(1, lambda g: results.at[0, g], lambda g: landed.at[0, g])
-    wait_arrivals(2, lambda g: results.at[1, g], lambda g: landed.at[1, g])
+    wait_arrivals(2, lambda g: results.at[1, g, :, early], lambda g: landed.at[1, g, :, early])
+    wait_arrivals(3, lambda g: results.at[1, g, :, late], lambda g: landed.at[1, g, :, late])
     back_first_ref[...] = landed[0]
     back_second_ref[...] = landed[1]
 
@@ -378,9 +388,9 @@
             pltpu.VMEM((2,) + returned, jnp.float32),
             pltpu.VMEM((coefs, width), jnp.float32),
             pltpu.VMEM((6 * coefs, width), jnp.bfloat16),
-            pltpu.SemaphoreType.DMA((3, groups)),
-            pltpu.SemaphoreType.DMA((3, groups)),
-            pltpu.SemaphoreType.DMA((3,)),
+            pltpu.SemaphoreType.DMA((4, groups)),
+            pltpu.SemaphoreType.DMA((4, groups)),
+            pltpu.SemaphoreType.DMA((4,)),
         ],
         compiler_params=pltpu.CompilerParams(
             collective_id=0, has_side_effects=True, vmem_limit_bytes=60 * 1024 * 1024

time: 191 us -> 192 us (level)
  no operation moved by 1% of the time
where the time goes in v4:
time: 192 us; the launch traced here: 191 us
  Pallas kernels  105 us (55%)
  other arithmetic  25.1 us (13%)
  waiting for transfers between devices  23 us (12%)
  local copies, waits for them, and re-layouts  21.9 us (11%)
  starting transfers between devices  16 us (8%)
    pallas_call x1, Pallas kernels, exchange_friction(): pl.pallas_call(functools.partial(exchange_kernel, groups, width), in_spec...  105 us
    all_to_all x1, waiting for transfers between devices, local(): lax.all_to_all(payloads[0], 'freq', split_axis=0, concat_axis=0, tiled=True)  23 us
    all_to_all x1, starting transfers between devices, local(): lax.all_to_all(payloads[0], 'freq', split_axis=0, concat_axis=0, tiled=True)  8.47 us
    mul x1, other arithmetic, local(): extended = extended * rim_keep[:, None]  5.92 us
    unnamed x36, local copies, waits for them, and re-layouts  5.84 us
    ppermute x2, starting transfers between devices, extended_2(): lax.ppermute(lax.slice_in_dim(block, 0, width, axis=dim), axis, backward)  5.12 us
    unnamed x9, other arithmetic  4.33 us
  transfers between devices with their start and end apart: 5, of which 1 were waited for; matrix products, arithmetic and copies ran while one was open for 16% of the time, Pallas kernels for 0%

profile of v4, /device:TPU:8, one launch (start us, length us, event | category | flops | bytes accessed | tf_op | source)
XLA Modules:
  0.0 191.5 jit_solution(291129171469859191)
XLA Ops:
  0.0 1.0 convert_element_type.53
  1.0 1.3 multiply_dynamic-update-slice_fusion.2
  2.4 1.4 constant_dynamic-update-slice_fusion.1
  3.8 1.4 constant_dynamic-update-slice_fusion
  5.5 2.3 %copy-done.2 = f32[5,4,128,512]{3,2,1,0:T(8,128)} copy-done((f32[5,4,128,512]{3,2,1,0:T(8,128)}, f32[5,4,128,512]{3,2,1,0:T(8,128)S(1)}, u32[]{:S(2)}) %copy-start.2) | copy-done | bytes 5242904
  7.9 2.4 %collective-permute-start = (f32[5,4,1,512]{3,2,1,0:T(1,128)S(1)}, f32[5,4,1,512]{3,2,1,0:T(1,128)S(1)}, u32[]{:S(2)}, u32[]{:S(2)}) collective-permute-start(f32[5,4,1,512]{3,2,1,0:T(1,128)S(1)} %get-tuple-element.60), channel_id=1, source_target_pairs={{0,4},{4,8},{8,12},{12,16},{16,20},{20,24},{24,28},{28,0},{1,5},{5... | collective-permute-start | bytes 122888 | tf_op jit(solution)/shard_map/ppermute | solution.py:27
  10.3 3.3 %collective-permute-start.1 = (f32[5,4,1,512]{3,2,1,0:T(1,128)S(1)}, f32[5,4,1,512]{3,2,1,0:T(1,128)}, u32[]{:S(2)}, u32[]{:S(2)}) collective-permute-start(f32[5,4,1,512]{3,2,1,0:T(1,128)S(1)} %get-tuple-element.61), channel_id=1, source_target_pairs={{4,0},{8,4},{12,8},{16,12},{20,16},{24,20},{28,24},{0,28},{5,1},{9... | collective-permute-start | bytes 122888 | tf_op jit(solution)/shard_map/ppermute | solution.py:30
  13.6 0.6 pad_maximum_fusion
  14.2 1.8 fusion.51
  16.0 0.2 copy.172
  16.2 1.6 reshape.867
  17.8 8.5 %all-to-all-start = ((f32[8,16,4096]{2,1,0:T(8,128)}), f32[8,16,4096]{2,1,0:T(8,128)}, u32[]{:S(2)}, u32[]{:S(2)}) async-start(f32[8,16,4096]{2,1,0:T(8,128)} %reshape.867), calls=%async_computation | async-start | bytes 4194304 | tf_op jit(solution)/shard_map/all_to_all | solution.py:427
  26.3 0.6 fusion.44
  26.9 0.6 slice_bitcast_fusion.17
  27.8 0.6 constant_dynamic-slice_fusion
  28.4 0.5 convert_multiply_fusion
  29.0 0.7 slice_bitcast_fusion.15
  29.7 2.3 %pad_maximum_fusion.7 = (f32[5,4,130,1]{3,2,1,0:T(8,128)S(1)}, f32[5,4,130,1]{3,2,1,0:T(8,128)S(1)}) fusion(f32[5,4,1,512]{3,2,1,0:T(1,128)} %collective-permute-done.1, f32[5,4,128,512]{3,2,1,0:T(8,128)} %copy-done.2, f32[5,4,1,512]{3,2,1,0:T(1,128)S(1)} %collective-permute-done), kind=kLoop, calls=%fused_computation.16 | loop fusion | flops 10400 | bytes 5345600 | tf_op jit(solution)/shard_map/slice | solution.py:28
  32.1 1.2 copy.124
  33.3 1.2 copy.125
  34.5 1.8 collective-permute-start.3
  36.3 1.8 copy.173
  38.2 1.7 reshape.860.second_ref
  39.9 0.8 copy.130.stacked_ref
  40.6 0.6 reshape.868.drag_ref
  41.3 0.5 copy.126
  41.8 0.5 copy.127
  42.3 5.9 %maximum_multiply_fusion = f32[5,4,130,514]{3,2,1,0:T(8,128)S(1)} fusion(f32[5,4,130,1]{3,2,1,0:T(8,128)S(1)} %copy.127, f32[5,4,1,512]{3,2,1,0:T(1,128)} %collective-permute-done.1, f32[5,4,128,512]{3,2,1,0:T(8,128)} %copy-done.2, f32[5,4,1,512]{3,2,1,0:T(1,128)S(1)} %collective-permute-done, f32[5,4,130,1]{3,2,1,0:T(8,128)S(1)} %copy.126, ...), kind=kLoop, calls=%fused_computation | loop fusion | flops 6682000 | bytes 10691720 | tf_op jit(solution)/shard_map/mul | solution.py:433
  48.2 0.4 slice.258
  48.6 0.2 slice_multiply_fusion.7
  48.9 1.8 slice_subtract_fusion.2
  50.7 0.3 slice_multiply_fusion.3
  51.2 2.7 %fusion.7 = (f32[1,4,128,512]{3,2,1,0:T(8,128)S(1)}, f32[1,4,128,512]{3,2,1,0:T(8,128)S(1)}) fusion(f32[5,4,130,514]{3,2,1,0:T(8,128)S(1)} %maximum_multiply_fusion, f32[128]{0:T(128)S(1)} %add_multiply_fusion, f32[1,4,128,512]{3,2,1,0:T(8,128)S(1)} %bitcast.304, f32[1,4,128,512]{3,2,1,0:T(8,128)S(1)} %bitcast.302), kind=kLoop, calls=%fused_computation.25 | loop fusion | flops 4718592 | bytes 15729152 | tf_op jit(solution)/shard_map/add | solution.py:77
  53.9 0.3 pad_maximum_fusion.1
  54.2 23.0 %all-to-all-done.first_ref = f32[8,16,4096]{2,1,0:T(8,128)} async-done(((f32[8,16,4096]{2,1,0:T(8,128)}), f32[8,16,4096]{2,1,0:T(8,128)}, u32[]{:S(2)}, u32[]{:S(2)}) %all-to-all-start) | async-done | bytes 2097184 | tf_op jit(solution)/shard_map/all_to_all | solution.py:427
  77.1 105.0 %shard_map.55 = (f32[8,8,4608]{2,1,0:T(8,128)}, f32[8,8,4608]{2,1,0:T(8,128)}) custom-call(bf16[256,192]{1,0:T(8,128)(2,1)} %copy.130.stacked_ref, f32[32,256]{1,0:T(8,128)} %bitcast.311, f32[8,16,4096]{2,1,0:T(8,128)} %all-to-all-done.first_ref, f32[8,16,4096]{2,1,0:T(8,128)} %reshape.860.second_ref, f32[2,1,4096]{2,1,0:T(1,128)} %reshape.868.drag_ref), custom_call_target="tpu_custom_call" | custom-call | tf_op jit(solution)/shard_map/pallas_call | solution.py:380
  182.1 1.4 slice.234
  183.5 0.9 slice_add_fusion.9
  184.6 0.6 copy.167
  185.3 0.6 copy.166
  186.0 0.2 copy-done.7
  186.2 0.7 fusion.3
  186.9 0.5 multiply_subtract_fusion.2
  187.5 0.4 multiply_subtract_fusion.5
  187.9 0.4 add_negate_fusion.3
  188.4 0.2 pad_maximum_fusion.4
  189.0 0.5 pad_maximum_fusion.2
  189.5 2.0 %copy.149 = f32[3,4,8,2,8,512]{5,4,3,2,1,0:T(8,128)} copy(f32[3,4,8,2,8,512]{5,4,2,1,0,3:T(8,128)S(1)} %pad_maximum_fusion.2) | data formatting | bytes 6291456 | tf_op jit(solution)/shard_map/stack | solution.py:469
  (67 shorter events, 1.8 us)
Async XLA Ops:
  0.0 27.8 %copy-start = (f32[128,512]{1,0:T(8,128)S(1)}, f32[128,512]{1,0:T(8,128)}, u32[]{:S(2)}) copy-start(f32[128,512]{1,0:T(8,128)} %param.12) | copy-start | bytes 786436
  3.8 1.5 copy-start.6
  5.2 8.4 %copy-start.4 = (f32[2,4,128,512]{3,2,1,0:T(8,128)S(1)}, f32[2,4,128,512]{3,2,1,0:T(8,128)}, u32[]{:S(2)}) copy-start(f32[2,4,128,512]{3,2,1,0:T(8,128)} %param.10) | copy-start | bytes 6291460
  5.5 2.3 %copy-start.2 = (f32[5,4,128,512]{3,2,1,0:T(8,128)}, f32[5,4,128,512]{3,2,1,0:T(8,128)S(1)}, u32[]{:S(2)}) copy-start(f32[5,4,128,512]{3,2,1,0:T(8,128)S(1)} %multiply_dynamic-update-slice_fusion) | copy-start | bytes 15728644
  7.9 21.8 %collective-permute-start = (f32[5,4,1,512]{3,2,1,0:T(1,128)S(1)}, f32[5,4,1,512]{3,2,1,0:T(1,128)S(1)}, u32[]{:S(2)}, u32[]{:S(2)}) collective-permute-start(f32[5,4,1,512]{3,2,1,0:T(1,128)S(1)} %get-tuple-element.60), channel_id=1, source_target_pairs={{0,4},{4,8},{8,12},{12,16},{16,20},{20,24},{24,28},{28,0},{1,5},{5... | collective-permute-start | bytes 122888 | tf_op jit(solution)/shard_map/ppermute | solution.py:27
  10.3 19.4 %collective-permute-start.1 = (f32[5,4,1,512]{3,2,1,0:T(1,128)S(1)}, f32[5,4,1,512]{3,2,1,0:T(1,128)}, u32[]{:S(2)}, u32[]{:S(2)}) collective-permute-start(f32[5,4,1,512]{3,2,1,0:T(1,128)S(1)} %get-tuple-element.61), channel_id=1, source_target_pairs={{4,0},{8,4},{12,8},{16,12},{20,16},{24,20},{28,24},{0,28},{5,1},{9... | collective-permute-start | bytes 122888 | tf_op jit(solution)/shard_map/ppermute | solution.py:30
  17.8 59.3 %all-to-all-start = ((f32[8,16,4096]{2,1,0:T(8,128)}), f32[8,16,4096]{2,1,0:T(8,128)}, u32[]{:S(2)}, u32[]{:S(2)}) async-start(f32[8,16,4096]{2,1,0:T(8,128)} %reshape.867), calls=%async_computation | async-start | bytes 4194304 | tf_op jit(solution)/shard_map/all_to_all | solution.py:427
  27.7 4.3 %copy-start.3 = (f32[256,32]{0,1:T(8,128)}, f32[256,32]{0,1:T(8,128)S(1)}, u32[]{:S(2)}) copy-start(f32[256,32]{0,1:T(8,128)S(1)} %reshape.866) | copy-start | bytes 98308
  29.0 21.7 %copy-start.13 = (f32[2]{0:T(128)}, f32[2]{0:T(128)S(1)}, u32[]{:S(2)}) copy-start(f32[2]{0:T(128)S(1)} %get-tuple-element.106) | copy-start | bytes 28
  29.0 0.7 copy-start.8
  33.3 8.0 %collective-permute-start.2 = (f32[5,4,130,1]{2,0,3,1:T(8,128)S(1)}, f32[5,4,130,1]{2,0,3,1:T(8,128)S(1)}, u32[]{:S(2)}, u32[]{:S(2)}) collective-permute-start(f32[5,4,130,1]{2,0,3,1:T(8,128)S(1)} %copy.124), channel_id=1, source_target_pairs={{0,1},{1,2},{2,3},{3,0},{4,5},{5,6},{6,7},{7,4},{8,9},{9,10},{10,1... | collective-permute-start | bytes 31208 | tf_op jit(solution)/shard_map/ppermute | solution.py:27
  34.5 7.3 %collective-permute-start.3 = (f32[5,4,130,1]{2,0,3,1:T(8,128)S(1)}, f32[5,4,130,1]{2,0,3,1:T(8,128)S(1)}, u32[]{:S(2)}, u32[]{:S(2)}) collective-permute-start(f32[5,4,130,1]{2,0,3,1:T(8,128)S(1)} %copy.125), channel_id=1, source_target_pairs={{1,0},{2,1},{3,2},{0,3},{5,4},{6,5},{7,6},{4,7},{9,8},{10,9},{11,1... | collective-permute-start | bytes 31208 | tf_op jit(solution)/shard_map/ppermute | solution.py:30
  38.2 1.7 copy-start.9
  38.2 2.5 %copy-start.10 = (f32[16,512]{1,0:T(8,128)S(1)}, f32[16,512]{1,0:T(8,128)}, u32[]{:S(2)}) copy-start(f32[16,512]{1,0:T(8,128)} %constant_dynamic-slice_fusion) | copy-start | bytes 98308
  182.1 2.4 %copy-start.5 = (f32[8,8,4608]{2,1,0:T(8,128)S(1)}, f32[8,8,4608]{2,1,0:T(8,128)}, u32[]{:S(2)}) copy-start(f32[8,8,4608]{2,1,0:T(8,128)} %get-tuple-element.36) | copy-start | bytes 3538948
  185.3 0.9 copy-start.7
  186.2 0.7 copy-start.11
  186.2 0.7 copy-start.12
  186.2 0.7 copy-start.14
  186.2 0.7 copy-start.15
  189.0 2.5 %copy-start.1 = (f32[128,512]{1,0:T(8,128)S(1)}, f32[128,512]{1,0:T(8,128)}, u32[]{:S(2)}) copy-start(f32[128,512]{1,0:T(8,128)} %param.12) | copy-start | bytes 786436

commit v5 on v3

--- a/solution.py
+++ b/solution.py
@@ -254,6 +254,7 @@
 def exchange_kernel(
     groups,
     width,
+    stacked_first_ref,
     stacked_ref,
     table_t_ref,
     first_ref,
@@ -315,10 +316,11 @@
             ).wait_recv()
 
     sending = [exchange(0, lambda g: second_ref.at[g], lambda g: arrived.at[g])]
-    stacked = stacked_ref[...]
     table_t = table_t_ref[...]
 
-    def compute(piece, flows_ref):
+    def compute(piece, flows_ref, stacked_in):
+        stacked = stacked_in[...]
+
         def block(index, carry):
             offset = pl.multiple_of(index * width, width)
             drag_row = drag_ref[piece, :, pl.ds(offset, width)]
@@ -337,11 +339,11 @@
 
         lax.fori_loop(0, blocks, block, 0)
 
-    compute(0, first_ref)
+    compute(0, first_ref, stacked_first_ref)
     sending.append(exchange(1, lambda g: results.at[0, g], lambda g: landed.at[0, g]))
     wait_arrivals(0, lambda g: second_ref.at[g], lambda g: arrived.at[g])
     sending[0][1].wait()
-    compute(1, arrived)
+    compute(1, arrived, stacked_ref)
     sending.append(exchange(2, lambda g: results.at[1, g], lambda g: landed.at[1, g]))
     for copies, local in sending:
         for copy in copies:
@@ -354,22 +356,30 @@
     back_second_ref[...] = landed[1]
 
 
+def stack_table(table):
+    high = lax.reduce_precision(table, exponent_bits=8, mantissa_bits=7)
+    rest = table - high
+    middle = lax.reduce_precision(rest, exponent_bits=8, mantissa_bits=7)
+    low = lax.reduce_precision(rest - middle, exponent_bits=8, mantissa_bits=7)
+    stacked = jnp.concatenate([high, middle, middle, high, low, high], axis=1)
+    return stacked.astype(jnp.bfloat16)
+
+
 def exchange_friction(first, second, drag_band, table, width):
     groups, rows_in, cells = first.shape
     coefs = table.shape[1]
     per = coefs // groups
     table_t = jnp.transpose(table)
-    high = lax.reduce_precision(table, exponent_bits=8, mantissa_bits=7)
-    rest = table - high
-    middle = lax.reduce_precision(rest, exponent_bits=8, mantissa_bits=7)
-    low = lax.reduce_precision(rest - middle, exponent_bits=8, mantissa_bits=7)
-    stacked = jnp.concatenate([high, middle, middle, high, low, high], axis=1)
-    stacked = stacked.astype(jnp.bfloat16)
+    member = lax.axis_index("freq")
+    senders = lax.rem(member + groups - jnp.arange(groups, dtype=jnp.int32), groups)
+    order = (senders[:, None] * per + jnp.arange(per, dtype=jnp.int32)[None, :]).reshape(coefs)
+    stacked_first = stack_table(jnp.take(table, order, axis=1))
+    stacked = stack_table(table)
     returned = (groups, 2 * per, cells + cells // (2 * per))
     vmem = pl.BlockSpec(memory_space=pltpu.VMEM)
     return pl.pallas_call(
         functools.partial(exchange_kernel, groups, width),
-        in_specs=[vmem] * 5,
+        in_specs=[vmem] * 6,
         out_specs=[vmem, vmem],
         out_shape=[jax.ShapeDtypeStruct(returned, jnp.float32)] * 2,
         scratch_shapes=[
@@ -385,7 +395,7 @@
         compiler_params=pltpu.CompilerParams(
             collective_id=0, has_side_effects=True, vmem_limit_bytes=60 * 1024 * 1024
         ),
-    )(stacked, table_t, first, second, drag_band)
+    )(stacked_first, stacked, table_t, first, second, drag_band)
 
 
 def local(direction, base_flow, water_depth, drag_factor, wet_mask, pieces=2):
@@ -414,7 +424,13 @@
         jnp.moveaxis(flows[:, :, piece], 1, 0).reshape(groups, 4 * local_coefs, piece_cells)
         for piece in range(pieces)
     ]
-    sent = [lax.all_to_all(payloads[0], "freq", split_axis=0, concat_axis=0, tiled=True)]
+    by_distance = [lax.dynamic_index_in_dim(payloads[0], member, 0, keepdims=False)]
+    for distance in range(1, groups):
+        target = lax.rem(member + distance, groups)
+        piece = lax.dynamic_index_in_dim(payloads[0], target, 0, keepdims=False)
+        pairs = [(source, (source + distance) % groups) for source in range(groups)]
+        by_distance.append(lax.ppermute(piece, "freq", pairs))
+    sent = [jnp.stack(by_distance)]
     planes = jnp.stack([height, east, north, water_depth * east, water_depth * north])
     extended = extended_2(planes, (("lat", 2), ("lon", 3)), 1)
     rim_keep = jnp.ones((tile_rows + 2,), jnp.float32)

time: 191 us -> 214 us (1.12)
  local copies, waits for them, and re-layouts: 21.9 us -> 35.5 us
  starting transfers between devices: 16 us -> 26.2 us
  waiting for transfers between devices: 23 us -> 15.1 us
  Pallas kernels: 104 us -> 108 us
  other arithmetic: 25.1 us -> 27.4 us
    all_to_all x1 -> x0, waiting for transfers between devices: 23 us -> none  [local(): lax.all_to_all(payloads[0], 'freq', split_axis=0, concat_axis=0, tiled=True)]
    ppermute x0 -> x7, starting transfers between devices: none -> 18.6 us  [local(): by_distance.append(lax.ppermute(piece, 'freq', pairs))]
    ppermute x0 -> x7, waiting for transfers between devices: none -> 15.1 us  [local(): by_distance.append(lax.ppermute(piece, 'freq', pairs))]
    all_to_all x1 -> x0, starting transfers between devices: 8.47 us -> none  [local(): lax.all_to_all(payloads[0], 'freq', split_axis=0, concat_axis=0, tiled=True)]
    unnamed x36 -> x26, local copies, waits for them, and re-layouts: 5.84 us -> 13.2 us
    pallas_call x1, Pallas kernels: 104 us -> 108 us  [exchange_friction(): pl.pallas_call(functools.partial(exchange_kernel, groups, width), in_spec...]
    transpose x0 -> x1, local copies, waits for them, and re-layouts: none -> 2.65 us  [local(): jnp.moveaxis(flows[:, :, piece], 1, 0)]
  transfers between devices with their start and end apart: 5 -> 11, of which waited for: 1 -> 3; matrix products, arithmetic and copies ran while one was open for 16% -> 21% of each run, Pallas kernels for 0% -> 0%
where the time goes in v5:
time: 214 us; the launch traced here: 213 us
  Pallas kernels  108 us (50%)
  local copies, waits for them, and re-layouts  35.5 us (17%)
  other arithmetic  27.4 us (13%)
  starting transfers between devices  26.2 us (12%)
  waiting for transfers between devices  15.1 us (7%)
    pallas_call x1, Pallas kernels, exchange_friction(): pl.pallas_call(functools.partial(exchange_kernel, groups, width), in_spec...  108 us
    ppermute x7, starting transfers between devices, local(): by_distance.append(lax.ppermute(piece, 'freq', pairs))  18.6 us
    ppermute x7, waiting for transfers between devices, local(): by_distance.append(lax.ppermute(piece, 'freq', pairs))  15.1 us
    unnamed x26, local copies, waits for them, and re-layouts  13.2 us
    mul x1, other arithmetic, local(): extended = extended * rim_keep[:, None]  5.89 us
    ppermute x2, starting transfers between devices, extended_2(): lax.ppermute(lax.slice_in_dim(block, 0, width, axis=dim), axis, backward)  5.12 us
    unnamed x9, other arithmetic  4.33 us
  transfers between devices with their start and end apart: 11, of which 3 were waited for; matrix products, arithmetic and copies ran while one was open for 21% of the time, Pallas kernels for 0%

profile of v5, /device:TPU:8, one launch (start us, length us, event | category | flops | bytes accessed | tf_op | source)
XLA Modules:
  0.0 212.5 jit_solution(17998078231309389889)
XLA Ops:
  0.0 1.0 convert_element_type.54
  1.0 1.3 multiply_dynamic-update-slice_fusion.2
  2.4 1.4 constant_dynamic-update-slice_fusion.1
  3.8 1.4 constant_dynamic-update-slice_fusion
  5.5 2.3 %copy-done.3 = f32[5,4,128,512]{3,2,1,0:T(8,128)} copy-done((f32[5,4,128,512]{3,2,1,0:T(8,128)}, f32[5,4,128,512]{3,2,1,0:T(8,128)S(1)}, u32[]{:S(2)}) %copy-start.3) | copy-done | bytes 5242904
  7.9 2.4 %collective-permute-start = (f32[5,4,1,512]{3,2,1,0:T(1,128)S(1)}, f32[5,4,1,512]{3,2,1,0:T(1,128)S(1)}, u32[]{:S(2)}, u32[]{:S(2)}) collective-permute-start(f32[5,4,1,512]{3,2,1,0:T(1,128)S(1)} %get-tuple-element.60), channel_id=1, source_target_pairs={{0,4},{4,8},{8,12},{12,16},{16,20},{20,24},{24,28},{28,0},{1,5},{5... | collective-permute-start | bytes 122888 | tf_op jit(solution)/shard_map/ppermute | solution.py:27
  10.3 3.3 %collective-permute-start.1 = (f32[5,4,1,512]{3,2,1,0:T(1,128)S(1)}, f32[5,4,1,512]{3,2,1,0:T(1,128)S(1)}, u32[]{:S(2)}, u32[]{:S(2)}) collective-permute-start(f32[5,4,1,512]{3,2,1,0:T(1,128)S(1)} %get-tuple-element.61), channel_id=1, source_target_pairs={{4,0},{8,4},{12,8},{16,12},{20,16},{24,20},{28,24},{0,28},{5,1},{9... | collective-permute-start | bytes 122888 | tf_op jit(solution)/shard_map/ppermute | solution.py:30
  13.6 2.2 %pad_maximum_fusion = f32[4,4,128,512]{3,2,1,0:T(8,128)S(1)} fusion(f32[1,4,128,512]{3,2,1,0:T(8,128)S(1)} %get-tuple-element.50, f32[1,4,128,512]{3,2,1,0:T(8,128)S(1)} %get-tuple-element.52, f32[2,4,128,512]{3,2,1,0:T(8,128)} %param.10), kind=kLoop, calls=%fused_computation.2 | loop fusion | flops 2097152 | bytes 8388608 | tf_op jit(solution)/shard_map/concatenate | solution.py:417
  15.8 0.6 fusion.56
  16.5 2.7 %copy_bitcast_fusion = (f32[8,16,8,512]{3,2,1,0:T(8,128)}, f32[8,16,8,512]{3,2,1,0:T(8,128)}) fusion(f32[16,8,1,8,512]{4,3,2,1,0:T(8,128)S(1)} %get-tuple-element.63, f32[16,8,1,8,512]{4,3,2,1,0:T(8,128)S(1)} %get-tuple-element.62), kind=kLoop, calls=%fused_computation.5 | loop fusion | bytes 8388608 | tf_op jit(solution)/shard_map/transpose | solution.py:424
  19.1 1.7 reshape.918
  20.9 1.3 dynamic-slice_bitcast_fusion
  22.3 1.9 collective-permute-start.4
  24.2 3.3 %collective-permute-start.5 = (f32[16,4096]{1,0:T(8,128)}, f32[16,4096]{1,0:T(8,128)}, u32[]{:S(2)}, u32[]{:S(2)}) collective-permute-start(f32[16,4096]{1,0:T(8,128)} %get-tuple-element.71), channel_id=1, source_target_pairs={{0,64},{32,96},{64,128},{96,160},{128,192},{160,224},{192,0},{224,... | collective-permute-start | bytes 786440 | tf_op jit(solution)/shard_map/ppermute | solution.py:432
  27.5 4.0 %collective-permute-start.6 = (f32[16,4096]{1,0:T(8,128)}, f32[16,4096]{1,0:T(8,128)}, u32[]{:S(2)}, u32[]{:S(2)}) collective-permute-start(f32[16,4096]{1,0:T(8,128)} %get-tuple-element.70), channel_id=1, source_target_pairs={{0,96},{32,128},{64,160},{96,192},{128,224},{160,0},{192,32},{224,... | collective-permute-start | bytes 786440 | tf_op jit(solution)/shard_map/ppermute | solution.py:432
  32.1 0.6 gather_fusion
  33.0 3.9 %pad_maximum_fusion.7 = (f32[5,4,130,1]{3,2,1,0:T(8,128)}, f32[5,4,130,1]{3,2,1,0:T(8,128)}) fusion(f32[5,4,1,512]{3,2,1,0:T(1,128)S(1)} %collective-permute-done.1, f32[5,4,128,512]{3,2,1,0:T(8,128)} %copy-done.3, f32[5,4,1,512]{3,2,1,0:T(1,128)S(1)} %collective-permute-done), kind=kLoop, calls=%fused_computation.17 | loop fusion | flops 10400 | bytes 5345600 | tf_op jit(solution)/shard_map/slice | solution.py:28
  36.9 2.7 %copy.148 = f32[5,4,130,1]{2,0,3,1:T(8,128)S(1)} copy(f32[5,4,130,1]{3,2,1,0:T(8,128)} %get-tuple-element.58) | data formatting | bytes 20800 | tf_op jit(solution)/shard_map/slice | solution.py:28
  39.7 2.6 %copy.149 = f32[5,4,130,1]{2,0,3,1:T(8,128)S(1)} copy(f32[5,4,130,1]{3,2,1,0:T(8,128)} %get-tuple-element.59) | data formatting | bytes 20800 | tf_op jit(solution)/shard_map/slice | solution.py:30
  42.2 1.8 collective-permute-start.3
  44.0 1.5 reshape.911.second_ref
  45.6 0.8 copy.155.stacked_ref
  46.3 0.6 reshape.919.drag_ref
  47.0 0.8 concatenate.30.stacked_first_ref
  48.9 5.2 %collective-permute-start.8 = (f32[16,4096]{1,0:T(8,128)}, f32[16,4096]{1,0:T(8,128)}, u32[]{:S(2)}, u32[]{:S(2)}) collective-permute-start(f32[16,4096]{1,0:T(8,128)} %get-tuple-element.68), channel_id=1, source_target_pairs={{0,160},{32,192},{64,224},{96,0},{128,32},{160,64},{192,96},{224,1... | collective-permute-start | bytes 786440 | tf_op jit(solution)/shard_map/ppermute | solution.py:432
  54.6 5.9 %maximum_multiply_fusion = f32[5,4,130,514]{3,2,1,0:T(8,128)S(1)} fusion(f32[5,4,130,1]{3,2,1,0:T(8,128)S(1)} %copy.151, f32[5,4,1,512]{3,2,1,0:T(1,128)S(1)} %collective-permute-done.1, f32[5,4,128,512]{3,2,1,0:T(8,128)} %copy-done.3, f32[5,4,1,512]{3,2,1,0:T(1,128)S(1)} %collective-permute-done, f32[5,4,130,1]{3,2,1,0:T(8,128)S(1)} %copy.150, ...), kind=kLoop, calls=%fused_computation.1 | loop fusion | flops 6682000 | bytes 10691720 | tf_op jit(solution)/shard_map/mul | solution.py:439
  61.1 1.8 slice_subtract_fusion.2
  63.4 2.7 %fusion.7 = (f32[1,4,128,512]{3,2,1,0:T(8,128)S(1)}, f32[1,4,128,512]{3,2,1,0:T(8,128)S(1)}) fusion(f32[5,4,130,514]{3,2,1,0:T(8,128)S(1)} %maximum_multiply_fusion, f32[128]{0:T(128)S(1)} %add_multiply_fusion, f32[1,4,128,512]{3,2,1,0:T(8,128)S(1)} %bitcast.338, f32[1,4,128,512]{3,2,1,0:T(8,128)S(1)} %bitcast.336), kind=kLoop, calls=%fused_computation.26 | loop fusion | flops 4718592 | bytes 15729152 | tf_op jit(solution)/shard_map/add | solution.py:77
  66.5 0.6 copy-done.8
  67.1 2.7 %collective-permute-start.9 = (f32[16,4096]{1,0:T(8,128)S(1)}, f32[16,4096]{1,0:T(8,128)S(1)}, u32[]{:S(2)}, u32[]{:S(2)}) collective-permute-start(f32[16,4096]{1,0:T(8,128)S(1)} %copy-done.8), channel_id=1, source_target_pairs={{0,192},{32,224},{64,0},{96,32},{128,64},{160,96},{192,128},{224,1... | collective-permute-start | bytes 786440 | tf_op jit(solution)/shard_map/ppermute | solution.py:432
  69.8 1.7 bitcast_dynamic-update-slice_fusion.6
  71.4 1.0 collective-permute-start.10
  72.4 1.7 bitcast_dynamic-update-slice_fusion.5
  74.1 1.7 bitcast_dynamic-update-slice_fusion.4
  75.8 1.7 bitcast_dynamic-update-slice_fusion.3
  77.5 5.9 %collective-permute-done.8 = f32[16,4096]{1,0:T(8,128)} collective-permute-done((f32[16,4096]{1,0:T(8,128)}, f32[16,4096]{1,0:T(8,128)}, u32[]{:S(2)}, u32[]{:S(2)}) %collective-permute-start.8) | collective-permute-done | bytes 262176 | tf_op jit(solution)/shard_map/ppermute | solution.py:432
  83.3 1.7 bitcast_dynamic-update-slice_fusion.2
  85.0 6.2 %collective-permute-done.9 = f32[16,4096]{1,0:T(8,128)S(1)} collective-permute-done((f32[16,4096]{1,0:T(8,128)S(1)}, f32[16,4096]{1,0:T(8,128)S(1)}, u32[]{:S(2)}, u32[]{:S(2)}) %collective-permute-start.9) | collective-permute-done | bytes 262176 | tf_op jit(solution)/shard_map/ppermute | solution.py:432
  91.2 0.7 bitcast_dynamic-update-slice_fusion.1
  91.9 3.0 %collective-permute-done.10 = f32[16,4096]{1,0:T(8,128)S(1)} collective-permute-done((f32[16,4096]{1,0:T(8,128)S(1)}, f32[16,4096]{1,0:T(8,128)S(1)}, u32[]{:S(2)}, u32[]{:S(2)}) %collective-permute-start.10) | collective-permute-done | bytes 262176 | tf_op jit(solution)/shard_map/ppermute | solution.py:432
  94.9 0.7 bitcast_dynamic-update-slice_fusion.first_ref
  95.6 107.8 %shard_map.55 = (f32[8,8,4608]{2,1,0:T(8,128)}, f32[8,8,4608]{2,1,0:T(8,128)}) custom-call(bf16[256,192]{1,0:T(8,128)(2,1)} %concatenate.30.stacked_first_ref, bf16[256,192]{1,0:T(8,128)(2,1)} %copy.155.stacked_ref, f32[32,256]{1,0:T(8,128)} %bitcast.325, f32[8,16,4096]{2,1,0:T(8,128)} %bitcast_dynamic-update-slice_fusion.first_ref, ...), custom_call_target="tpu_custom_call" | custom-call | tf_op jit(solution)/shard_map/pallas_call | solution.py:380
  203.4 1.4 slice.234
  204.8 0.9 slice_add_fusion.9
  205.9 0.6 copy.192
  206.6 0.6 copy.191
  207.3 0.7 fusion.3
  210.6 2.0 copy.174
  (83 shorter events, 7.0 us)
Async XLA Ops:
  0.0 33.0 %copy-start = (f32[128,512]{1,0:T(8,128)S(1)}, f32[128,512]{1,0:T(8,128)}, u32[]{:S(2)}) copy-start(f32[128,512]{1,0:T(8,128)} %param.12) | copy-start | bytes 786436
  3.8 1.5 copy-start.6
  5.5 2.3 %copy-start.3 = (f32[5,4,128,512]{3,2,1,0:T(8,128)}, f32[5,4,128,512]{3,2,1,0:T(8,128)S(1)}, u32[]{:S(2)}) copy-start(f32[5,4,128,512]{3,2,1,0:T(8,128)S(1)} %multiply_dynamic-update-slice_fusion) | copy-start | bytes 15728644
  7.9 25.1 %collective-permute-start = (f32[5,4,1,512]{3,2,1,0:T(1,128)S(1)}, f32[5,4,1,512]{3,2,1,0:T(1,128)S(1)}, u32[]{:S(2)}, u32[]{:S(2)}) collective-permute-start(f32[5,4,1,512]{3,2,1,0:T(1,128)S(1)} %get-tuple-element.60), channel_id=1, source_target_pairs={{0,4},{4,8},{8,12},{12,16},{16,20},{20,24},{24,28},{28,0},{1,5},{5... | collective-permute-start | bytes 122888 | tf_op jit(solution)/shard_map/ppermute | solution.py:27
  10.3 22.8 %collective-permute-start.1 = (f32[5,4,1,512]{3,2,1,0:T(1,128)S(1)}, f32[5,4,1,512]{3,2,1,0:T(1,128)S(1)}, u32[]{:S(2)}, u32[]{:S(2)}) collective-permute-start(f32[5,4,1,512]{3,2,1,0:T(1,128)S(1)} %get-tuple-element.61), channel_id=1, source_target_pairs={{4,0},{8,4},{12,8},{16,12},{20,16},{24,20},{28,24},{0,28},{5,1},{9... | collective-permute-start | bytes 122888 | tf_op jit(solution)/shard_map/ppermute | solution.py:30
  22.3 44.2 %collective-permute-start.4 = (f32[16,4096]{1,0:T(8,128)}, f32[16,4096]{1,0:T(8,128)}, u32[]{:S(2)}, u32[]{:S(2)}) collective-permute-start(f32[16,4096]{1,0:T(8,128)} %get-tuple-element.72), channel_id=1, source_target_pairs={{0,32},{32,64},{64,96},{96,128},{128,160},{160,192},{192,224},{224... | collective-permute-start | bytes 786440 | tf_op jit(solution)/shard_map/ppermute | solution.py:432
  24.2 47.2 %collective-permute-start.5 = (f32[16,4096]{1,0:T(8,128)}, f32[16,4096]{1,0:T(8,128)}, u32[]{:S(2)}, u32[]{:S(2)}) collective-permute-start(f32[16,4096]{1,0:T(8,128)} %get-tuple-element.71), channel_id=1, source_target_pairs={{0,64},{32,96},{64,128},{96,160},{128,192},{160,224},{192,0},{224,... | collective-permute-start | bytes 786440 | tf_op jit(solution)/shard_map/ppermute | solution.py:432
  27.5 46.7 %collective-permute-start.6 = (f32[16,4096]{1,0:T(8,128)}, f32[16,4096]{1,0:T(8,128)}, u32[]{:S(2)}, u32[]{:S(2)}) collective-permute-start(f32[16,4096]{1,0:T(8,128)} %get-tuple-element.70), channel_id=1, source_target_pairs={{0,96},{32,128},{64,160},{96,192},{128,224},{160,0},{192,32},{224,... | collective-permute-start | bytes 786440 | tf_op jit(solution)/shard_map/ppermute | solution.py:432
  32.1 4.8 %copy-start.2 = (f32[256,32]{0,1:T(8,128)}, f32[256,32]{0,1:T(8,128)S(1)}, u32[]{:S(2)}) copy-start(f32[256,32]{0,1:T(8,128)S(1)} %reshape.917) | copy-start | bytes 98308
  36.9 7.1 %copy-start.4 = (f32[8,16,8,512]{3,2,1,0:T(8,128)S(1)}, f32[8,16,8,512]{3,2,1,0:T(8,128)}, u32[]{:S(2)}) copy-start(f32[8,16,8,512]{3,2,1,0:T(8,128)} %get-tuple-element.120) | copy-start | bytes 6291460
  39.6 8.2 %collective-permute-start.2 = (f32[5,4,130,1]{2,0,3,1:T(8,128)S(1)}, f32[5,4,130,1]{2,0,3,1:T(8,128)S(1)}, u32[]{:S(2)}, u32[]{:S(2)}) collective-permute-start(f32[5,4,130,1]{2,0,3,1:T(8,128)S(1)} %copy.148), channel_id=1, source_target_pairs={{0,1},{1,2},{2,3},{3,0},{4,5},{5,6},{6,7},{7,4},{8,9},{9,10},{10,1... | collective-permute-start | bytes 31208 | tf_op jit(solution)/shard_map/ppermute | solution.py:27
  42.2 6.6 %collective-permute-start.3 = (f32[5,4,130,1]{2,0,3,1:T(8,128)S(1)}, f32[5,4,130,1]{2,0,3,1:T(8,128)S(1)}, u32[]{:S(2)}, u32[]{:S(2)}) collective-permute-start(f32[5,4,130,1]{2,0,3,1:T(8,128)S(1)} %copy.149), channel_id=1, source_target_pairs={{1,0},{2,1},{3,2},{0,3},{5,4},{6,5},{7,6},{4,7},{9,8},{10,9},{11,1... | collective-permute-start | bytes 31208 | tf_op jit(solution)/shard_map/ppermute | solution.py:30
  47.8 28.0 %collective-permute-start.7 = (f32[16,4096]{1,0:T(8,128)}, f32[16,4096]{1,0:T(8,128)}, u32[]{:S(2)}, u32[]{:S(2)}) collective-permute-start(f32[16,4096]{1,0:T(8,128)} %get-tuple-element.69), channel_id=1, source_target_pairs={{0,128},{32,160},{64,192},{96,224},{128,0},{160,32},{192,64},{224,... | collective-permute-start | bytes 786440 | tf_op jit(solution)/shard_map/ppermute | solution.py:432
  48.9 34.5 %collective-permute-start.8 = (f32[16,4096]{1,0:T(8,128)}, f32[16,4096]{1,0:T(8,128)}, u32[]{:S(2)}, u32[]{:S(2)}) collective-permute-start(f32[16,4096]{1,0:T(8,128)} %get-tuple-element.68), channel_id=1, source_target_pairs={{0,160},{32,192},{64,224},{96,0},{128,32},{160,64},{192,96},{224,1... | collective-permute-start | bytes 786440 | tf_op jit(solution)/shard_map/ppermute | solution.py:432
  66.1 1.0 copy-start.8
  66.2 5.3 %copy-start.7 = (f32[16,4096]{1,0:T(8,128)S(1)}, f32[16,4096]{1,0:T(8,128)}, u32[]{:S(2)}) copy-start(f32[16,4096]{1,0:T(8,128)} %get-tuple-element.66) | copy-start | bytes 786436
  67.1 24.1 %collective-permute-start.9 = (f32[16,4096]{1,0:T(8,128)S(1)}, f32[16,4096]{1,0:T(8,128)S(1)}, u32[]{:S(2)}, u32[]{:S(2)}) collective-permute-start(f32[16,4096]{1,0:T(8,128)S(1)} %copy-done.8), channel_id=1, source_target_pairs={{0,192},{32,224},{64,0},{96,32},{128,64},{160,96},{192,128},{224,1... | collective-permute-start | bytes 786440 | tf_op jit(solution)/shard_map/ppermute | solution.py:432
  71.4 23.5 %collective-permute-start.10 = (f32[16,4096]{1,0:T(8,128)S(1)}, f32[16,4096]{1,0:T(8,128)S(1)}, u32[]{:S(2)}, u32[]{:S(2)}) collective-permute-start(f32[16,4096]{1,0:T(8,128)S(1)} %copy-done.7), channel_id=1, source_target_pairs={{0,224},{32,0},{64,32},{96,64},{128,96},{160,128},{192,160},{224,1... | collective-permute-start | bytes 786440 | tf_op jit(solution)/shard_map/ppermute | solution.py:432
  203.4 2.4 %copy-start.5 = (f32[8,8,4608]{2,1,0:T(8,128)S(1)}, f32[8,8,4608]{2,1,0:T(8,128)}, u32[]{:S(2)}) copy-start(f32[8,8,4608]{2,1,0:T(8,128)} %get-tuple-element.36) | copy-start | bytes 3538948
  210.1 2.5 %copy-start.1 = (f32[128,512]{1,0:T(8,128)S(1)}, f32[128,512]{1,0:T(8,128)}, u32[]{:S(2)}) copy-start(f32[128,512]{1,0:T(8,128)} %param.12) | copy-start | bytes 786436

commit v6 on v3

--- a/solution.py
+++ b/solution.py
@@ -100,6 +100,14 @@
     analysed = jnp.einsum("tc,ftn->fcn", table, forces, precision=highest) * (2.0 / table.shape[0])
     drag_rate = drag_row * jnp.mean(magnitude, axis=0)
     return (analysed, drag_rate)
+
+
+def height_result(residual_height, angular):
+    shaped = residual_height.reshape((residual_height.shape[0] // 2, 2) + residual_height.shape[1:])
+    cos_part = shaped[:, 0]
+    sin_part = shaped[:, 1]
+    moved = jnp.stack([-sin_part / angular, cos_part / angular], axis=1)
+    return moved.reshape(residual_height.shape)
 
 
 def precondition(residual, angular, rotation, drag_rate):
@@ -431,8 +439,10 @@
     linear_part = linear_residual(
         extended, tile_rows, tile_cols, angular_local[:, None, None], rotation[:, None]
     )
-    later = lax.optimization_barrier((payloads[1], linear_part))
+    height_out = height_result(linear_part[0] * wet_cells, angular_local[:, None, None])
+    later = lax.optimization_barrier((payloads[1], linear_part, height_out))
     linear_part = later[1]
+    height_out = later[2]
     shape_piece = (groups, pieces, piece_rows, tile_cols)
     linear_part = linear_part.reshape(3, local_coefs, *shape_piece)
     wet_piece = wet_cells.reshape(shape_piece)
@@ -454,9 +464,10 @@
                 angular_local[:, None, None, None],
                 rotation_piece[:, piece],
                 drag_rate,
-            )
+            )[1:]
         )
-    return jnp.stack(results, axis=3).reshape(3, local_coefs, tile_rows, tile_cols)
+    moving = jnp.stack(results, axis=3).reshape(2, local_coefs, tile_rows, tile_cols)
+    return jnp.concatenate([height_out[None], moving], axis=0)
 
 
 def solution(mesh):

time: 191 us -> 192 us (level)
  other arithmetic: 25.1 us -> 28.7 us
  waiting for transfers between devices: 23 us -> 21 us
    concatenate x0 -> x1, other arithmetic: none -> 2 us  [local(): return jnp.concatenate([height_out[None], moving], axis=0)]
    another operation x2 -> x1, local copies, waits for them, and re-layouts: 2.12 us -> 0.17 us  [local(): jnp.stack(results, axis=3).reshape(2, local_coefs, tile_rows, tile_cols)]
    all_to_all x1, waiting for transfers between devices: 23 us -> 21 us  [local(): lax.all_to_all(payloads[0], 'freq', split_axis=0, concat_axis=0, tiled=True)]
    unnamed x36 -> x38, local copies, waits for them, and re-layouts: 5.84 us -> 6.76 us
  transfers between devices with their start and end apart: 5 -> 5, of which waited for: 1 -> 1; matrix products, arithmetic and copies ran while one was open for 16% -> 17% of each run, Pallas kernels for 0% -> 0%
where the time goes in v6:
time: 192 us; the launch traced here: 191 us
  Pallas kernels  104 us (54%)
  other arithmetic  28.7 us (15%)
  waiting for transfers between devices  21 us (11%)
  local copies, waits for them, and re-layouts  20.8 us (11%)
  starting transfers between devices  16.2 us (8%)
    pallas_call x1, Pallas kernels, exchange_friction(): pl.pallas_call(functools.partial(exchange_kernel, groups, width), in_spec...  104 us
    all_to_all x1, waiting for transfers between devices, local(): lax.all_to_all(payloads[0], 'freq', split_axis=0, concat_axis=0, tiled=True)  21 us
    all_to_all x1, starting transfers between devices, local(): lax.all_to_all(payloads[0], 'freq', split_axis=0, concat_axis=0, tiled=True)  8.47 us
    unnamed x38, local copies, waits for them, and re-layouts  6.76 us
    mul x1, other arithmetic, local(): extended = extended * rim_keep[:, None]  5.92 us
    ppermute x2, starting transfers between devices, extended_2(): lax.ppermute(lax.slice_in_dim(block, 0, width, axis=dim), axis, backward)  5.3 us
    unnamed x9, other arithmetic  4.33 us
  transfers between devices with their start and end apart: 5, of which 1 were waited for; matrix products, arithmetic and copies ran while one was open for 17% of the time, Pallas kernels for 0%

profile of v6, /device:TPU:8, one launch (start us, length us, event | category | flops | bytes accessed | tf_op | source)
XLA Modules:
  0.0 191.3 jit_solution(11728462652849192814)
XLA Ops:
  0.0 1.0 convert_element_type.53
  1.0 1.3 multiply_dynamic-update-slice_fusion.2
  2.4 1.4 constant_dynamic-update-slice_fusion.1
  3.8 1.4 constant_dynamic-update-slice_fusion
  5.5 2.3 %copy-done.2 = f32[5,4,128,512]{3,2,1,0:T(8,128)} copy-done((f32[5,4,128,512]{3,2,1,0:T(8,128)}, f32[5,4,128,512]{3,2,1,0:T(8,128)S(1)}, u32[]{:S(2)}) %copy-start.2) | copy-done | bytes 5242904
  7.9 2.4 %collective-permute-start = (f32[5,4,1,512]{3,2,1,0:T(1,128)S(1)}, f32[5,4,1,512]{3,2,1,0:T(1,128)S(1)}, u32[]{:S(2)}, u32[]{:S(2)}) collective-permute-start(f32[5,4,1,512]{3,2,1,0:T(1,128)S(1)} %get-tuple-element.66), channel_id=1, source_target_pairs={{0,4},{4,8},{8,12},{12,16},{16,20},{20,24},{24,28},{28,0},{1,5},{5... | collective-permute-start | bytes 122888 | tf_op jit(solution)/shard_map/ppermute | solution.py:27
  10.3 3.3 %collective-permute-start.1 = (f32[5,4,1,512]{3,2,1,0:T(1,128)S(1)}, f32[5,4,1,512]{3,2,1,0:T(1,128)}, u32[]{:S(2)}, u32[]{:S(2)}) collective-permute-start(f32[5,4,1,512]{3,2,1,0:T(1,128)S(1)} %get-tuple-element.67), channel_id=1, source_target_pairs={{4,0},{8,4},{12,8},{16,12},{20,16},{24,20},{28,24},{0,28},{5,1},{9... | collective-permute-start | bytes 122888 | tf_op jit(solution)/shard_map/ppermute | solution.py:30
  13.6 0.6 pad_maximum_fusion
  14.2 1.8 fusion.56
  16.0 0.2 copy.174
  16.2 1.6 reshape.882
  17.8 8.5 %all-to-all-start = ((f32[8,16,4096]{2,1,0:T(8,128)}), f32[8,16,4096]{2,1,0:T(8,128)}, u32[]{:S(2)}, u32[]{:S(2)}) async-start(f32[8,16,4096]{2,1,0:T(8,128)} %reshape.882), calls=%async_computation | async-start | bytes 4194304 | tf_op jit(solution)/shard_map/all_to_all | solution.py:425
  26.3 0.6 fusion.48
  26.9 0.6 slice_bitcast_fusion.17
  27.8 0.7 slice_bitcast_fusion.15
  28.5 0.6 constant_dynamic-slice_fusion
  29.1 0.5 convert_multiply_fusion
  29.7 2.3 %pad_maximum_fusion.6 = (f32[5,4,130,1]{3,2,1,0:T(8,128)S(1)}, f32[5,4,130,1]{3,2,1,0:T(8,128)S(1)}) fusion(f32[5,4,1,512]{3,2,1,0:T(1,128)} %collective-permute-done.1, f32[5,4,128,512]{3,2,1,0:T(8,128)} %copy-done.2, f32[5,4,1,512]{3,2,1,0:T(1,128)S(1)} %collective-permute-done), kind=kLoop, calls=%fused_computation.15 | loop fusion | flops 10400 | bytes 5345600 | tf_op jit(solution)/shard_map/slice | solution.py:28
  32.0 1.2 copy.126
  33.3 1.2 copy.127
  34.5 2.0 %collective-permute-start.3 = (f32[5,4,130,1]{2,0,3,1:T(8,128)S(1)}, f32[5,4,130,1]{2,0,3,1:T(8,128)S(1)}, u32[]{:S(2)}, u32[]{:S(2)}) collective-permute-start(f32[5,4,130,1]{2,0,3,1:T(8,128)S(1)} %copy.127), channel_id=1, source_target_pairs={{1,0},{2,1},{3,2},{0,3},{5,4},{6,5},{7,6},{4,7},{9,8},{10,9},{11,1... | collective-permute-start | bytes 31208 | tf_op jit(solution)/shard_map/ppermute | solution.py:30
  36.5 1.8 copy.175
  38.3 1.5 reshape.874.second_ref
  39.8 0.8 copy.132.stacked_ref
  40.6 0.7 reshape.883.drag_ref
  41.3 0.5 copy.128
  41.8 0.5 copy.129
  42.3 5.9 %maximum_multiply_fusion = f32[5,4,130,514]{3,2,1,0:T(8,128)S(1)} fusion(f32[5,4,130,1]{3,2,1,0:T(8,128)S(1)} %copy.129, f32[5,4,1,512]{3,2,1,0:T(1,128)} %collective-permute-done.1, f32[5,4,128,512]{3,2,1,0:T(8,128)} %copy-done.2, f32[5,4,1,512]{3,2,1,0:T(1,128)S(1)} %collective-permute-done, f32[5,4,130,1]{3,2,1,0:T(8,128)S(1)} %copy.128, ...), kind=kLoop, calls=%fused_computation | loop fusion | flops 6682000 | bytes 10691720 | tf_op jit(solution)/shard_map/mul | solution.py:431
  48.2 0.4 slice.276
  48.9 1.8 fusion.54
  50.7 0.7 subtract_multiply_fusion
  51.4 0.5 fusion.13
  51.9 1.1 pad_maximum_fusion.12
  53.1 2.7 %fusion.7 = (f32[1,4,128,512]{3,2,1,0:T(8,128)S(1)}, f32[1,4,128,512]{3,2,1,0:T(8,128)S(1)}) fusion(f32[5,4,130,514]{3,2,1,0:T(8,128)S(1)} %maximum_multiply_fusion, f32[128]{0:T(128)S(1)} %add_multiply_fusion, f32[1,4,128,512]{3,2,1,0:T(8,128)S(1)} %bitcast.319, f32[1,4,128,512]{3,2,1,0:T(8,128)S(1)} %bitcast.317), kind=kLoop, calls=%fused_computation.26 | loop fusion | flops 4718592 | bytes 15729152 | tf_op jit(solution)/shard_map/add | solution.py:77
  55.8 0.3 pad_maximum_fusion.1
  56.1 21.0 %all-to-all-done.first_ref = f32[8,16,4096]{2,1,0:T(8,128)} async-done(((f32[8,16,4096]{2,1,0:T(8,128)}), f32[8,16,4096]{2,1,0:T(8,128)}, u32[]{:S(2)}, u32[]{:S(2)}) %all-to-all-start) | async-done | bytes 2097184 | tf_op jit(solution)/shard_map/all_to_all | solution.py:425
  77.1 104.0 %shard_map.55 = (f32[8,8,4608]{2,1,0:T(8,128)}, f32[8,8,4608]{2,1,0:T(8,128)}) custom-call(bf16[256,192]{1,0:T(8,128)(2,1)} %copy.132.stacked_ref, f32[32,256]{1,0:T(8,128)} %bitcast.328, f32[8,16,4096]{2,1,0:T(8,128)} %all-to-all-done.first_ref, f32[8,16,4096]{2,1,0:T(8,128)} %reshape.874.second_ref, f32[2,1,4096]{2,1,0:T(1,128)} %reshape.883.drag_ref), custom_call_target="tpu_custom_call" | custom-call | tf_op jit(solution)/shard_map/pallas_call | solution.py:378
  181.2 1.4 slice.250
  182.6 0.9 slice_add_fusion.7
  183.7 0.6 copy.169
  184.4 0.6 copy.168
  185.2 0.7 fusion.3
  185.9 0.5 multiply_subtract_fusion.2
  186.5 0.4 multiply_subtract_fusion.5
  186.9 0.4 add_negate_fusion.3
  187.8 0.2 pad_maximum_fusion.3
  188.3 1.0 copy-done.3
  189.3 2.0 %pad_maximum_fusion.2 = f32[3,4,128,512]{3,2,1,0:T(8,128)} fusion(f32[2,4,128,512]{3,2,1,0:T(8,128)S(1)} %bitcast.304, f32[1,4,128,512]{3,2,1,0:T(8,128)S(1)} %bitcast.325), kind=kLoop, calls=%fused_computation.3 | loop fusion | flops 786432 | bytes 6291456 | tf_op jit(solution)/shard_map/concatenate | solution.py:470
  (72 shorter events, 2.3 us)
Async XLA Ops:
  0.0 28.5 %copy-start = (f32[128,512]{1,0:T(8,128)S(1)}, f32[128,512]{1,0:T(8,128)}, u32[]{:S(2)}) copy-start(f32[128,512]{1,0:T(8,128)} %param.12) | copy-start | bytes 786436
  2.4 2.9 %copy-start.7 = (f32[128,512]{1,0:T(8,128)S(1)}, f32[128,512]{1,0:T(8,128)}, u32[]{:S(2)}) copy-start(f32[128,512]{1,0:T(8,128)} %param.11) | copy-start | bytes 786436
  5.2 8.4 %copy-start.5 = (f32[2,4,128,512]{3,2,1,0:T(8,128)S(1)}, f32[2,4,128,512]{3,2,1,0:T(8,128)}, u32[]{:S(2)}) copy-start(f32[2,4,128,512]{3,2,1,0:T(8,128)} %param.10) | copy-start | bytes 6291460
  5.5 2.3 %copy-start.2 = (f32[5,4,128,512]{3,2,1,0:T(8,128)}, f32[5,4,128,512]{3,2,1,0:T(8,128)S(1)}, u32[]{:S(2)}) copy-start(f32[5,4,128,512]{3,2,1,0:T(8,128)S(1)} %multiply_dynamic-update-slice_fusion) | copy-start | bytes 15728644
  7.9 21.8 %collective-permute-start = (f32[5,4,1,512]{3,2,1,0:T(1,128)S(1)}, f32[5,4,1,512]{3,2,1,0:T(1,128)S(1)}, u32[]{:S(2)}, u32[]{:S(2)}) collective-permute-start(f32[5,4,1,512]{3,2,1,0:T(1,128)S(1)} %get-tuple-element.66), channel_id=1, source_target_pairs={{0,4},{4,8},{8,12},{12,16},{16,20},{20,24},{24,28},{28,0},{1,5},{5... | collective-permute-start | bytes 122888 | tf_op jit(solution)/shard_map/ppermute | solution.py:27
  10.3 19.4 %collective-permute-start.1 = (f32[5,4,1,512]{3,2,1,0:T(1,128)S(1)}, f32[5,4,1,512]{3,2,1,0:T(1,128)}, u32[]{:S(2)}, u32[]{:S(2)}) collective-permute-start(f32[5,4,1,512]{3,2,1,0:T(1,128)S(1)} %get-tuple-element.67), channel_id=1, source_target_pairs={{4,0},{8,4},{12,8},{16,12},{20,16},{24,20},{28,24},{0,28},{5,1},{9... | collective-permute-start | bytes 122888 | tf_op jit(solution)/shard_map/ppermute | solution.py:30
  17.8 59.3 %all-to-all-start = ((f32[8,16,4096]{2,1,0:T(8,128)}), f32[8,16,4096]{2,1,0:T(8,128)}, u32[]{:S(2)}, u32[]{:S(2)}) async-start(f32[8,16,4096]{2,1,0:T(8,128)} %reshape.882), calls=%async_computation | async-start | bytes 4194304 | tf_op jit(solution)/shard_map/all_to_all | solution.py:425
  27.7 4.3 %copy-start.4 = (f32[256,32]{0,1:T(8,128)}, f32[256,32]{0,1:T(8,128)S(1)}, u32[]{:S(2)}) copy-start(f32[256,32]{0,1:T(8,128)S(1)} %reshape.881) | copy-start | bytes 98308
  27.8 1.8 copy-start.9
  29.6 21.7 %copy-start.14 = (f32[2]{0:T(128)}, f32[2]{0:T(128)S(1)}, u32[]{:S(2)}) copy-start(f32[2]{0:T(128)S(1)} %get-tuple-element.118) | copy-start | bytes 28
  33.2 8.1 %collective-permute-start.2 = (f32[5,4,130,1]{2,0,3,1:T(8,128)S(1)}, f32[5,4,130,1]{2,0,3,1:T(8,128)S(1)}, u32[]{:S(2)}, u32[]{:S(2)}) collective-permute-start(f32[5,4,130,1]{2,0,3,1:T(8,128)S(1)} %copy.126), channel_id=1, source_target_pairs={{0,1},{1,2},{2,3},{3,0},{4,5},{5,6},{6,7},{7,4},{8,9},{9,10},{10,1... | collective-permute-start | bytes 31208 | tf_op jit(solution)/shard_map/ppermute | solution.py:27
  34.5 7.3 %collective-permute-start.3 = (f32[5,4,130,1]{2,0,3,1:T(8,128)S(1)}, f32[5,4,130,1]{2,0,3,1:T(8,128)S(1)}, u32[]{:S(2)}, u32[]{:S(2)}) collective-permute-start(f32[5,4,130,1]{2,0,3,1:T(8,128)S(1)} %copy.127), channel_id=1, source_target_pairs={{1,0},{2,1},{3,2},{0,3},{5,4},{6,5},{7,6},{4,7},{9,8},{10,9},{11,1... | collective-permute-start | bytes 31208 | tf_op jit(solution)/shard_map/ppermute | solution.py:30
  38.3 1.5 copy-start.10
  38.3 2.3 %copy-start.11 = (f32[16,512]{1,0:T(8,128)S(1)}, f32[16,512]{1,0:T(8,128)}, u32[]{:S(2)}) copy-start(f32[16,512]{1,0:T(8,128)} %constant_dynamic-slice_fusion) | copy-start | bytes 98308
  181.2 2.4 %copy-start.6 = (f32[8,8,4608]{2,1,0:T(8,128)S(1)}, f32[8,8,4608]{2,1,0:T(8,128)}, u32[]{:S(2)}) copy-start(f32[8,8,4608]{2,1,0:T(8,128)} %get-tuple-element.38) | copy-start | bytes 3538948
  184.3 0.9 copy-start.8
  185.2 0.7 copy-start.12
  185.2 0.7 copy-start.13
  185.2 0.7 copy-start.15
  185.2 0.7 copy-start.16
  188.1 1.2 copy-start.3
  188.3 3.0 %copy-start.1 = (f32[128,512]{1,0:T(8,128)S(1)}, f32[128,512]{1,0:T(8,128)}, u32[]{:S(2)}) copy-start(f32[128,512]{1,0:T(8,128)} %param.12) | copy-start | bytes 786436

commit v7 on v3

--- a/solution.py
+++ b/solution.py
@@ -259,8 +259,10 @@
     first_ref,
     second_ref,
     drag_ref,
-    back_first_ref,
-    back_second_ref,
+    friction_first_ref,
+    friction_second_ref,
+    rate_first_ref,
+    rate_second_ref,
     arrived,
     results,
     landed,
@@ -350,8 +352,10 @@
     sending[2][1].wait()
     wait_arrivals(1, lambda g: results.at[0, g], lambda g: landed.at[0, g])
     wait_arrivals(2, lambda g: results.at[1, g], lambda g: landed.at[1, g])
-    back_first_ref[...] = landed[0]
-    back_second_ref[...] = landed[1]
+    friction_first_ref[...] = landed[0, :, :, 0:cells]
+    friction_second_ref[...] = landed[1, :, :, 0:cells]
+    rate_first_ref[...] = landed[0, :, :, cells:]
+    rate_second_ref[...] = landed[1, :, :, cells:]
 
 
 def exchange_friction(first, second, drag_band, table, width):
@@ -370,8 +374,9 @@
     return pl.pallas_call(
         functools.partial(exchange_kernel, groups, width),
         in_specs=[vmem] * 5,
-        out_specs=[vmem, vmem],
-        out_shape=[jax.ShapeDtypeStruct(returned, jnp.float32)] * 2,
+        out_specs=[vmem] * 4,
+        out_shape=[jax.ShapeDtypeStruct((groups, 2 * per, cells), jnp.float32)] * 2
+        + [jax.ShapeDtypeStruct((groups, 2 * per, cells // (2 * per)), jnp.float32)] * 2,
         scratch_shapes=[
             pltpu.VMEM(first.shape, jnp.float32),
             pltpu.VMEM((2,) + returned, jnp.float32),
@@ -440,10 +445,9 @@
     backs = exchange_friction(sent[0], later[0], drag_band, table, tile_cols)
     results = []
     for piece in range(pieces):
-        back = backs[piece]
-        friction = back[:, :, :piece_cells].reshape(groups, 2, local_coefs, piece_rows, tile_cols)
+        friction = backs[piece].reshape(groups, 2, local_coefs, piece_rows, tile_cols)
         friction = jnp.moveaxis(friction, 0, 2)
-        drag_rate = back[:, :, piece_cells:].reshape(groups, piece_rows, tile_cols)
+        drag_rate = backs[pieces + piece].reshape(groups, piece_rows, tile_cols)
         linear_piece = linear_part[:, :, :, piece]
         residual = (
             linear_piece + jnp.concatenate([jnp.zeros_like(friction[:1]), friction], axis=0)

time: 191 us -> 190 us (level)
    unnamed x36 -> x40, local copies, waits for them, and re-layouts: 5.84 us -> 7.1 us
where the time goes in v7:
time: 190 us; the launch traced here: 189 us
  Pallas kernels  104 us (55%)
  other arithmetic  24.1 us (13%)
  waiting for transfers between devices  23 us (12%)
  local copies, waits for them, and re-layouts  21.7 us (11%)
  starting transfers between devices  16 us (8%)
    pallas_call x1, Pallas kernels, exchange_friction(): pl.pallas_call(functools.partial(exchange_kernel, groups, width), in_spec...  104 us
    all_to_all x1, waiting for transfers between devices, local(): lax.all_to_all(payloads[0], 'freq', split_axis=0, concat_axis=0, tiled=True)  23 us
    all_to_all x1, starting transfers between devices, local(): lax.all_to_all(payloads[0], 'freq', split_axis=0, concat_axis=0, tiled=True)  8.47 us
    unnamed x40, local copies, waits for them, and re-layouts  7.1 us
    mul x1, other arithmetic, local(): extended = extended * rim_keep[:, None]  5.92 us
    ppermute x2, starting transfers between devices, extended_2(): lax.ppermute(lax.slice_in_dim(block, 0, width, axis=dim), axis, backward)  5.12 us
    unnamed x9, other arithmetic  4.33 us
  transfers between devices with their start and end apart: 5, of which 1 were waited for; matrix products, arithmetic and copies ran while one was open for 16% of the time, Pallas kernels for 0%

profile of v7, /device:TPU:8, one launch (start us, length us, event | category | flops | bytes accessed | tf_op | source)
XLA Modules:
  0.0 189.4 jit_solution(6832171733690522707)
XLA Ops:
  0.0 1.0 convert_element_type.53
  1.0 1.3 multiply_dynamic-update-slice_fusion.2
  2.4 1.4 constant_dynamic-update-slice_fusion.1
  3.8 1.4 constant_dynamic-update-slice_fusion
  5.2 0.1 multiply_dynamic-update-slice_fusion.1
  5.5 2.3 %copy-done.2 = f32[5,4,128,512]{3,2,1,0:T(8,128)} copy-done((f32[5,4,128,512]{3,2,1,0:T(8,128)}, f32[5,4,128,512]{3,2,1,0:T(8,128)S(1)}, u32[]{:S(2)}) %copy-start.2) | copy-done | bytes 5242904
  7.9 2.4 %collective-permute-start = (f32[5,4,1,512]{3,2,1,0:T(1,128)S(1)}, f32[5,4,1,512]{3,2,1,0:T(1,128)S(1)}, u32[]{:S(2)}, u32[]{:S(2)}) collective-permute-start(f32[5,4,1,512]{3,2,1,0:T(1,128)S(1)} %get-tuple-element.64), channel_id=1, source_target_pairs={{0,4},{4,8},{8,12},{12,16},{16,20},{20,24},{24,28},{28,0},{1,5},{5... | collective-permute-start | bytes 122888 | tf_op jit(solution)/shard_map/ppermute | solution.py:27
  10.3 3.3 %collective-permute-start.1 = (f32[5,4,1,512]{3,2,1,0:T(1,128)S(1)}, f32[5,4,1,512]{3,2,1,0:T(1,128)}, u32[]{:S(2)}, u32[]{:S(2)}) collective-permute-start(f32[5,4,1,512]{3,2,1,0:T(1,128)S(1)} %get-tuple-element.65), channel_id=1, source_target_pairs={{4,0},{8,4},{12,8},{16,12},{20,16},{24,20},{28,24},{0,28},{5,1},{9... | collective-permute-start | bytes 122888 | tf_op jit(solution)/shard_map/ppermute | solution.py:30
  13.6 0.6 pad_maximum_fusion
  14.2 1.8 fusion.51
  16.0 0.2 copy.172
  16.2 1.6 reshape.867
  17.8 8.5 %all-to-all-start = ((f32[8,16,4096]{2,1,0:T(8,128)}), f32[8,16,4096]{2,1,0:T(8,128)}, u32[]{:S(2)}, u32[]{:S(2)}) async-start(f32[8,16,4096]{2,1,0:T(8,128)} %reshape.867), calls=%async_computation | async-start | bytes 4194304 | tf_op jit(solution)/shard_map/all_to_all | solution.py:422
  26.3 0.6 fusion.44
  26.9 0.6 slice_bitcast_fusion.17
  27.5 0.2 fusion.41
  27.8 0.6 constant_dynamic-slice_fusion
  28.4 0.5 convert_multiply_fusion
  29.0 0.7 slice_bitcast_fusion.15
  29.7 2.3 %pad_maximum_fusion.7 = (f32[5,4,130,1]{3,2,1,0:T(8,128)S(1)}, f32[5,4,130,1]{3,2,1,0:T(8,128)S(1)}) fusion(f32[5,4,1,512]{3,2,1,0:T(1,128)} %collective-permute-done.1, f32[5,4,128,512]{3,2,1,0:T(8,128)} %copy-done.2, f32[5,4,1,512]{3,2,1,0:T(1,128)S(1)} %collective-permute-done), kind=kLoop, calls=%fused_computation.16 | loop fusion | flops 10400 | bytes 5345600 | tf_op jit(solution)/shard_map/slice | solution.py:28
  32.0 1.2 copy.124
  33.3 1.2 copy.125
  34.5 1.8 collective-permute-start.3
  36.3 1.8 copy.173
  38.1 1.7 reshape.860.second_ref
  39.9 0.8 copy.130.stacked_ref
  40.6 0.6 reshape.868.drag_ref
  41.3 0.5 copy.126
  41.8 0.5 copy.127
  42.3 5.9 %maximum_multiply_fusion = f32[5,4,130,514]{3,2,1,0:T(8,128)S(1)} fusion(f32[5,4,130,1]{3,2,1,0:T(8,128)S(1)} %copy.127, f32[5,4,1,512]{3,2,1,0:T(1,128)} %collective-permute-done.1, f32[5,4,128,512]{3,2,1,0:T(8,128)} %copy-done.2, f32[5,4,1,512]{3,2,1,0:T(1,128)S(1)} %collective-permute-done, f32[5,4,130,1]{3,2,1,0:T(8,128)S(1)} %copy.126, ...), kind=kLoop, calls=%fused_computation | loop fusion | flops 6682000 | bytes 10691720 | tf_op jit(solution)/shard_map/mul | solution.py:428
  48.2 0.4 slice.242
  48.6 0.2 slice_multiply_fusion.7
  48.9 1.8 slice_subtract_fusion.2
  50.7 0.3 slice_multiply_fusion.3
  51.1 2.7 %fusion.7 = (f32[1,4,128,512]{3,2,1,0:T(8,128)S(1)}, f32[1,4,128,512]{3,2,1,0:T(8,128)S(1)}) fusion(f32[5,4,130,514]{3,2,1,0:T(8,128)S(1)} %maximum_multiply_fusion, f32[128]{0:T(128)S(1)} %add_multiply_fusion, f32[1,4,128,512]{3,2,1,0:T(8,128)S(1)} %bitcast.304, f32[1,4,128,512]{3,2,1,0:T(8,128)S(1)} %bitcast.303), kind=kLoop, calls=%fused_computation.25 | loop fusion | flops 4718592 | bytes 15729152 | tf_op jit(solution)/shard_map/add | solution.py:77
  53.8 0.3 pad_maximum_fusion.1
  54.2 23.0 %all-to-all-done.first_ref = f32[8,16,4096]{2,1,0:T(8,128)} async-done(((f32[8,16,4096]{2,1,0:T(8,128)}), f32[8,16,4096]{2,1,0:T(8,128)}, u32[]{:S(2)}, u32[]{:S(2)}) %all-to-all-start) | async-done | bytes 2097184 | tf_op jit(solution)/shard_map/all_to_all | solution.py:422
  77.1 104.0 %shard_map.55 = (f32[8,8,4096]{2,1,0:T(8,128)}, f32[8,8,4096]{2,1,0:T(8,128)}, f32[8,8,512]{2,1,0:T(8,128)}, f32[8,8,512]{2,1,0:T(8,128)}) custom-call(bf16[256,192]{1,0:T(8,128)(2,1)} %copy.130.stacked_ref, f32[32,256]{1,0:T(8,128)} %bitcast.309, f32[8,16,4096]{2,1,0:T(8,128)} %all-to-all-done.first_ref, f32[8,16,4096]{2,1,0:T(8,128)} %reshape.860.second_ref, ...), custom_call_target="tpu_custom_call" | custom-call | tf_op jit(solution)/shard_map/pallas_call | solution.py:374
  181.1 1.9 %copy.167 = f32[8,8,8,512]{3,2,1,0:T(8,128)S(1)} copy(f32[8,8,8,512]{3,1,2,0:T(8,128)} %bitcast.311) | data formatting | bytes 2097152
  183.2 0.6 copy.166
  184.1 0.7 fusion.3
  184.9 0.5 multiply_subtract_fusion.2
  185.4 0.4 multiply_subtract_fusion.5
  185.8 0.4 add_negate_fusion.3
  186.3 0.2 pad_maximum_fusion.4
  186.5 0.1 copy.148
  186.9 0.5 pad_maximum_fusion.2
  187.4 2.0 %copy.149 = f32[3,4,8,2,8,512]{5,4,3,2,1,0:T(8,128)} copy(f32[3,4,8,2,8,512]{5,4,2,1,0,3:T(8,128)S(1)} %pad_maximum_fusion.2) | data formatting | bytes 6291456 | tf_op jit(solution)/shard_map/stack | solution.py:463
  (69 shorter events, 1.5 us)
Async XLA Ops:
  0.0 27.8 %copy-start = (f32[128,512]{1,0:T(8,128)S(1)}, f32[128,512]{1,0:T(8,128)}, u32[]{:S(2)}) copy-start(f32[128,512]{1,0:T(8,128)} %param.12) | copy-start | bytes 786436
  2.4 2.9 %copy-start.5 = (f32[128,512]{1,0:T(8,128)S(1)}, f32[128,512]{1,0:T(8,128)}, u32[]{:S(2)}) copy-start(f32[128,512]{1,0:T(8,128)} %param.11) | copy-start | bytes 786436
  5.2 8.4 %copy-start.4 = (f32[2,4,128,512]{3,2,1,0:T(8,128)S(1)}, f32[2,4,128,512]{3,2,1,0:T(8,128)}, u32[]{:S(2)}) copy-start(f32[2,4,128,512]{3,2,1,0:T(8,128)} %param.10) | copy-start | bytes 6291460
  5.5 2.3 %copy-start.2 = (f32[5,4,128,512]{3,2,1,0:T(8,128)}, f32[5,4,128,512]{3,2,1,0:T(8,128)S(1)}, u32[]{:S(2)}) copy-start(f32[5,4,128,512]{3,2,1,0:T(8,128)S(1)} %multiply_dynamic-update-slice_fusion) | copy-start | bytes 15728644
  7.9 21.8 %collective-permute-start = (f32[5,4,1,512]{3,2,1,0:T(1,128)S(1)}, f32[5,4,1,512]{3,2,1,0:T(1,128)S(1)}, u32[]{:S(2)}, u32[]{:S(2)}) collective-permute-start(f32[5,4,1,512]{3,2,1,0:T(1,128)S(1)} %get-tuple-element.64), channel_id=1, source_target_pairs={{0,4},{4,8},{8,12},{12,16},{16,20},{20,24},{24,28},{28,0},{1,5},{5... | collective-permute-start | bytes 122888 | tf_op jit(solution)/shard_map/ppermute | solution.py:27
  10.3 19.4 %collective-permute-start.1 = (f32[5,4,1,512]{3,2,1,0:T(1,128)S(1)}, f32[5,4,1,512]{3,2,1,0:T(1,128)}, u32[]{:S(2)}, u32[]{:S(2)}) collective-permute-start(f32[5,4,1,512]{3,2,1,0:T(1,128)S(1)} %get-tuple-element.65), channel_id=1, source_target_pairs={{4,0},{8,4},{12,8},{16,12},{20,16},{24,20},{28,24},{0,28},{5,1},{9... | collective-permute-start | bytes 122888 | tf_op jit(solution)/shard_map/ppermute | solution.py:30
  17.8 59.3 %all-to-all-start = ((f32[8,16,4096]{2,1,0:T(8,128)}), f32[8,16,4096]{2,1,0:T(8,128)}, u32[]{:S(2)}, u32[]{:S(2)}) async-start(f32[8,16,4096]{2,1,0:T(8,128)} %reshape.867), calls=%async_computation | async-start | bytes 4194304 | tf_op jit(solution)/shard_map/all_to_all | solution.py:422
  27.7 4.3 %copy-start.3 = (f32[256,32]{0,1:T(8,128)}, f32[256,32]{0,1:T(8,128)S(1)}, u32[]{:S(2)}) copy-start(f32[256,32]{0,1:T(8,128)S(1)} %reshape.866) | copy-start | bytes 98308
  28.9 21.7 %copy-start.15 = (f32[2]{0:T(128)}, f32[2]{0:T(128)S(1)}, u32[]{:S(2)}) copy-start(f32[2]{0:T(128)S(1)} %get-tuple-element.110) | copy-start | bytes 28
  29.0 0.7 copy-start.8
  33.2 8.1 %collective-permute-start.2 = (f32[5,4,130,1]{2,0,3,1:T(8,128)S(1)}, f32[5,4,130,1]{2,0,3,1:T(8,128)S(1)}, u32[]{:S(2)}, u32[]{:S(2)}) collective-permute-start(f32[5,4,130,1]{2,0,3,1:T(8,128)S(1)} %copy.124), channel_id=1, source_target_pairs={{0,1},{1,2},{2,3},{3,0},{4,5},{5,6},{6,7},{7,4},{8,9},{9,10},{10,1... | collective-permute-start | bytes 31208 | tf_op jit(solution)/shard_map/ppermute | solution.py:27
  34.5 7.3 %collective-permute-start.3 = (f32[5,4,130,1]{2,0,3,1:T(8,128)S(1)}, f32[5,4,130,1]{2,0,3,1:T(8,128)S(1)}, u32[]{:S(2)}, u32[]{:S(2)}) collective-permute-start(f32[5,4,130,1]{2,0,3,1:T(8,128)S(1)} %copy.125), channel_id=1, source_target_pairs={{1,0},{2,1},{3,2},{0,3},{5,4},{6,5},{7,6},{4,7},{9,8},{10,9},{11,1... | collective-permute-start | bytes 31208 | tf_op jit(solution)/shard_map/ppermute | solution.py:30
  38.1 1.7 copy-start.9
  38.1 2.5 %copy-start.10 = (f32[16,512]{1,0:T(8,128)S(1)}, f32[16,512]{1,0:T(8,128)}, u32[]{:S(2)}) copy-start(f32[16,512]{1,0:T(8,128)} %constant_dynamic-slice_fusion) | copy-start | bytes 98308
  181.1 2.1 %copy-start.6 = (f32[8,8,4096]{2,1,0:T(8,128)S(1)}, f32[8,8,4096]{2,1,0:T(8,128)}, u32[]{:S(2)}) copy-start(f32[8,8,4096]{2,1,0:T(8,128)} %get-tuple-element.37) | copy-start | bytes 3145732
  183.1 0.9 copy-start.12
  183.1 1.0 copy-start.11
  183.2 0.9 copy-start.7
  184.1 0.7 copy-start.13
  184.1 0.7 copy-start.14
  184.1 0.7 copy-start.16
  184.1 0.7 copy-start.17
  186.9 2.5 %copy-start.1 = (f32[128,512]{1,0:T(8,128)S(1)}, f32[128,512]{1,0:T(8,128)}, u32[]{:S(2)}) copy-start(f32[128,512]{1,0:T(8,128)} %param.12) | copy-start | bytes 786436

commit v8 on v7

--- a/solution.py
+++ b/solution.py
@@ -24,10 +24,13 @@
         forward = [(i, i + 1) for i in range(count - 1)]
         forward.append((count - 1, 0))
         backward = [(target, source) for source, target in forward]
+        sent = 128 if dim == block.ndim - 1 else width
         low = lax.ppermute(
-            lax.slice_in_dim(block, block.shape[dim] - width, None, axis=dim), axis, forward
+            lax.slice_in_dim(block, block.shape[dim] - sent, None, axis=dim), axis, forward
         )
-        high = lax.ppermute(lax.slice_in_dim(block, 0, width, axis=dim), axis, backward)
+        high = lax.ppermute(lax.slice_in_dim(block, 0, sent, axis=dim), axis, backward)
+        low = lax.slice_in_dim(low, sent - width, None, axis=dim)
+        high = lax.slice_in_dim(high, 0, width, axis=dim)
         block = jnp.concatenate([low, block, high], axis=dim)
     return block
 

time: 190 us -> 197 us (1.037)
  other arithmetic: 24.1 us -> 26.4 us
  Pallas kernels: 104 us -> 106 us
    ppermute x4, waiting for transfers between devices: 0.01 us -> 23.2 us  [the longest x2 23.2 us: extended_2(): lax.ppermute(lax.slice_in_dim(block, block.shape[dim] - sent, None, axis=...]
    all_to_all x1, waiting for transfers between devices: 23 us -> 0.01 us  [local(): lax.all_to_all(payloads[0], 'freq', split_axis=0, concat_axis=0, tiled=True)]
    unnamed x40 -> x28, local copies, waits for them, and re-layouts: 7.1 us -> 11.2 us
    another operation x1 -> x0, local copies, waits for them, and re-layouts: 1.97 us -> none  [local(): jnp.stack(results, axis=3).reshape(3, local_coefs, tile_rows, tile_cols)]
where the time goes in v8:
time: 197 us; the launch traced here: 195 us
  Pallas kernels  106 us (54%)
  other arithmetic  26.4 us (13%)
  local copies, waits for them, and re-layouts  23.2 us (12%)
  waiting for transfers between devices  23.2 us (12%)
  starting transfers between devices  15.9 us (8%)
    pallas_call x1, Pallas kernels, exchange_friction(): pl.pallas_call(functools.partial(exchange_kernel, groups, width), in_spec...  106 us
    ppermute x2, waiting for transfers between devices, extended_2(): lax.ppermute(lax.slice_in_dim(block, block.shape[dim] - sent, None, axis=...  23.2 us
    unnamed x28, local copies, waits for them, and re-layouts  11.2 us
    all_to_all x1, starting transfers between devices, local(): lax.all_to_all(payloads[0], 'freq', split_axis=0, concat_axis=0, tiled=True)  8.47 us
    mul x1, other arithmetic, local(): extended = extended * rim_keep[:, None]  6.11 us
    ppermute x2, starting transfers between devices, extended_2(): lax.ppermute(lax.slice_in_dim(block, 0, sent, axis=dim), axis, backward)  5.09 us
    reshape x2, local copies, waits for them, and re-layouts, local(): jnp.moveaxis(flows[:, :, piece], 1, 0)  4.34 us
    unnamed x9, other arithmetic  4.33 us
  transfers between devices with their start and end apart: 5, of which 1 were waited for; matrix products, arithmetic and copies ran while one was open for 16% of the time, Pallas kernels for 0%

profile of v8, /device:TPU:8, one launch (start us, length us, event | category | flops | bytes accessed | tf_op | source)
XLA Modules:
  0.0 195.0 jit_solution(16974155599129698383)
XLA Ops:
  0.0 1.0 convert_element_type.53
  1.0 1.3 multiply_dynamic-update-slice_fusion.2
  2.4 1.4 constant_dynamic-update-slice_fusion.1
  3.8 1.4 constant_dynamic-update-slice_fusion
  5.2 0.1 multiply_dynamic-update-slice_fusion.1
  5.4 0.1 multiply_dynamic-update-slice_fusion
  5.5 2.3 %copy-done.2 = f32[5,4,128,512]{3,2,1,0:T(8,128)} copy-done((f32[5,4,128,512]{3,2,1,0:T(8,128)}, f32[5,4,128,512]{3,2,1,0:T(8,128)S(1)}, u32[]{:S(2)}) %copy-start.2) | copy-done | bytes 5242904
  7.9 2.4 %collective-permute-start = (f32[5,4,1,512]{3,2,1,0:T(1,128)S(1)}, f32[5,4,1,512]{3,2,1,0:T(1,128)S(1)}, u32[]{:S(2)}, u32[]{:S(2)}) collective-permute-start(f32[5,4,1,512]{3,2,1,0:T(1,128)S(1)} %get-tuple-element.64), channel_id=1, source_target_pairs={{0,4},{4,8},{8,12},{12,16},{16,20},{20,24},{24,28},{28,0},{1,5},{5... | collective-permute-start | bytes 122888 | tf_op jit(solution)/shard_map/ppermute | solution.py:28
  10.3 3.3 %collective-permute-start.1 = (f32[5,4,1,512]{3,2,1,0:T(1,128)S(1)}, f32[5,4,1,512]{3,2,1,0:T(1,128)S(1)}, u32[]{:S(2)}, u32[]{:S(2)}) collective-permute-start(f32[5,4,1,512]{3,2,1,0:T(1,128)S(1)} %get-tuple-element.65), channel_id=1, source_target_pairs={{4,0},{8,4},{12,8},{16,12},{20,16},{24,20},{28,24},{0,28},{5,1},{9... | collective-permute-start | bytes 122888 | tf_op jit(solution)/shard_map/ppermute | solution.py:31
  13.6 0.6 pad_maximum_fusion
  14.2 1.8 fusion.51
  16.0 0.2 copy.72
  16.2 1.5 reshape.867
  17.8 8.5 %all-to-all-start = ((f32[8,16,4096]{2,1,0:T(8,128)}), f32[8,16,4096]{2,1,0:T(8,128)S(1)}, u32[]{:S(2)}, u32[]{:S(2)}) async-start(f32[8,16,4096]{2,1,0:T(8,128)} %reshape.867), calls=%async_computation | async-start | bytes 4194304 | tf_op jit(solution)/shard_map/all_to_all | solution.py:425
  26.3 0.2 fusion.41
  26.6 3.6 %pad_maximum_fusion.7 = (f32[5,4,130,128]{3,2,1,0:T(8,128)}, f32[5,4,130,128]{3,2,1,0:T(8,128)}) fusion(f32[5,4,1,512]{3,2,1,0:T(1,128)S(1)} %collective-permute-done.1, f32[5,4,128,512]{3,2,1,0:T(8,128)} %copy-done.2, f32[5,4,1,512]{3,2,1,0:T(1,128)S(1)} %collective-permute-done), kind=kLoop, calls=%fused_computation.16 | loop fusion | flops 1331200 | bytes 7987200 | tf_op jit(solution)/shard_map/slice | solution.py:29
  30.2 1.7 collective-permute-start.3
  32.1 3.1 %copy.73 = f32[16,8,1,8,512]{4,3,0,1,2:T(8,128)} copy(f32[16,8,1,8,512]{4,3,2,1,0:T(8,128)} %get-tuple-element.66) | data formatting | bytes 4194304
  35.2 2.8 %reshape.860.second_ref = f32[8,16,4096]{2,1,0:T(8,128)} reshape(f32[8,16,8,512]{3,2,1,0:T(8,128)} %bitcast.284) | data formatting | bytes 4194304 | tf_op jit(solution)/shard_map/reshape | solution.py:422
  38.0 0.8 copy.28.stacked_ref
  38.8 0.6 reshape.868.drag_ref
  39.5 23.2 %collective-permute-done.2 = f32[5,4,130,128]{3,2,1,0:T(8,128)} collective-permute-done((f32[5,4,130,128]{3,2,1,0:T(8,128)}, f32[5,4,130,128]{3,2,1,0:T(8,128)}, u32[]{:S(2)}, u32[]{:S(2)}) %collective-permute-start.2) | collective-permute-done | bytes 1331232 | tf_op jit(solution)/shard_map/ppermute | solution.py:28
  62.7 1.8 slice.250
  64.5 6.1 %maximum_multiply_fusion = f32[5,4,130,514]{3,2,1,0:T(8,128)S(1)} fusion(f32[5,4,130,1]{3,2,1,0:T(8,128)} %bitcast.280, f32[5,4,1,512]{3,2,1,0:T(1,128)S(1)} %collective-permute-done.1, f32[5,4,128,512]{3,2,1,0:T(8,128)} %copy-done.2, f32[5,4,1,512]{3,2,1,0:T(1,128)S(1)} %collective-permute-done, f32[5,4,130,1]{3,2,1,0:T(8,128)S(1)} %slice.250, ...), kind=kLoop, calls=%fused_computation | loop fusion | flops 6682000 | bytes 10691720 | tf_op jit(solution)/shard_map/mul | solution.py:431
  70.6 0.4 slice.252
  71.0 0.2 slice_multiply_fusion.7
  71.2 1.8 slice_subtract_fusion.2
  73.0 0.4 slice_multiply_fusion.3
  73.4 0.1 pad_maximum_fusion.10
  73.6 2.7 %fusion.7 = (f32[1,4,128,512]{3,2,1,0:T(8,128)S(1)}, f32[1,4,128,512]{3,2,1,0:T(8,128)S(1)}) fusion(f32[5,4,130,514]{3,2,1,0:T(8,128)S(1)} %maximum_multiply_fusion, f32[128]{0:T(128)S(1)} %add_multiply_fusion, f32[1,4,128,512]{3,2,1,0:T(8,128)S(1)} %bitcast.293, f32[1,4,128,512]{3,2,1,0:T(8,128)S(1)} %bitcast.292), kind=kLoop, calls=%fused_computation.25 | loop fusion | flops 4718592 | bytes 15729152 | tf_op jit(solution)/shard_map/add | solution.py:80
  76.3 0.6 pad_maximum_fusion.1
  76.8 1.9 fusion.52
  78.8 1.3 copy-done.3
  80.1 105.7 %shard_map.55 = (f32[8,8,4096]{2,1,0:T(8,128)}, f32[8,8,4096]{2,1,0:T(8,128)}, f32[8,8,512]{2,1,0:T(8,128)}, f32[8,8,512]{2,1,0:T(8,128)}) custom-call(bf16[256,192]{1,0:T(8,128)(2,1)} %copy.28.stacked_ref, f32[32,256]{1,0:T(8,128)} %bitcast.298, f32[8,16,4096]{2,1,0:T(8,128)} %copy-done.3, f32[8,16,4096]{2,1,0:T(8,128)} %reshape.860.second_ref, ...), custom_call_target="tpu_custom_call" | custom-call | tf_op jit(solution)/shard_map/pallas_call | solution.py:377
  185.9 1.9 copy.58
  187.9 0.6 copy.59
  188.5 0.7 copy-done.5
  189.2 0.4 fusion.3
  189.6 0.4 multiply_subtract_fusion.5
  190.1 0.9 copy-done.4
  191.0 0.4 fusion.1
  191.3 0.4 multiply_subtract_fusion.2
  191.8 0.4 add_negate_fusion.3
  192.3 0.2 pad_maximum_fusion.3
  192.4 0.1 copy.35
  192.7 0.2 pad_maximum_fusion.4
  192.9 0.1 copy.42
  193.1 2.0 %pad_maximum_fusion.2 = f32[3,4,8,2,8,512]{5,4,3,2,1,0:T(8,128)} fusion(f32[3,4,8,1,8,512]{5,4,3,2,1,0:T(8,128)S(1)} %bitcast.289, f32[3,4,8,1,8,512]{5,4,3,2,1,0:T(8,128)S(1)} %bitcast.288), kind=kLoop, calls=%fused_computation.3 | loop fusion | flops 786432 | bytes 6291456 | tf_op jit(solution)/shard_map/stack | solution.py:466
  (54 shorter events, 0.8 us)
Async XLA Ops:
  0.0 26.6 %copy-start = (f32[128,512]{1,0:T(8,128)S(1)}, f32[128,512]{1,0:T(8,128)}, u32[]{:S(2)}) copy-start(f32[128,512]{1,0:T(8,128)} %param.12) | copy-start | bytes 786436
  3.8 1.5 copy-start.8
  5.2 8.4 %copy-start.7 = (f32[2,4,128,512]{3,2,1,0:T(8,128)S(1)}, f32[2,4,128,512]{3,2,1,0:T(8,128)}, u32[]{:S(2)}) copy-start(f32[2,4,128,512]{3,2,1,0:T(8,128)} %param.10) | copy-start | bytes 6291460
  5.5 2.3 %copy-start.2 = (f32[5,4,128,512]{3,2,1,0:T(8,128)}, f32[5,4,128,512]{3,2,1,0:T(8,128)S(1)}, u32[]{:S(2)}) copy-start(f32[5,4,128,512]{3,2,1,0:T(8,128)S(1)} %multiply_dynamic-update-slice_fusion) | copy-start | bytes 15728644
  7.9 18.7 %collective-permute-start = (f32[5,4,1,512]{3,2,1,0:T(1,128)S(1)}, f32[5,4,1,512]{3,2,1,0:T(1,128)S(1)}, u32[]{:S(2)}, u32[]{:S(2)}) collective-permute-start(f32[5,4,1,512]{3,2,1,0:T(1,128)S(1)} %get-tuple-element.64), channel_id=1, source_target_pairs={{0,4},{4,8},{8,12},{12,16},{16,20},{20,24},{24,28},{28,0},{1,5},{5... | collective-permute-start | bytes 122888 | tf_op jit(solution)/shard_map/ppermute | solution.py:28
  10.3 16.4 %collective-permute-start.1 = (f32[5,4,1,512]{3,2,1,0:T(1,128)S(1)}, f32[5,4,1,512]{3,2,1,0:T(1,128)S(1)}, u32[]{:S(2)}, u32[]{:S(2)}) collective-permute-start(f32[5,4,1,512]{3,2,1,0:T(1,128)S(1)} %get-tuple-element.65), channel_id=1, source_target_pairs={{4,0},{8,4},{12,8},{16,12},{20,16},{24,20},{28,24},{0,28},{5,1},{9... | collective-permute-start | bytes 122888 | tf_op jit(solution)/shard_map/ppermute | solution.py:31
  17.8 61.0 %all-to-all-start = ((f32[8,16,4096]{2,1,0:T(8,128)}), f32[8,16,4096]{2,1,0:T(8,128)S(1)}, u32[]{:S(2)}, u32[]{:S(2)}) async-start(f32[8,16,4096]{2,1,0:T(8,128)} %reshape.867), calls=%async_computation | async-start | bytes 4194304 | tf_op jit(solution)/shard_map/all_to_all | solution.py:425
  26.5 5.5 %copy-start.6 = (f32[256,32]{0,1:T(8,128)}, f32[256,32]{0,1:T(8,128)S(1)}, u32[]{:S(2)}) copy-start(f32[256,32]{0,1:T(8,128)S(1)} %reshape.866) | copy-start | bytes 98308
  30.2 32.4 %collective-permute-start.2 = (f32[5,4,130,128]{3,2,1,0:T(8,128)}, f32[5,4,130,128]{3,2,1,0:T(8,128)}, u32[]{:S(2)}, u32[]{:S(2)}) collective-permute-start(f32[5,4,130,128]{3,2,1,0:T(8,128)} %get-tuple-element.62), channel_id=1, source_target_pairs={{0,1},{1,2},{2,3},{3,0},{4,5},{5,6},{6,7},{7,4},{8,9},{9,10},{10,1... | collective-permute-start | bytes 3993608 | tf_op jit(solution)/shard_map/ppermute | solution.py:28
  30.2 34.2 %collective-permute-start.3 = (f32[5,4,130,128]{3,2,1,0:T(8,128)}, f32[5,4,130,128]{3,2,1,0:T(8,128)}, u32[]{:S(2)}, u32[]{:S(2)}) collective-permute-start(f32[5,4,130,128]{3,2,1,0:T(8,128)} %get-tuple-element.63), channel_id=1, source_target_pairs={{1,0},{2,1},{3,2},{0,3},{5,4},{6,5},{7,6},{4,7},{9,8},{10,9},{11,1... | collective-permute-start | bytes 3993608 | tf_op jit(solution)/shard_map/ppermute | solution.py:31
  78.8 1.3 copy-start.3
  185.8 2.0 %copy-start.11 = (f32[8,8,512]{2,1,0:T(8,128)S(1)}, f32[8,8,512]{2,1,0:T(8,128)}, u32[]{:S(2)}) copy-start(f32[8,8,512]{2,1,0:T(8,128)} %get-tuple-element.38) | copy-start | bytes 393220
  185.9 2.0 %copy-start.9 = (f32[8,8,4096]{2,1,0:T(8,128)S(1)}, f32[8,8,4096]{2,1,0:T(8,128)}, u32[]{:S(2)}) copy-start(f32[8,8,4096]{2,1,0:T(8,128)} %get-tuple-element.39) | copy-start | bytes 3145732
  185.9 2.6 %copy-start.10 = (f32[8,8,512]{2,1,0:T(8,128)S(1)}, f32[8,8,512]{2,1,0:T(8,128)}, u32[]{:S(2)}) copy-start(f32[8,8,512]{2,1,0:T(8,128)} %get-tuple-element.40) | copy-start | bytes 393220
  187.8 1.4 copy-start.5
  189.6 1.4 copy-start.4
  193.0 2.0 %copy-start.1 = (f32[128,512]{1,0:T(8,128)S(1)}, f32[128,512]{1,0:T(8,128)}, u32[]{:S(2)}) copy-start(f32[128,512]{1,0:T(8,128)} %param.12) | copy-start | bytes 786436

commit v9 on v7

--- a/solution.py
+++ b/solution.py
@@ -340,9 +340,9 @@
         lax.fori_loop(0, blocks, block, 0)
 
     compute(0, first_ref)
-    sending.append(exchange(1, lambda g: results.at[0, g], lambda g: landed.at[0, g]))
     wait_arrivals(0, lambda g: second_ref.at[g], lambda g: arrived.at[g])
     sending[0][1].wait()
+    sending.append(exchange(1, lambda g: results.at[0, g], lambda g: landed.at[0, g]))
     compute(1, arrived)
     sending.append(exchange(2, lambda g: results.at[1, g], lambda g: landed.at[1, g]))
     for copies, local in sending:

time: 190 us -> 191 us (level)
  no operation moved by 1% of the time
where the time goes in v9:
time: 191 us; the launch traced here: 189 us
  Pallas kernels  104 us (54%)
  other arithmetic  24.1 us (13%)
  waiting for transfers between devices  23 us (12%)
  local copies, waits for them, and re-layouts  21.7 us (11%)
  starting transfers between devices  16 us (8%)
    pallas_call x1, Pallas kernels, exchange_friction(): pl.pallas_call(functools.partial(exchange_kernel, groups, width), in_spec...  104 us
    all_to_all x1, waiting for transfers between devices, local(): lax.all_to_all(payloads[0], 'freq', split_axis=0, concat_axis=0, tiled=True)  23 us
    all_to_all x1, starting transfers between devices, local(): lax.all_to_all(payloads[0], 'freq', split_axis=0, concat_axis=0, tiled=True)  8.47 us
    unnamed x40, local copies, waits for them, and re-layouts  7.1 us
    mul x1, other arithmetic, local(): extended = extended * rim_keep[:, None]  5.92 us
    ppermute x2, starting transfers between devices, extended_2(): lax.ppermute(lax.slice_in_dim(block, 0, width, axis=dim), axis, backward)  5.12 us
    unnamed x9, other arithmetic  4.33 us
  transfers between devices with their start and end apart: 5, of which 1 were waited for; matrix products, arithmetic and copies ran while one was open for 16% of the time, Pallas kernels for 0%

profile of v9, /device:TPU:8, one launch (start us, length us, event | category | flops | bytes accessed | tf_op | source)
XLA Modules:
  0.0 189.1 jit_solution(11795091320791240604)
XLA Ops:
  0.0 1.0 convert_element_type.53
  1.0 1.3 multiply_dynamic-update-slice_fusion.2
  2.4 1.4 constant_dynamic-update-slice_fusion.1
  3.8 1.4 constant_dynamic-update-slice_fusion
  5.4 0.1 multiply_dynamic-update-slice_fusion
  5.5 2.3 %copy-done.2 = f32[5,4,128,512]{3,2,1,0:T(8,128)} copy-done((f32[5,4,128,512]{3,2,1,0:T(8,128)}, f32[5,4,128,512]{3,2,1,0:T(8,128)S(1)}, u32[]{:S(2)}) %copy-start.2) | copy-done | bytes 5242904
  7.9 2.4 %collective-permute-start = (f32[5,4,1,512]{3,2,1,0:T(1,128)S(1)}, f32[5,4,1,512]{3,2,1,0:T(1,128)S(1)}, u32[]{:S(2)}, u32[]{:S(2)}) collective-permute-start(f32[5,4,1,512]{3,2,1,0:T(1,128)S(1)} %get-tuple-element.64), channel_id=1, source_target_pairs={{0,4},{4,8},{8,12},{12,16},{16,20},{20,24},{24,28},{28,0},{1,5},{5... | collective-permute-start | bytes 122888 | tf_op jit(solution)/shard_map/ppermute | solution.py:27
  10.3 3.3 %collective-permute-start.1 = (f32[5,4,1,512]{3,2,1,0:T(1,128)S(1)}, f32[5,4,1,512]{3,2,1,0:T(1,128)}, u32[]{:S(2)}, u32[]{:S(2)}) collective-permute-start(f32[5,4,1,512]{3,2,1,0:T(1,128)S(1)} %get-tuple-element.65), channel_id=1, source_target_pairs={{4,0},{8,4},{12,8},{16,12},{20,16},{24,20},{28,24},{0,28},{5,1},{9... | collective-permute-start | bytes 122888 | tf_op jit(solution)/shard_map/ppermute | solution.py:30
  13.6 0.6 pad_maximum_fusion
  14.2 1.8 fusion.51
  16.0 0.2 copy.172
  16.2 1.6 reshape.867
  17.8 8.5 %all-to-all-start = ((f32[8,16,4096]{2,1,0:T(8,128)}), f32[8,16,4096]{2,1,0:T(8,128)}, u32[]{:S(2)}, u32[]{:S(2)}) async-start(f32[8,16,4096]{2,1,0:T(8,128)} %reshape.867), calls=%async_computation | async-start | bytes 4194304 | tf_op jit(solution)/shard_map/all_to_all | solution.py:422
  26.3 0.6 fusion.44
  26.9 0.6 slice_bitcast_fusion.17
  27.5 0.2 fusion.41
  27.8 0.6 constant_dynamic-slice_fusion
  28.4 0.5 convert_multiply_fusion
  29.0 0.7 slice_bitcast_fusion.15
  29.7 2.3 %pad_maximum_fusion.7 = (f32[5,4,130,1]{3,2,1,0:T(8,128)S(1)}, f32[5,4,130,1]{3,2,1,0:T(8,128)S(1)}) fusion(f32[5,4,1,512]{3,2,1,0:T(1,128)} %collective-permute-done.1, f32[5,4,128,512]{3,2,1,0:T(8,128)} %copy-done.2, f32[5,4,1,512]{3,2,1,0:T(1,128)S(1)} %collective-permute-done), kind=kLoop, calls=%fused_computation.16 | loop fusion | flops 10400 | bytes 5345600 | tf_op jit(solution)/shard_map/slice | solution.py:28
  32.0 1.2 copy.124
  33.3 1.2 copy.125
  34.5 1.8 collective-permute-start.3
  36.3 1.8 copy.173
  38.1 1.7 reshape.860.second_ref
  39.9 0.8 copy.130.stacked_ref
  40.6 0.6 reshape.868.drag_ref
  41.3 0.5 copy.126
  41.8 0.5 copy.127
  42.3 5.9 %maximum_multiply_fusion = f32[5,4,130,514]{3,2,1,0:T(8,128)S(1)} fusion(f32[5,4,130,1]{3,2,1,0:T(8,128)S(1)} %copy.127, f32[5,4,1,512]{3,2,1,0:T(1,128)} %collective-permute-done.1, f32[5,4,128,512]{3,2,1,0:T(8,128)} %copy-done.2, f32[5,4,1,512]{3,2,1,0:T(1,128)S(1)} %collective-permute-done, f32[5,4,130,1]{3,2,1,0:T(8,128)S(1)} %copy.126, ...), kind=kLoop, calls=%fused_computation | loop fusion | flops 6682000 | bytes 10691720 | tf_op jit(solution)/shard_map/mul | solution.py:428
  48.2 0.4 slice.242
  48.6 0.2 slice_multiply_fusion.7
  48.9 1.8 slice_subtract_fusion.2
  50.7 0.3 slice_multiply_fusion.3
  51.1 2.7 %fusion.7 = (f32[1,4,128,512]{3,2,1,0:T(8,128)S(1)}, f32[1,4,128,512]{3,2,1,0:T(8,128)S(1)}) fusion(f32[5,4,130,514]{3,2,1,0:T(8,128)S(1)} %maximum_multiply_fusion, f32[128]{0:T(128)S(1)} %add_multiply_fusion, f32[1,4,128,512]{3,2,1,0:T(8,128)S(1)} %bitcast.304, f32[1,4,128,512]{3,2,1,0:T(8,128)S(1)} %bitcast.303), kind=kLoop, calls=%fused_computation.25 | loop fusion | flops 4718592 | bytes 15729152 | tf_op jit(solution)/shard_map/add | solution.py:77
  53.8 0.3 pad_maximum_fusion.1
  54.2 23.0 %all-to-all-done.first_ref = f32[8,16,4096]{2,1,0:T(8,128)} async-done(((f32[8,16,4096]{2,1,0:T(8,128)}), f32[8,16,4096]{2,1,0:T(8,128)}, u32[]{:S(2)}, u32[]{:S(2)}) %all-to-all-start) | async-done | bytes 2097184 | tf_op jit(solution)/shard_map/all_to_all | solution.py:422
  77.1 103.7 %shard_map.55 = (f32[8,8,4096]{2,1,0:T(8,128)}, f32[8,8,4096]{2,1,0:T(8,128)}, f32[8,8,512]{2,1,0:T(8,128)}, f32[8,8,512]{2,1,0:T(8,128)}) custom-call(bf16[256,192]{1,0:T(8,128)(2,1)} %copy.130.stacked_ref, f32[32,256]{1,0:T(8,128)} %bitcast.309, f32[8,16,4096]{2,1,0:T(8,128)} %all-to-all-done.first_ref, f32[8,16,4096]{2,1,0:T(8,128)} %reshape.860.second_ref, ...), custom_call_target="tpu_custom_call" | custom-call | tf_op jit(solution)/shard_map/pallas_call | solution.py:374
  180.9 1.9 %copy.167 = f32[8,8,8,512]{3,2,1,0:T(8,128)S(1)} copy(f32[8,8,8,512]{3,1,2,0:T(8,128)} %bitcast.311) | data formatting | bytes 2097152
  182.9 0.6 copy.166
  183.9 0.7 fusion.3
  184.6 0.5 multiply_subtract_fusion.2
  185.1 0.4 multiply_subtract_fusion.5
  185.5 0.4 add_negate_fusion.3
  186.0 0.2 pad_maximum_fusion.4
  186.2 0.1 copy.148
  186.6 0.5 pad_maximum_fusion.2
  187.1 2.0 %copy.149 = f32[3,4,8,2,8,512]{5,4,3,2,1,0:T(8,128)} copy(f32[3,4,8,2,8,512]{5,4,2,1,0,3:T(8,128)S(1)} %pad_maximum_fusion.2) | data formatting | bytes 6291456 | tf_op jit(solution)/shard_map/stack | solution.py:463
  (69 shorter events, 1.5 us)
Async XLA Ops:
  0.0 27.8 %copy-start = (f32[128,512]{1,0:T(8,128)S(1)}, f32[128,512]{1,0:T(8,128)}, u32[]{:S(2)}) copy-start(f32[128,512]{1,0:T(8,128)} %param.12) | copy-start | bytes 786436
  2.4 2.9 %copy-start.5 = (f32[128,512]{1,0:T(8,128)S(1)}, f32[128,512]{1,0:T(8,128)}, u32[]{:S(2)}) copy-start(f32[128,512]{1,0:T(8,128)} %param.11) | copy-start | bytes 786436
  5.2 8.4 %copy-start.4 = (f32[2,4,128,512]{3,2,1,0:T(8,128)S(1)}, f32[2,4,128,512]{3,2,1,0:T(8,128)}, u32[]{:S(2)}) copy-start(f32[2,4,128,512]{3,2,1,0:T(8,128)} %param.10) | copy-start | bytes 6291460
  5.5 2.3 %copy-start.2 = (f32[5,4,128,512]{3,2,1,0:T(8,128)}, f32[5,4,128,512]{3,2,1,0:T(8,128)S(1)}, u32[]{:S(2)}) copy-start(f32[5,4,128,512]{3,2,1,0:T(8,128)S(1)} %multiply_dynamic-update-slice_fusion) | copy-start | bytes 15728644
  7.9 21.8 %collective-permute-start = (f32[5,4,1,512]{3,2,1,0:T(1,128)S(1)}, f32[5,4,1,512]{3,2,1,0:T(1,128)S(1)}, u32[]{:S(2)}, u32[]{:S(2)}) collective-permute-start(f32[5,4,1,512]{3,2,1,0:T(1,128)S(1)} %get-tuple-element.64), channel_id=1, source_target_pairs={{0,4},{4,8},{8,12},{12,16},{16,20},{20,24},{24,28},{28,0},{1,5},{5... | collective-permute-start | bytes 122888 | tf_op jit(solution)/shard_map/ppermute | solution.py:27
  10.3 19.4 %collective-permute-start.1 = (f32[5,4,1,512]{3,2,1,0:T(1,128)S(1)}, f32[5,4,1,512]{3,2,1,0:T(1,128)}, u32[]{:S(2)}, u32[]{:S(2)}) collective-permute-start(f32[5,4,1,512]{3,2,1,0:T(1,128)S(1)} %get-tuple-element.65), channel_id=1, source_target_pairs={{4,0},{8,4},{12,8},{16,12},{20,16},{24,20},{28,24},{0,28},{5,1},{9... | collective-permute-start | bytes 122888 | tf_op jit(solution)/shard_map/ppermute | solution.py:30
  17.8 59.3 %all-to-all-start = ((f32[8,16,4096]{2,1,0:T(8,128)}), f32[8,16,4096]{2,1,0:T(8,128)}, u32[]{:S(2)}, u32[]{:S(2)}) async-start(f32[8,16,4096]{2,1,0:T(8,128)} %reshape.867), calls=%async_computation | async-start | bytes 4194304 | tf_op jit(solution)/shard_map/all_to_all | solution.py:422
  27.7 4.3 %copy-start.3 = (f32[256,32]{0,1:T(8,128)}, f32[256,32]{0,1:T(8,128)S(1)}, u32[]{:S(2)}) copy-start(f32[256,32]{0,1:T(8,128)S(1)} %reshape.866) | copy-start | bytes 98308
  28.9 21.7 %copy-start.15 = (f32[2]{0:T(128)}, f32[2]{0:T(128)S(1)}, u32[]{:S(2)}) copy-start(f32[2]{0:T(128)S(1)} %get-tuple-element.110) | copy-start | bytes 28
  29.0 0.7 copy-start.8
  33.2 8.1 %collective-permute-start.2 = (f32[5,4,130,1]{2,0,3,1:T(8,128)S(1)}, f32[5,4,130,1]{2,0,3,1:T(8,128)S(1)}, u32[]{:S(2)}, u32[]{:S(2)}) collective-permute-start(f32[5,4,130,1]{2,0,3,1:T(8,128)S(1)} %copy.124), channel_id=1, source_target_pairs={{0,1},{1,2},{2,3},{3,0},{4,5},{5,6},{6,7},{7,4},{8,9},{9,10},{10,1... | collective-permute-start | bytes 31208 | tf_op jit(solution)/shard_map/ppermute | solution.py:27
  34.5 7.3 %collective-permute-start.3 = (f32[5,4,130,1]{2,0,3,1:T(8,128)S(1)}, f32[5,4,130,1]{2,0,3,1:T(8,128)S(1)}, u32[]{:S(2)}, u32[]{:S(2)}) collective-permute-start(f32[5,4,130,1]{2,0,3,1:T(8,128)S(1)} %copy.125), channel_id=1, source_target_pairs={{1,0},{2,1},{3,2},{0,3},{5,4},{6,5},{7,6},{4,7},{9,8},{10,9},{11,1... | collective-permute-start | bytes 31208 | tf_op jit(solution)/shard_map/ppermute | solution.py:30
  38.1 1.7 copy-start.9
  38.1 2.5 %copy-start.10 = (f32[16,512]{1,0:T(8,128)S(1)}, f32[16,512]{1,0:T(8,128)}, u32[]{:S(2)}) copy-start(f32[16,512]{1,0:T(8,128)} %constant_dynamic-slice_fusion) | copy-start | bytes 98308
  180.9 2.1 %copy-start.6 = (f32[8,8,4096]{2,1,0:T(8,128)S(1)}, f32[8,8,4096]{2,1,0:T(8,128)}, u32[]{:S(2)}) copy-start(f32[8,8,4096]{2,1,0:T(8,128)} %get-tuple-element.37) | copy-start | bytes 3145732
  182.8 0.9 copy-start.12
  182.8 1.0 copy-start.11
  182.9 0.9 copy-start.7
  183.8 0.7 copy-start.13
  183.8 0.7 copy-start.14
  183.8 0.7 copy-start.16
  183.8 0.7 copy-start.17
  186.6 2.5 %copy-start.1 = (f32[128,512]{1,0:T(8,128)S(1)}, f32[128,512]{1,0:T(8,128)}, u32[]{:S(2)}) copy-start(f32[128,512]{1,0:T(8,128)} %param.12) | copy-start | bytes 786436
